TPU v7x, 512 devices: a whole 4x4x16 slice. The times are simulated.
512 devices in a mesh: dp: 8 (over y, core), expert: 64 (over z, x).
Axes of the slice: x: 4, y: 4, z: 16, core: 2. Of those that a mesh axis runs over, the one named last changes fastest.
Arguments:
- latent: bfloat16 [65536, 4096], P(('dp', 'expert')), may hold values from -6 to 6
- dout: bfloat16 [65536, 4096], P(('dp', 'expert')), may hold values from -6 to 6
- routes: int32 [65536, 2], P(('dp', 'expert')), may hold values from 0 to 63, as said below
- gate_w: float32 [65536, 2], P(('dp', 'expert')), may hold values from 0.1 to 1
- norm_gain: float32 [4096], replicated, may hold values from 0.1 to 1.9
- w_gate_up: bfloat16 [64, 4096, 256], P('expert', 'dp'), may hold values from -0.09375 to 0.09375
- w_down: bfloat16 [64, 128, 4096], P('expert', None, 'dp'), may hold values from -0.1875 to 0.1875
Outputs:
- d_latent: bfloat16 [65536, 4096], P(('dp', 'expert'))
- grad_gate_up: bfloat16 [64, 4096, 256], P('expert', 'dp')
- grad_down: bfloat16 [64, 128, 4096], P('expert', None, 'dp')
Inputs may be any that keep to these rules, and one draw needn't show every extreme that they name: `routes`: each patch names two different experts, at most one of them below 8. The patches of one device name no expert below 8 more than 4 times, and in every draw some expert below 8 is named exactly 4 times by the patches of every device of one index of dp.
All inputs are finite; a program needn't handle non-finite values.
Results may differ from a plain program's by a relative error of at most 0.013.
Values may be sent and summed in bfloat16 or wider, within the bound.
No kernel may reach another device: no remote copies, remote signals or barrier semaphores. Data moves between devices by JAX's collectives and lax.ppermute only.
A program may use at most 64 MiB of HBM per device.

v0:
```python
import jax
import jax.numpy as jnp
from jax import lax
from jax.sharding import PartitionSpec as P

SLICES = 8
CAP = 4


EPS = 1e-06


def expert_pass(rows_in, rows_dy, wgu, wd):
    hid = wd.shape[0]
    pre = jnp.dot(rows_in, wgu, preferred_element_type=jnp.float32)
    gate = pre[:, :hid]
    up = pre[:, hid:]
    sig = jax.nn.sigmoid(gate)
    act = gate * sig
    hidden = (act * up).astype(jnp.bfloat16)
    dh = lax.dot_general(rows_dy, wd, (((1,), (1,)), ((), ())), preferred_element_type=jnp.float32)
    d_up = dh * act
    d_gate = dh * up * sig * (1.0 + gate * (1.0 - sig))
    d_pre = jnp.concatenate([d_gate, d_up], axis=1).astype(jnp.bfloat16)
    return (hidden, d_pre)


def body(latent, dout, routes, gate_w, norm_gain, w_gate_up, w_down):
    width = latent.shape[1]
    members = lax.axis_size("expert")
    groups = members // SLICES
    values = latent.astype(jnp.float32)
    inverse = lax.rsqrt(jnp.mean(values * values, axis=1, keepdims=True) + EPS)
    scaled = values * inverse
    expert_in = (scaled * norm_gain[None, :]).astype(jnp.bfloat16)
    inside = routes < groups
    chosen = jnp.sum(jnp.where(inside, routes, 0), axis=1)
    present = jnp.any(inside, axis=1)
    weight = jnp.sum(jnp.where(inside, gate_w, jnp.float32(0.0)), axis=1)
    grad_scale = (weight[:, None] * dout.astype(jnp.float32)).astype(jnp.bfloat16)
    onehot = (
        (chosen[:, None] == jnp.arange(groups, dtype=jnp.int32)[None, :]) & present[:, None]
    ).astype(jnp.int32)
    slot = jnp.sum((jnp.cumsum(onehot, axis=0) - 1) * onehot, axis=1)
    target = chosen * CAP + slot
    select = (
        (target[None, :] == jnp.arange(groups * CAP, dtype=jnp.int32)[:, None]) & present[None, :]
    ).astype(jnp.bfloat16)
    send_in = (
        jnp.dot(select, expert_in, preferred_element_type=jnp.float32)
        .astype(jnp.bfloat16)
        .reshape(groups, CAP, width)
    )
    send_dy = (
        jnp.dot(select, grad_scale, preferred_element_type=jnp.float32)
        .astype(jnp.bfloat16)
        .reshape(groups, CAP, width)
    )
    full_gu, full_down = (
        lax.all_gather(w_gate_up, "dp", axis=1, tiled=True),
        lax.all_gather(w_down, "dp", axis=2, tiled=True),
    )
    wgu = full_gu[0]
    wd = full_down[0]
    wide_in = jnp.repeat(send_in, SLICES, axis=0)
    wide_dy = jnp.repeat(send_dy, SLICES, axis=0)
    got_in, got_dy = (
        lax.all_to_all(wide_in, "expert", split_axis=0, concat_axis=0, tiled=True),
        lax.all_to_all(wide_dy, "expert", split_axis=0, concat_axis=0, tiled=True),
    )
    rows_in = got_in.reshape(-1, width)
    rows_dy = got_dy.reshape(-1, width)
    hidden, d_pre = expert_pass(rows_in, rows_dy, wgu, wd)
    part_gu = lax.dot_general(
        rows_in, d_pre, (((0,), (0,)), ((), ())), preferred_element_type=jnp.float32
    )
    part_d = lax.dot_general(
        hidden, rows_dy, (((0,), (0,)), ((), ())), preferred_element_type=jnp.float32
    )
    back = lax.dot_general(
        d_pre, wgu, (((1,), (1,)), ((), ())), preferred_element_type=jnp.float32
    ).astype(jnp.bfloat16)
    grad_gu, grad_d = (
        lax.psum_scatter(
            part_gu[None].astype(jnp.bfloat16), "dp", scatter_dimension=1, tiled=True
        ).astype(jnp.float32),
        lax.psum_scatter(
            part_d[None].astype(jnp.bfloat16), "dp", scatter_dimension=2, tiled=True
        ).astype(jnp.float32),
    )
    home = lax.all_to_all(
        back.reshape(members, CAP, width), "expert", split_axis=0, concat_axis=0, tiled=True
    )
    summed = jnp.sum(home.reshape(groups, SLICES, CAP, width).astype(jnp.float32), axis=1).astype(
        jnp.bfloat16
    )
    d_in = lax.dot_general(
        select,
        summed.reshape(groups * CAP, width),
        (((0,), (0,)), ((), ())),
        preferred_element_type=jnp.float32,
    )
    grad_in = d_in * norm_gain[None, :]
    d_latent = inverse * (grad_in - scaled * jnp.mean(grad_in * scaled, axis=1, keepdims=True))
    return (
        d_latent.astype(jnp.bfloat16),
        grad_gu.astype(jnp.bfloat16),
        grad_d.astype(jnp.bfloat16),
    )


def solution(mesh):
    placed = (
        P(("dp", "expert"), None),
        P(("dp", "expert"), None),
        P(("dp", "expert"), None),
        P(("dp", "expert"), None),
        P(),
        P("expert", "dp", None),
        P("expert", None, "dp"),
    )
    return jax.shard_map(
        body,
        mesh=mesh,
        in_specs=placed,
        out_specs=(P(("dp", "expert"), None), P("expert", "dp", None), P("expert", None, "dp")),
        check_vma=False,
    )
```

profile of v0, /device:TPU:24, one launch (start us, length us, event | category | flops | bytes accessed | tf_op | source)
XLA Modules:
  0.0 374.2 jit_solution(10510814662575036172)
XLA Ops:
  7.2 0.7 fusion.34
  7.9 0.7 select_reduce_fusion.2
  8.6 0.1 fusion.22
  8.7 0.2 reduce_window_sum.11
  8.8 0.2 select_reduce_fusion
  9.0 1.5 fusion.10
  10.6 1.7 convolution_convert_fusion.3
  12.3 0.1 reshape.61
  12.4 2.4 broadcast_in_dim.15
  14.7 0.0 copy-start.5
  14.7 18.7 %all-to-all-start.1 = ((bf16[64,4,4096]{2,1,0:T(4,128)(2,1)}), bf16[64,4,4096]{2,1,0:T(4,128)(2,1)S(1)}, u32[]{:S(2)}, u32[]{:S(2)}) async-start(bf16[64,4,4096]{2,1,0:T(4,128)(2,1)} %bitcast.24), calls=%async_computation.1 | async-start | bytes 4194304 | tf_op jit(solution)/shard_map/all_to_all | solution.py:68
  33.4 0.0 copy-done.5
  33.5 0.0 copy-done.6
  33.5 0.0 copy-done.3
  33.5 0.4 convolution_convert_fusion.4
  33.9 0.1 reshape.58
  34.0 99.7 %all-to-all-done.1 = bf16[64,4,4096]{2,1,0:T(4,128)(2,1)S(1)} async-done(((bf16[64,4,4096]{2,1,0:T(4,128)(2,1)}), bf16[64,4,4096]{2,1,0:T(4,128)(2,1)S(1)}, u32[]{:S(2)}, u32[]{:S(2)}) %all-to-all-start.1) | async-done | bytes 2097184 | tf_op jit(solution)/shard_map/all_to_all | solution.py:68
  133.7 2.4 broadcast_in_dim.14
  136.0 0.0 copy-done.1
  136.0 6.1 %all-to-all-start = ((bf16[64,4,4096]{2,1,0:T(4,128)(2,1)}), bf16[64,4,4096]{2,1,0:T(4,128)(2,1)}, u32[]{:S(2)}, u32[]{:S(2)}) async-start(bf16[64,4,4096]{2,1,0:T(4,128)(2,1)} %bitcast.23), calls=%async_computation | async-start | bytes 4194304 | tf_op jit(solution)/shard_map/all_to_all | solution.py:69
  142.1 0.0 all-gather.5.cloned.1.call-start
  142.2 0.7 all-gather.5.cloned.1.call-update
  142.9 0.0 all-gather.3.cloned.1.call-start
  142.9 0.7 all-gather.3.cloned.1.call-update
  143.6 2.5 reshape.63
  146.2 95.5 %all-to-all-done = bf16[64,4,4096]{2,1,0:T(4,128)(2,1)} async-done(((bf16[64,4,4096]{2,1,0:T(4,128)(2,1)}), bf16[64,4,4096]{2,1,0:T(4,128)(2,1)}, u32[]{:S(2)}, u32[]{:S(2)}) %all-to-all-start) | async-done | bytes 2097184 | tf_op jit(solution)/shard_map/all_to_all | solution.py:69
  241.7 4.0 %reshape.60 = bf16[256,4096]{1,0:T(8,128)(2,1)} reshape(bf16[64,4,4096]{2,1,0:T(4,128)(2,1)} %all-to-all-done) | data formatting | bytes 4194304 | tf_op jit(solution)/shard_map/reshape | solution.py:72
  245.7 2.5 fusion.12
  248.2 0.0 all-gather.3.cloned.1.call-done
  248.2 0.0 copy-start.2
  248.2 2.8 multiply_convert_fusion.4
  251.1 0.0 copy-done.2
  251.1 2.1 convolution_convert_fusion.1
  253.2 4.1 %reshape.64 = bf16[64,4,4096]{2,1,0:T(4,128)(2,1)} reshape(bf16[256,4096]{1,0:T(8,128)(2,1)} %convolution_convert_fusion.1) | data formatting | bytes 4194304 | tf_op jit(solution)/shard_map/reshape | solution.py:92
  257.3 6.1 %all-to-all-start.2 = ((bf16[64,4,4096]{2,1,0:T(4,128)(2,1)}), bf16[64,4,4096]{2,1,0:T(4,128)(2,1)}, u32[]{:S(2)}, u32[]{:S(2)}) async-start(bf16[64,4,4096]{2,1,0:T(4,128)(2,1)} %reshape.64), calls=%async_computation.2 | async-start | bytes 4194304 | tf_op jit(solution)/shard_map/all_to_all | solution.py:91
  263.4 0.0 reduce-scatter.5.cloned.1.call-start
  263.5 3.1 fusion.1
  266.6 0.0 reduce-scatter.5.cloned.1.call-update
  266.6 0.2 reduce-scatter.3.cloned.1.call-start
  266.8 2.1 fusion
  268.9 0.0 reduce-scatter.3.cloned.1.call-update
  269.0 93.7 %all-to-all-done.2 = bf16[64,4,4096]{2,1,0:T(4,128)(2,1)} async-done(((bf16[64,4,4096]{2,1,0:T(4,128)(2,1)}), bf16[64,4,4096]{2,1,0:T(4,128)(2,1)}, u32[]{:S(2)}, u32[]{:S(2)}) %all-to-all-start.2) | async-done | bytes 2097184 | tf_op jit(solution)/shard_map/all_to_all | solution.py:91
  362.7 2.8 bitcast_reduce_fusion
  365.4 0.1 reshape.66
  365.5 0.0 copy-done
  365.5 0.0 copy-done.4
  365.5 0.6 fusion.6
  366.1 1.5 fusion.9
  (12 shorter events, 0.1 us)
Async XLA Ops:
  14.7 18.7 %copy-start.5 = (s32[128,2]{0,1:T(2,128)S(1)}, s32[128,2]{0,1:T(2,128)}, u32[]{:S(2)}) copy-start(s32[128,2]{0,1:T(2,128)} %param.9) | copy-start | bytes 3076
  14.7 18.7 %copy-start.6 = (f32[128,2]{0,1:T(2,128)S(1)}, f32[128,2]{0,1:T(2,128)}, u32[]{:S(2)}) copy-start(f32[128,2]{0,1:T(2,128)} %param.10) | copy-start | bytes 3076
  14.7 18.7 %copy-start.3 = (bf16[128,4096]{1,0:T(8,128)(2,1)S(1)}, bf16[128,4096]{1,0:T(8,128)(2,1)}, u32[]{:S(2)}) copy-start(bf16[128,4096]{1,0:T(8,128)(2,1)} %param.8) | copy-start | bytes 3145732
  14.7 118.9 %all-to-all-start.1 = ((bf16[64,4,4096]{2,1,0:T(4,128)(2,1)}), bf16[64,4,4096]{2,1,0:T(4,128)(2,1)S(1)}, u32[]{:S(2)}, u32[]{:S(2)}) async-start(bf16[64,4,4096]{2,1,0:T(4,128)(2,1)} %bitcast.24), calls=%async_computation.1 | async-start | bytes 4194304 | tf_op jit(solution)/shard_map/all_to_all | solution.py:68
  133.7 2.4 copy-start.1
  136.0 105.7 %all-to-all-start = ((bf16[64,4,4096]{2,1,0:T(4,128)(2,1)}), bf16[64,4,4096]{2,1,0:T(4,128)(2,1)}, u32[]{:S(2)}, u32[]{:S(2)}) async-start(bf16[64,4,4096]{2,1,0:T(4,128)(2,1)} %bitcast.23), calls=%async_computation | async-start | bytes 4194304 | tf_op jit(solution)/shard_map/all_to_all | solution.py:69
  142.1 103.5 %all-gather.5.cloned.1.call-start = ((), (), s32[]{:S(2)}) async-start(), calls=%async_computation.6 | async-start | bytes 2359296 | tf_op jit(solution)/shard_map/all_gather | solution.py:60
  142.9 105.3 %all-gather.3.cloned.1.call-start = ((), (), s32[]{:S(2)}) async-start(), calls=%async_computation.5 | async-start | bytes 1179648 | tf_op jit(solution)/shard_map/all_gather | solution.py:61
  248.2 2.9 copy-start.2
  257.3 105.3 %all-to-all-start.2 = ((bf16[64,4,4096]{2,1,0:T(4,128)(2,1)}), bf16[64,4,4096]{2,1,0:T(4,128)(2,1)}, u32[]{:S(2)}, u32[]{:S(2)}) async-start(bf16[64,4,4096]{2,1,0:T(4,128)(2,1)} %reshape.64), calls=%async_computation.2 | async-start | bytes 4194304 | tf_op jit(solution)/shard_map/all_to_all | solution.py:91
  263.4 104.2 %reduce-scatter.5.cloned.1.call-start = ((), (), s32[]{:S(2)}) async-start(), calls=%async_computation.8 | async-start | bytes 1179648 | tf_op jit(solution)/shard_map/reduce_scatter | solution.py:87
  266.6 101.0 %reduce-scatter.3.cloned.1.call-start = ((), (), s32[]{:S(2)}) async-start(), calls=%async_computation.7 | async-start | bytes 2359296 | tf_op jit(solution)/shard_map/reduce_scatter | solution.py:84
  268.9 96.5 %copy-start = (bf16[128,4096]{1,0:T(8,128)(2,1)S(1)}, bf16[128,4096]{1,0:T(8,128)(2,1)}, u32[]{:S(2)}) copy-start(bf16[128,4096]{1,0:T(8,128)(2,1)} %param.7) | copy-start | bytes 3145732
  268.9 96.5 %copy-start.4 = (f32[4096]{0:T(1024)S(1)}, f32[4096]{0:T(1024)}, u32[]{:S(2)}) copy-start(f32[4096]{0:T(1024)} %param.11) | copy-start | bytes 49156
Sparse Core Ops, SparseCore 0:
  145.1 32.0 all-gather.4
  179.3 31.6 all-gather.2
  267.6 37.9 reduce-scatter.4
  308.9 41.6 reduce-scatter.2
where the time goes:
time: 375 us; the launch traced here: 374 us
  waiting for transfers between devices  290 us (77%)
  starting transfers between devices  31.2 us (8%)
  local copies, waits for them, and re-layouts  15.7 us (4%)
  matrix products  15.3 us (4%)
  between operations  13.9 us (4%)
  other arithmetic  7.66 us (2%)
    all_to_all x1, waiting for transfers between devices, body(): lax.all_to_all(wide_in, 'expert', split_axis=0, concat_axis=0, tiled=True)  99.7 us
    all_to_all x1, waiting for transfers between devices, body(): lax.all_to_all(wide_dy, 'expert', split_axis=0, concat_axis=0, tiled=True)  95.5 us
    all_to_all x1, waiting for transfers between devices, body(): lax.all_to_all(back.reshape(members, CAP, width), 'expert', split_axis=0,...  93.7 us
    all_to_all x1, starting transfers between devices, body(): lax.all_to_all(wide_in, 'expert', split_axis=0, concat_axis=0, tiled=True)  18.7 us
  transfers between devices with their start and end apart: 7, of which 3 were waited for; matrix products, arithmetic and copies ran while one was open for 5% of the time, Pallas kernels for 0%

commit v1 on v0

v1 whole, which is shorter than its diff:
```python
import jax
import jax.numpy as jnp
from jax import lax
from jax.sharding import Mesh, PartitionSpec as P

SLICES = 8
CAP = 4
EPS = 1e-06
Y, C, Z, X = 4, 2, 16, 4
GROUPS = 8
HID = 128
F32 = jnp.float32
BF16 = jnp.bfloat16

SWAP = [
    (c * Z + 2 * e + p, p * Z + 2 * e + c) for c in range(C) for e in range(GROUPS) for p in range(2)
]
FLIP = [(i, i ^ 1) for i in range(Z)]
PLUS = [(i, (i + 1) % X) for i in range(X)]
MINUS = [(i, (i - 1) % X) for i in range(X)]


def outward(rows):
    cut = rows.reshape(GROUPS, CAP, Y, 2, 512)
    return cut.transpose(0, 3, 1, 2, 4).reshape(Z, CAP, 2048)


def homeward(blocks):
    cut = blocks.reshape(GROUPS, 2, CAP, Y, 512)
    return cut.transpose(0, 2, 3, 1, 4).reshape(GROUPS * CAP, 4096)


def gather_x(own):
    half = own.shape[0] // 2
    left = lax.ppermute(own, "x", PLUS)
    right = lax.ppermute(own, "x", MINUS)
    far_a = lax.ppermute(left[:half], "x", PLUS)
    far_b = lax.ppermute(right[half:], "x", MINUS)
    return jnp.concatenate([own, left, right, far_a, far_b], axis=0)


def scatter_x(part):
    n = part.shape[0] // 4
    half = n // 2
    own, left, right = part[:n], part[n : 2 * n], part[2 * n : 3 * n]
    far = part[3 * n :].astype(BF16)
    got_a = lax.ppermute(far[:half], "x", MINUS).astype(F32)
    got_b = lax.ppermute(far[half:], "x", PLUS).astype(F32)
    left = jnp.concatenate([left[:half] + got_a, left[half:]], axis=0).astype(BF16)
    right = jnp.concatenate([right[:half], right[half:] + got_b], axis=0).astype(BF16)
    from_right = lax.ppermute(left, "x", MINUS)
    from_left = lax.ppermute(right, "x", PLUS)
    return own + from_right.astype(F32) + from_left.astype(F32)


def body(latent, dout, routes, gate_w, norm_gain, w_gate_up, w_down):
    zp = lax.axis_index("z") % 2
    even = zp == 0

    piece = jnp.concatenate([w_gate_up[0], w_down[0].T], axis=1)
    piece = lax.ppermute(piece, ("c", "z"), SWAP)
    weights = lax.all_gather(piece, ("c", "y"), axis=0, tiled=True)
    weights = weights.reshape(2, 2048, 3 * HID)

    values = latent.astype(F32)
    inverse = lax.rsqrt(jnp.mean(values * values, axis=1, keepdims=True) + EPS)
    scaled = values * inverse
    expert_in = (scaled * norm_gain[None, :]).astype(BF16)
    inside = routes < GROUPS
    chosen = jnp.sum(jnp.where(inside, routes, 0), axis=1)
    present = jnp.any(inside, axis=1)
    weight = jnp.sum(jnp.where(inside, gate_w, F32(0.0)), axis=1)
    grad_scale = (weight[:, None] * dout.astype(F32)).astype(BF16)
    onehot = (
        (chosen[:, None] == jnp.arange(GROUPS, dtype=jnp.int32)[None, :]) & present[:, None]
    ).astype(jnp.int32)
    slot = jnp.sum((jnp.cumsum(onehot, axis=0) - 1) * onehot, axis=1)
    target = chosen * CAP + slot
    select = (
        (target[None, :] == jnp.arange(GROUPS * CAP, dtype=jnp.int32)[:, None]) & present[None, :]
    ).astype(BF16)
    send_in = jnp.dot(select, expert_in, preferred_element_type=F32).astype(BF16)
    send_dy = jnp.dot(select, grad_scale, preferred_element_type=F32).astype(BF16)

    got_in = lax.all_to_all(outward(send_in), "z", 0, 0, tiled=True).reshape(-1, 2048)
    got_dy = lax.all_to_all(outward(send_dy), "z", 0, 0, tiled=True).reshape(-1, 2048)
    rows_in = gather_x(got_in)
    rows_dy = gather_x(got_dy)

    def joined(rows, low, high):
        part = [
            jnp.dot(rows, weights[g, :, low:high], preferred_element_type=F32) for g in range(2)
        ]
        mine = jnp.where(even, part[0], part[1])
        other = jnp.where(even, part[1], part[0]).astype(BF16)
        return mine + lax.ppermute(other, "z", FLIP).astype(F32)

    pre = joined(rows_in, 0, 2 * HID)
    dh = joined(rows_dy, 2 * HID, 3 * HID)
    gate = pre[:, :HID]
    up = pre[:, HID:]
    sig = jax.nn.sigmoid(gate)
    act = gate * sig
    hidden = act * up
    d_up = dh * act
    d_gate = dh * up * sig * (1.0 + gate * (1.0 - sig))
    mine = jnp.concatenate([d_gate, d_up, hidden], axis=1).astype(BF16)
    other = lax.ppermute(mine, "z", FLIP)
    inner = [jnp.where(even, mine, other), jnp.where(even, other, mine)]

    part_in = sum(
        lax.dot_general(
            inner[g][:, : 2 * HID],
            weights[g, :, : 2 * HID],
            (((1,), (1,)), ((), ())),
            preferred_element_type=F32,
        )
        for g in range(2)
    )
    summed = scatter_x(part_in).astype(BF16)
    home = lax.all_to_all(summed.reshape(Z, CAP, 2048), "z", 0, 0, tiled=True)

    def over_rows(a, b):
        return lax.dot_general(a, b, (((0,), (0,)), ((), ())), preferred_element_type=F32)

    grads = jnp.concatenate(
        [
            jnp.concatenate(
                [
                    over_rows(rows_in, inner[g][:, : 2 * HID]).astype(BF16),
                    over_rows(rows_dy, inner[g][:, 2 * HID :]).astype(BF16),
                ],
                axis=1,
            )
            for g in range(2)
        ],
        axis=0,
    )
    grads = lax.psum_scatter(grads, ("c", "y"), scatter_dimension=0, tiled=True)
    grads = lax.ppermute(grads, ("c", "z"), SWAP)
    grad_gu = grads[:, : 2 * HID][None]
    grad_d = grads[:, 2 * HID :].T[None]

    d_in = lax.dot_general(
        select, homeward(home), (((0,), (0,)), ((), ())), preferred_element_type=F32
    )
    grad_in = d_in * norm_gain[None, :]
    d_latent = inverse * (grad_in - scaled * jnp.mean(grad_in * scaled, axis=1, keepdims=True))
    return d_latent.astype(BF16), grad_gu, grad_d


def solution(mesh):
    fine = Mesh(mesh.devices.reshape(Y, C, Z, X), ("y", "c", "z", "x"))
    rows = P(("y", "c", "z", "x"), None)
    gate_up = P(("z", "x"), ("y", "c"), None)
    down = P(("z", "x"), None, ("y", "c"))
    return jax.shard_map(
        body,
        mesh=fine,
        in_specs=(rows, rows, rows, rows, P(), gate_up, down),
        out_specs=(rows, gate_up, down),
        check_vma=False,
    )
```

time: 375 us -> 217 us (0.58)
  the two profiles are of different devices: /device:TPU:24 before, /device:TPU:23 now
where the time goes in v1:
time: 217 us; the launch traced here: 216 us
  starting transfers between devices  87.8 us (40%)
  waiting for transfers between devices  51.9 us (24%)
  other arithmetic  17.8 us (8%)
  blocking collectives  17.7 us (8%)
  between operations  14.7 us (7%)
  local copies, waits for them, and re-layouts  13.1 us (6%)
  matrix products  12.9 us (6%)
    all_to_all x1, blocking collectives, body(): home = lax.all_to_all(summed.reshape(Z, CAP, 2048), 'z', 0, 0, tiled=True)  17.7 us
    all_to_all x1, starting transfers between devices, body(): lax.all_to_all(outward(send_in), 'z', 0, 0, tiled=True).reshape(-1, 2048)  14.5 us
    ppermute x1, starting transfers between devices, body(): grads = lax.ppermute(grads, ('c', 'z'), SWAP)  12.4 us
    all_to_all x1, waiting for transfers between devices, body(): lax.all_to_all(outward(send_in), 'z', 0, 0, tiled=True).reshape(-1, 2048)  12.3 us
    concatenate x1, other arithmetic, body(): jnp.concatenate([jnp.concatenate([over_rows(rows_in, inner[g][:, :2 * HID...  12 us
    all_to_all x1, starting transfers between devices, body(): lax.all_to_all(outward(send_dy), 'z', 0, 0, tiled=True).reshape(-1, 2048)  10.2 us
    ppermute x2, starting transfers between devices, gather_x(): far_a = lax.ppermute(left[:half], 'x', PLUS)  7.85 us
    all_to_all x1, waiting for transfers between devices, body(): lax.all_to_all(outward(send_dy), 'z', 0, 0, tiled=True).reshape(-1, 2048)  7.72 us
  transfers between devices with their start and end apart: 21, of which 12 were waited for; matrix products, arithmetic and copies ran while one was open for 10% of the time, Pallas kernels for 0%

profile of v1, /device:TPU:23, one launch (start us, length us, event | category | flops | bytes accessed | tf_op | source)
XLA Modules:
  0.0 216.0 jit_solution(2886406188486794126)
XLA Ops:
  7.2 1.1 copy.26
  8.3 1.0 pad_maximum_fusion
  9.3 4.1 %collective-permute-start.4 = (bf16[512,384]{1,0:T(8,128)(2,1)S(1)}, bf16[512,384]{1,0:T(8,128)(2,1)S(1)}, u32[]{:S(2)}, u32[]{:S(2)}) collective-permute-start(bf16[512,384]{1,0:T(8,128)(2,1)S(1)} %pad_maximum_fusion), channel_id=1, source_target_pairs={{0,0},{4,64},{8,8},{12,72},{16,16},{20,80},{24,24},{28,88},{32,32}... | collective-permute-start | bytes 1179656 | tf_op jit(solution)/shard_map/ppermute | solution.py:61
  14.1 4.7 %collective-permute-done.4 = bf16[512,384]{1,0:T(8,128)(2,1)S(1)} collective-permute-done((bf16[512,384]{1,0:T(8,128)(2,1)S(1)}, bf16[512,384]{1,0:T(8,128)(2,1)S(1)}, u32[]{:S(2)}, u32[]{:S(2)}) %collective-permute-start.4) | collective-permute-done | bytes 393248 | tf_op jit(solution)/shard_map/ppermute | solution.py:61
  22.6 0.9 copy.28
  23.5 14.5 %all-to-all-start.1 = ((bf16[16,4,2048]{2,1,0:T(4,128)(2,1)}), bf16[16,4,2048]{2,1,0:T(4,128)(2,1)S(1)}, u32[]{:S(2)}, u32[]{:S(2)}) async-start(bf16[16,4,2048]{2,1,0:T(4,128)(2,1)} %copy.28), calls=%async_computation.1 | async-start | bytes 524288 | tf_op jit(solution)/shard_map/all_to_all | solution.py:85
  38.9 0.9 copy.25
  39.8 12.3 %all-to-all-done.1 = bf16[16,4,2048]{2,1,0:T(4,128)(2,1)S(1)} async-done(((bf16[16,4,2048]{2,1,0:T(4,128)(2,1)}), bf16[16,4,2048]{2,1,0:T(4,128)(2,1)S(1)}, u32[]{:S(2)}, u32[]{:S(2)}) %all-to-all-start.1) | async-done | bytes 262176 | tf_op jit(solution)/shard_map/all_to_all | solution.py:85
  52.1 10.2 %all-to-all-start = ((bf16[16,4,2048]{2,1,0:T(4,128)(2,1)}), bf16[16,4,2048]{2,1,0:T(4,128)(2,1)S(1)}, u32[]{:S(2)}, u32[]{:S(2)}) async-start(bf16[16,4,2048]{2,1,0:T(4,128)(2,1)} %copy.25), calls=%async_computation | async-start | bytes 524288 | tf_op jit(solution)/shard_map/all_to_all | solution.py:86
  63.2 2.1 collective-permute-start.6
  65.3 3.2 %collective-permute-start.7 = (bf16[64,2048]{1,0:T(8,128)(2,1)}, bf16[64,2048]{1,0:T(8,128)(2,1)}, u32[]{:S(2)}, u32[]{:S(2)}) collective-permute-start(bf16[64,2048]{1,0:T(8,128)(2,1)} %reshape.65), channel_id=1, source_target_pairs={{0,3},{1,0},{2,1},{3,2},{4,7},{5,4},{6,5},{7,6},{8,11},{9,8},{10,9... | collective-permute-start | bytes 786440 | tf_op jit(solution)/shard_map/ppermute | solution.py:36
  68.5 7.7 %all-to-all-done = bf16[16,4,2048]{2,1,0:T(4,128)(2,1)S(1)} async-done(((bf16[16,4,2048]{2,1,0:T(4,128)(2,1)}), bf16[16,4,2048]{2,1,0:T(4,128)(2,1)S(1)}, u32[]{:S(2)}, u32[]{:S(2)}) %all-to-all-start) | async-done | bytes 262176 | tf_op jit(solution)/shard_map/all_to_all | solution.py:86
  76.3 2.1 collective-permute-start
  78.4 3.2 %collective-permute-start.1 = (bf16[64,2048]{1,0:T(8,128)(2,1)S(1)}, bf16[64,2048]{1,0:T(8,128)(2,1)S(1)}, u32[]{:S(2)}, u32[]{:S(2)}) collective-permute-start(bf16[64,2048]{1,0:T(8,128)(2,1)S(1)} %reshape.61), channel_id=1, source_target_pairs={{0,3},{1,0},{2,1},{3,2},{4,7},{5,4},{6,5},{7,6},{8,11},{9,8},{10,9... | collective-permute-start | bytes 786440 | tf_op jit(solution)/shard_map/ppermute | solution.py:36
  81.6 1.0 constant_dynamic-update-slice_fusion.9
  82.6 0.9 slice.112
  83.5 3.3 %collective-permute-start.8 = (bf16[32,2048]{1,0:T(8,128)(2,1)S(1)}, bf16[32,2048]{1,0:T(8,128)(2,1)S(1)}, u32[]{:S(2)}, u32[]{:S(2)}) collective-permute-start(bf16[32,2048]{1,0:T(8,128)(2,1)S(1)} %slice.112), channel_id=1, source_target_pairs={{0,1},{1,2},{2,3},{3,0},{4,5},{5,6},{6,7},{7,4},{8,9},{9,10},{10,1... | collective-permute-start | bytes 393224 | tf_op jit(solution)/shard_map/ppermute | solution.py:37
  86.8 0.9 slice.113
  87.8 2.0 collective-permute-start.9
  89.8 4.5 %collective-permute-start.2 = (bf16[32,2048]{1,0:T(8,128)(2,1)S(1)}, bf16[32,2048]{1,0:T(8,128)(2,1)S(1)}, u32[]{:S(2)}, u32[]{:S(2)}) collective-permute-start(bf16[32,2048]{1,0:T(8,128)(2,1)S(1)} %slice.108), channel_id=1, source_target_pairs={{0,1},{1,2},{2,3},{3,0},{4,5},{5,6},{6,7},{7,4},{8,9},{9,10},{10,1... | collective-permute-start | bytes 393224 | tf_op jit(solution)/shard_map/ppermute | solution.py:37
  94.3 1.9 collective-permute-start.3
  96.2 1.0 constant_dynamic-update-slice_fusion.8
  97.2 1.0 constant_dynamic-update-slice_fusion.7
  98.3 4.6 %collective-permute-done.3 = bf16[32,2048]{1,0:T(8,128)(2,1)S(1)} collective-permute-done((bf16[32,2048]{1,0:T(8,128)(2,1)S(1)}, bf16[32,2048]{1,0:T(8,128)(2,1)S(1)}, u32[]{:S(2)}, u32[]{:S(2)}) %collective-permute-start.3) | collective-permute-done | bytes 131104 | tf_op jit(solution)/shard_map/ppermute | solution.py:38
  102.9 1.7 fusion.13
  104.7 1.8 select_convert_fusion
  106.5 5.7 %collective-permute-start.10 = (bf16[256,256]{0,1:T(8,128)(2,1)S(1)}, bf16[256,256]{0,1:T(8,128)(2,1)S(1)}, u32[]{:S(2)}, u32[]{:S(2)}) collective-permute-start(bf16[256,256]{0,1:T(8,128)(2,1)S(1)} %get-tuple-element.26), channel_id=1, source_target_pairs={{0,4},{4,0},{8,12},{12,8},{16,20},{20,16},{24,28},{28,24},{32,36},... | collective-permute-start | bytes 393224 | tf_op jit(solution)/shard_map/ppermute | solution.py:96
  112.2 1.5 fusion.19
  113.7 1.5 select_convert_fusion.1
  115.3 1.9 collective-permute-start.5
  117.3 3.0 %collective-permute-done.5 = bf16[256,128]{0,1:T(8,128)(2,1)S(1)} collective-permute-done((bf16[256,128]{0,1:T(8,128)(2,1)S(1)}, bf16[256,128]{0,1:T(8,128)(2,1)S(1)}, u32[]{:S(2)}, u32[]{:S(2)}) %collective-permute-start.5) | collective-permute-done | bytes 65568 | tf_op jit(solution)/shard_map/ppermute | solution.py:96
  120.4 3.1 %collective-permute-start.11 = (bf16[256,384]{0,1:T(8,128)(2,1)S(1)}, bf16[256,384]{0,1:T(8,128)(2,1)S(1)}, u32[]{:S(2)}, u32[]{:S(2)}) collective-permute-start(bf16[256,384]{0,1:T(8,128)(2,1)S(1)} %pad_maximum_fusion.3), channel_id=1, source_target_pairs={{0,4},{4,0},{8,12},{12,8},{16,20},{20,16},{24,28},{28,24},{32,36},... | collective-permute-start | bytes 589832 | tf_op jit(solution)/shard_map/ppermute | solution.py:108
  123.5 3.5 %collective-permute-done.11 = bf16[256,384]{0,1:T(8,128)(2,1)S(1)} collective-permute-done((bf16[256,384]{0,1:T(8,128)(2,1)S(1)}, bf16[256,384]{0,1:T(8,128)(2,1)S(1)}, u32[]{:S(2)}, u32[]{:S(2)}) %collective-permute-start.11) | collective-permute-done | bytes 196640 | tf_op jit(solution)/shard_map/ppermute | solution.py:108
  128.6 12.0 %maximum_maximum_fusion = bf16[4096,384]{0,1:T(8,128)(2,1)} fusion(bf16[2048,128]{0,1:T(8,128)(2,1)S(1)} %convolution_convert_fusion.4, bf16[2048,256]{0,1:T(8,128)(2,1)S(1)} %convolution_convert_fusion.2, bf16[2048,128]{0,1:T(8,128)(2,1)S(1)} %convolution_convert_fusion.5, bf16[2048,256]{0,1:T(8,128)(2,1)S(1)} %convolution_convert_fusion.3), kind=kLoop, calls=%fused_computation.3 | loop fusion | flops 12582912 | bytes 6291456 | tf_op jit(solution)/shard_map/concatenate | solution.py:126
  140.7 1.7 fusion.14
  142.4 1.7 fusion.43
  144.2 1.9 collective-permute-start.12
  146.1 4.6 %collective-permute-start.14 = (bf16[32,2048]{1,0:T(8,128)(2,1)S(1)}, bf16[32,2048]{1,0:T(8,128)(2,1)S(1)}, u32[]{:S(2)}, u32[]{:S(2)}) collective-permute-start(bf16[32,2048]{1,0:T(8,128)(2,1)S(1)} %get-tuple-element.18), channel_id=1, source_target_pairs={{0,1},{1,2},{2,3},{3,0},{4,5},{5,6},{6,7},{7,4},{8,9},{9,10},{10,1... | collective-permute-start | bytes 393224 | tf_op jit(solution)/shard_map/ppermute | solution.py:48
  151.1 1.5 collective-permute-done.14
  152.7 5.0 %collective-permute-start.15 = (bf16[64,2048]{1,0:T(8,128)(2,1)S(1)}, bf16[64,2048]{1,0:T(8,128)(2,1)S(1)}, u32[]{:S(2)}, u32[]{:S(2)}) collective-permute-start(bf16[64,2048]{1,0:T(8,128)(2,1)S(1)} %pad_maximum_fusion.2), channel_id=1, source_target_pairs={{0,1},{1,2},{2,3},{3,0},{4,5},{5,6},{6,7},{7,4},{8,9},{9,10},{10,1... | collective-permute-start | bytes 786440 | tf_op jit(solution)/shard_map/ppermute | solution.py:52
  157.8 1.9 collective-permute-start.13
  159.7 2.7 %collective-permute-done.15 = bf16[64,2048]{1,0:T(8,128)(2,1)S(1)} collective-permute-done((bf16[64,2048]{1,0:T(8,128)(2,1)S(1)}, bf16[64,2048]{1,0:T(8,128)(2,1)S(1)}, u32[]{:S(2)}, u32[]{:S(2)}) %collective-permute-start.15) | collective-permute-done | bytes 262176 | tf_op jit(solution)/shard_map/ppermute | solution.py:52
  162.4 3.7 %collective-permute-done.13 = bf16[64,2048]{1,0:T(8,128)(2,1)S(1)} collective-permute-done((bf16[64,2048]{1,0:T(8,128)(2,1)S(1)}, bf16[64,2048]{1,0:T(8,128)(2,1)S(1)}, u32[]{:S(2)}, u32[]{:S(2)}) %collective-permute-start.13) | collective-permute-done | bytes 262176 | tf_op jit(solution)/shard_map/ppermute | solution.py:51
  166.3 17.7 %all_to_all.15 = bf16[16,4,2048]{2,1,0:T(4,128)(2,1)S(1)} all-to-all(bf16[16,4,2048]{2,1,0:T(4,128)(2,1)S(1)} %reshape.66), channel_id=1, replica_groups=mesh['y'=4,'c'=2,'z'=16,'x'=4] {'z'}, dimensions={0} | all-to-all | bytes 524288 | tf_op jit(solution)/shard_map/all_to_all | solution.py:121
  185.4 4.2 %reduce-scatter.2.cloned.1.call-done = bf16[512,384]{0,1:T(8,128)(2,1)} async-done(((bf16[4096,384]{0,1:T(8,128)(2,1)}), bf16[512,384]{0,1:T(8,128)(2,1)}) %reduce-scatter.2.cloned.1.call-update) | async-done | bytes 393232 | tf_op jit(solution)/shard_map/reduce_scatter | solution.py:139
  189.5 12.4 %collective-permute-start.16 = (bf16[512,384]{0,1:T(8,128)(2,1)}, bf16[512,384]{0,1:T(8,128)(2,1)S(1)}, u32[]{:S(2)}, u32[]{:S(2)}) collective-permute-start(bf16[512,384]{0,1:T(8,128)(2,1)} %reduce-scatter.2.cloned.1.call-done), channel_id=1, source_target_pairs={{0,0},{4,64},{8,8},{12,72},{16,16},{20,80},{24,24},{28,88},{32,32}... | collective-permute-start | bytes 1179656 | tf_op jit(solution)/shard_map/ppermute | solution.py:140
  201.9 2.2 fusion.7
  204.1 3.5 %collective-permute-done.16 = bf16[512,384]{0,1:T(8,128)(2,1)S(1)} collective-permute-done((bf16[512,384]{0,1:T(8,128)(2,1)}, bf16[512,384]{0,1:T(8,128)(2,1)S(1)}, u32[]{:S(2)}, u32[]{:S(2)}) %collective-permute-start.16) | collective-permute-done | bytes 393248 | tf_op jit(solution)/shard_map/ppermute | solution.py:140
  (88 shorter events, 11.6 us)
Async XLA Ops:
  7.2 13.7 %copy-start = (bf16[128,4096]{1,0:T(8,128)(2,1)S(1)}, bf16[128,4096]{1,0:T(8,128)(2,1)}, u32[]{:S(2)}) copy-start(bf16[128,4096]{1,0:T(8,128)(2,1)} %param.7) | copy-start | bytes 3145732
  7.2 14.5 %copy-start.3 = (f32[4096]{0:T(1024)S(1)}, f32[4096]{0:T(1024)}, u32[]{:S(2)}) copy-start(f32[4096]{0:T(1024)} %param.11) | copy-start | bytes 49156
  7.2 95.7 %all-gather.2.cloned.1.call-start = ((), (), s32[]{:S(2)}) async-start(), calls=%async_computation.4 | async-start | bytes 3538944 | tf_op jit(solution)/shard_map/all_gather | solution.py:62
  9.3 9.6 %collective-permute-start.4 = (bf16[512,384]{1,0:T(8,128)(2,1)S(1)}, bf16[512,384]{1,0:T(8,128)(2,1)S(1)}, u32[]{:S(2)}, u32[]{:S(2)}) collective-permute-start(bf16[512,384]{1,0:T(8,128)(2,1)S(1)} %pad_maximum_fusion), channel_id=1, source_target_pairs={{0,0},{4,64},{8,8},{12,72},{16,16},{20,80},{24,24},{28,88},{32,32}... | collective-permute-start | bytes 1179656 | tf_op jit(solution)/shard_map/ppermute | solution.py:61
  18.9 0.7 copy-start.2
  20.4 17.7 %copy-start.4 = (pred[128]{0:T(512)(128)(4,1)}, pred[128]{0:T(512)(128)(4,1)S(1)}, u32[]{:S(2)}) copy-start(pred[128]{0:T(512)(128)(4,1)S(1)} %fusion.41) | copy-start | bytes 388
  21.1 0.5 copy-start.6
  21.7 16.4 %copy-start.8 = (s32[128]{0:T(128)}, s32[128]{0:T(128)S(1)}, u32[]{:S(2)}) copy-start(s32[128]{0:T(128)S(1)} %multiply_add_fusion) | copy-start | bytes 1540
  21.7 16.3 %copy-start.10 = (s32[128,2]{0,1:T(2,128)S(1)}, s32[128,2]{0,1:T(2,128)}, u32[]{:S(2)}) copy-start(s32[128,2]{0,1:T(2,128)} %param.9) | copy-start | bytes 3076
  21.7 16.4 %copy-start.11 = (f32[128,2]{0,1:T(2,128)S(1)}, f32[128,2]{0,1:T(2,128)}, u32[]{:S(2)}) copy-start(f32[128,2]{0,1:T(2,128)} %param.10) | copy-start | bytes 3076
  21.7 16.4 %copy-start.1 = (bf16[128,4096]{1,0:T(8,128)(2,1)S(1)}, bf16[128,4096]{1,0:T(8,128)(2,1)}, u32[]{:S(2)}) copy-start(bf16[128,4096]{1,0:T(8,128)(2,1)} %param.8) | copy-start | bytes 3145732
  23.5 28.6 %all-to-all-start.1 = ((bf16[16,4,2048]{2,1,0:T(4,128)(2,1)}), bf16[16,4,2048]{2,1,0:T(4,128)(2,1)S(1)}, u32[]{:S(2)}, u32[]{:S(2)}) async-start(bf16[16,4,2048]{2,1,0:T(4,128)(2,1)} %copy.28), calls=%async_computation.1 | async-start | bytes 524288 | tf_op jit(solution)/shard_map/all_to_all | solution.py:85
  52.1 24.1 %all-to-all-start = ((bf16[16,4,2048]{2,1,0:T(4,128)(2,1)}), bf16[16,4,2048]{2,1,0:T(4,128)(2,1)S(1)}, u32[]{:S(2)}, u32[]{:S(2)}) async-start(bf16[16,4,2048]{2,1,0:T(4,128)(2,1)} %copy.25), calls=%async_computation | async-start | bytes 524288 | tf_op jit(solution)/shard_map/all_to_all | solution.py:86
  62.4 127.2 %reduce-scatter.2.cloned.1.call-start = ((), (), s32[]{:S(2)}) async-start(), calls=%async_computation.5 | async-start | bytes 3538944 | tf_op jit(solution)/shard_map/reduce_scatter | solution.py:139
  63.2 19.4 %collective-permute-start.6 = (bf16[64,2048]{1,0:T(8,128)(2,1)}, bf16[64,2048]{1,0:T(8,128)(2,1)}, u32[]{:S(2)}, u32[]{:S(2)}) collective-permute-start(bf16[64,2048]{1,0:T(8,128)(2,1)} %reshape.65), channel_id=1, source_target_pairs={{0,1},{1,2},{2,3},{3,0},{4,5},{5,6},{6,7},{7,4},{8,9},{9,10},{10,1... | collective-permute-start | bytes 786440 | tf_op jit(solution)/shard_map/ppermute | solution.py:35
  65.3 21.5 %collective-permute-start.7 = (bf16[64,2048]{1,0:T(8,128)(2,1)}, bf16[64,2048]{1,0:T(8,128)(2,1)}, u32[]{:S(2)}, u32[]{:S(2)}) collective-permute-start(bf16[64,2048]{1,0:T(8,128)(2,1)} %reshape.65), channel_id=1, source_target_pairs={{0,3},{1,0},{2,1},{3,2},{4,7},{5,4},{6,5},{7,6},{8,11},{9,8},{10,9... | collective-permute-start | bytes 786440 | tf_op jit(solution)/shard_map/ppermute | solution.py:36
  76.3 13.5 %collective-permute-start = (bf16[64,2048]{1,0:T(8,128)(2,1)S(1)}, bf16[64,2048]{1,0:T(8,128)(2,1)S(1)}, u32[]{:S(2)}, u32[]{:S(2)}) collective-permute-start(bf16[64,2048]{1,0:T(8,128)(2,1)S(1)} %reshape.61), channel_id=1, source_target_pairs={{0,1},{1,2},{2,3},{3,0},{4,5},{5,6},{6,7},{7,4},{8,9},{9,10},{10,1... | collective-permute-start | bytes 786440 | tf_op jit(solution)/shard_map/ppermute | solution.py:35
  78.4 15.9 %collective-permute-start.1 = (bf16[64,2048]{1,0:T(8,128)(2,1)S(1)}, bf16[64,2048]{1,0:T(8,128)(2,1)S(1)}, u32[]{:S(2)}, u32[]{:S(2)}) collective-permute-start(bf16[64,2048]{1,0:T(8,128)(2,1)S(1)} %reshape.61), channel_id=1, source_target_pairs={{0,3},{1,0},{2,1},{3,2},{4,7},{5,4},{6,5},{7,6},{8,11},{9,8},{10,9... | collective-permute-start | bytes 786440 | tf_op jit(solution)/shard_map/ppermute | solution.py:36
  83.5 14.8 %collective-permute-start.8 = (bf16[32,2048]{1,0:T(8,128)(2,1)S(1)}, bf16[32,2048]{1,0:T(8,128)(2,1)S(1)}, u32[]{:S(2)}, u32[]{:S(2)}) collective-permute-start(bf16[32,2048]{1,0:T(8,128)(2,1)S(1)} %slice.112), channel_id=1, source_target_pairs={{0,1},{1,2},{2,3},{3,0},{4,5},{5,6},{6,7},{7,4},{8,9},{9,10},{10,1... | collective-permute-start | bytes 393224 | tf_op jit(solution)/shard_map/ppermute | solution.py:37
  87.8 10.5 %collective-permute-start.9 = (bf16[32,2048]{1,0:T(8,128)(2,1)S(1)}, bf16[32,2048]{1,0:T(8,128)(2,1)S(1)}, u32[]{:S(2)}, u32[]{:S(2)}) collective-permute-start(bf16[32,2048]{1,0:T(8,128)(2,1)S(1)} %slice.113), channel_id=1, source_target_pairs={{0,3},{1,0},{2,1},{3,2},{4,7},{5,4},{6,5},{7,6},{8,11},{9,8},{10,9... | collective-permute-start | bytes 393224 | tf_op jit(solution)/shard_map/ppermute | solution.py:38
  89.8 8.6 %collective-permute-start.2 = (bf16[32,2048]{1,0:T(8,128)(2,1)S(1)}, bf16[32,2048]{1,0:T(8,128)(2,1)S(1)}, u32[]{:S(2)}, u32[]{:S(2)}) collective-permute-start(bf16[32,2048]{1,0:T(8,128)(2,1)S(1)} %slice.108), channel_id=1, source_target_pairs={{0,1},{1,2},{2,3},{3,0},{4,5},{5,6},{6,7},{7,4},{8,9},{9,10},{10,1... | collective-permute-start | bytes 393224 | tf_op jit(solution)/shard_map/ppermute | solution.py:37
  94.3 8.6 %collective-permute-start.3 = (bf16[32,2048]{1,0:T(8,128)(2,1)S(1)}, bf16[32,2048]{1,0:T(8,128)(2,1)S(1)}, u32[]{:S(2)}, u32[]{:S(2)}) collective-permute-start(bf16[32,2048]{1,0:T(8,128)(2,1)S(1)} %slice.109), channel_id=1, source_target_pairs={{0,3},{1,0},{2,1},{3,2},{4,7},{5,4},{6,5},{7,6},{8,11},{9,8},{10,9... | collective-permute-start | bytes 393224 | tf_op jit(solution)/shard_map/ppermute | solution.py:38
  106.5 10.8 %collective-permute-start.10 = (bf16[256,256]{0,1:T(8,128)(2,1)S(1)}, bf16[256,256]{0,1:T(8,128)(2,1)S(1)}, u32[]{:S(2)}, u32[]{:S(2)}) collective-permute-start(bf16[256,256]{0,1:T(8,128)(2,1)S(1)} %get-tuple-element.26), channel_id=1, source_target_pairs={{0,4},{4,0},{8,12},{12,8},{16,20},{20,16},{24,28},{28,24},{32,36},... | collective-permute-start | bytes 393224 | tf_op jit(solution)/shard_map/ppermute | solution.py:96
  115.3 5.0 %collective-permute-start.5 = (bf16[256,128]{0,1:T(8,128)(2,1)S(1)}, bf16[256,128]{0,1:T(8,128)(2,1)S(1)}, u32[]{:S(2)}, u32[]{:S(2)}) collective-permute-start(bf16[256,128]{0,1:T(8,128)(2,1)S(1)} %get-tuple-element.28), channel_id=1, source_target_pairs={{0,4},{4,0},{8,12},{12,8},{16,20},{20,16},{24,28},{28,24},{32,36},... | collective-permute-start | bytes 196616 | tf_op jit(solution)/shard_map/ppermute | solution.py:96
  120.4 6.6 %collective-permute-start.11 = (bf16[256,384]{0,1:T(8,128)(2,1)S(1)}, bf16[256,384]{0,1:T(8,128)(2,1)S(1)}, u32[]{:S(2)}, u32[]{:S(2)}) collective-permute-start(bf16[256,384]{0,1:T(8,128)(2,1)S(1)} %pad_maximum_fusion.3), channel_id=1, source_target_pairs={{0,4},{4,0},{8,12},{12,8},{16,20},{20,16},{24,28},{28,24},{32,36},... | collective-permute-start | bytes 589832 | tf_op jit(solution)/shard_map/ppermute | solution.py:108
  144.2 6.9 %collective-permute-start.12 = (bf16[32,2048]{1,0:T(8,128)(2,1)S(1)}, bf16[32,2048]{1,0:T(8,128)(2,1)S(1)}, u32[]{:S(2)}, u32[]{:S(2)}) collective-permute-start(bf16[32,2048]{1,0:T(8,128)(2,1)S(1)} %get-tuple-element.17), channel_id=1, source_target_pairs={{0,3},{1,0},{2,1},{3,2},{4,7},{5,4},{6,5},{7,6},{8,11},{9,8},{10,9... | collective-permute-start | bytes 393224 | tf_op jit(solution)/shard_map/ppermute | solution.py:47
  146.1 6.5 %collective-permute-start.14 = (bf16[32,2048]{1,0:T(8,128)(2,1)S(1)}, bf16[32,2048]{1,0:T(8,128)(2,1)S(1)}, u32[]{:S(2)}, u32[]{:S(2)}) collective-permute-start(bf16[32,2048]{1,0:T(8,128)(2,1)S(1)} %get-tuple-element.18), channel_id=1, source_target_pairs={{0,1},{1,2},{2,3},{3,0},{4,5},{5,6},{6,7},{7,4},{8,9},{9,10},{10,1... | collective-permute-start | bytes 393224 | tf_op jit(solution)/shard_map/ppermute | solution.py:48
  152.7 9.7 %collective-permute-start.15 = (bf16[64,2048]{1,0:T(8,128)(2,1)S(1)}, bf16[64,2048]{1,0:T(8,128)(2,1)S(1)}, u32[]{:S(2)}, u32[]{:S(2)}) collective-permute-start(bf16[64,2048]{1,0:T(8,128)(2,1)S(1)} %pad_maximum_fusion.2), channel_id=1, source_target_pairs={{0,1},{1,2},{2,3},{3,0},{4,5},{5,6},{6,7},{7,4},{8,9},{9,10},{10,1... | collective-permute-start | bytes 786440 | tf_op jit(solution)/shard_map/ppermute | solution.py:52
  157.7 27.0 %copy-start.5 = (pred[128]{0:T(512)(128)(4,1)S(1)}, pred[128]{0:T(512)(128)(4,1)}, u32[]{:S(2)}) copy-start(pred[128]{0:T(512)(128)(4,1)} %copy-done.4) | copy-start | bytes 388
  157.8 27.0 %copy-start.7 = (f32[128]{0:T(128)S(1)}, f32[128]{0:T(128)}, u32[]{:S(2)}) copy-start(f32[128]{0:T(128)} %copy-done.6) | copy-start | bytes 1540
  157.8 27.0 %copy-start.9 = (s32[128]{0:T(128)S(1)}, s32[128]{0:T(128)}, u32[]{:S(2)}) copy-start(s32[128]{0:T(128)} %copy-done.8) | copy-start | bytes 1540
  157.8 8.3 %collective-permute-start.13 = (bf16[64,2048]{1,0:T(8,128)(2,1)S(1)}, bf16[64,2048]{1,0:T(8,128)(2,1)S(1)}, u32[]{:S(2)}, u32[]{:S(2)}) collective-permute-start(bf16[64,2048]{1,0:T(8,128)(2,1)S(1)} %pad_maximum_fusion.1), channel_id=1, source_target_pairs={{0,3},{1,0},{2,1},{3,2},{4,7},{5,4},{6,5},{7,6},{8,11},{9,8},{10,9... | collective-permute-start | bytes 786440 | tf_op jit(solution)/shard_map/ppermute | solution.py:51
  189.5 18.1 %collective-permute-start.16 = (bf16[512,384]{0,1:T(8,128)(2,1)}, bf16[512,384]{0,1:T(8,128)(2,1)S(1)}, u32[]{:S(2)}, u32[]{:S(2)}) collective-permute-start(bf16[512,384]{0,1:T(8,128)(2,1)} %reduce-scatter.2.cloned.1.call-done), channel_id=1, source_target_pairs={{0,0},{4,64},{8,8},{12,72},{16,16},{20,80},{24,24},{28,88},{32,32}... | collective-permute-start | bytes 1179656 | tf_op jit(solution)/shard_map/ppermute | solution.py:140
Sparse Core Ops, SparseCore 0:
  19.8 37.6 all-gather.1
  140.8 48.6 reduce-scatter.1

commit v2 on v1

v2 whole, which is shorter than its diff:
```python
import jax
import jax.numpy as jnp
from jax import lax
from jax.experimental import pallas as pl
from jax.experimental.pallas import tpu as pltpu
from jax.sharding import Mesh, PartitionSpec as P


CAP = 4
EPS = 1e-06
Y, C, Z, X = 4, 2, 16, 4
GROUPS = 8
HID = 128
D = 4096
HALF = D // 2
CUT = 512
ROWS = 2 * Z * X * CAP
F32 = jnp.float32
BF16 = jnp.bfloat16

SWAP = [
    (c * Z + 2 * e + p, p * Z + 2 * e + c) for c in range(C) for e in range(GROUPS) for p in range(2)
]
FLIP = [(i, i ^ 1) for i in range(Z)]
PLUS = [(i, (i + 1) % X) for i in range(X)]
MINUS = [(i, (i - 1) % X) for i in range(X)]
ORDER = (0, 3, 1, 2)


def shape(dims, kind):
    return jax.ShapeDtypeStruct(dims, kind)


def iota(dims, axis):
    return lax.broadcasted_iota(jnp.int32, dims, axis)


def placing(routes):
    n = routes.shape[1]
    inside = routes < GROUPS
    chosen = jnp.sum(jnp.where(inside, routes, 0), axis=0, keepdims=True)
    present = jnp.sum(inside.astype(jnp.int32), axis=0, keepdims=True) > 0
    onehot = jnp.where((iota((GROUPS, n), 0) == chosen) & present, 1.0, 0.0)
    earlier = jnp.where(iota((n, n), 0) < iota((n, n), 1), 1.0, 0.0)
    rank = jnp.dot(onehot.astype(BF16), earlier.astype(BF16), preferred_element_type=F32)
    slot = jnp.sum(rank * onehot, axis=0, keepdims=True).astype(jnp.int32)
    return jnp.where(present, chosen * CAP + slot, -1)


def send_kernel(routes, gate_w, latent, dout, gain, out, held):
    n = routes.shape[1]
    where_to = placing(routes[...])
    weight = jnp.sum(
        jnp.where(routes[...] < GROUPS, gate_w[...], F32(0.0)), axis=0, keepdims=True
    )
    row = iota((2 * GROUPS * CAP, n), 0)
    hit = (row // 8 * CAP + row % CAP) == where_to
    take_in = hit & (row % 8 < CAP)
    take_dy = hit & (row % 8 >= CAP)
    factor = jnp.sum(jnp.where(take_dy, weight, F32(0.0)), axis=1, keepdims=True)
    take_in = jnp.where(take_in, 1.0, 0.0).astype(BF16)
    take_dy = jnp.where(take_dy, 1.0, 0.0).astype(BF16)
    square = jnp.zeros((2 * GROUPS * CAP, 1), F32)
    for d in range(D // CUT):
        cols = pl.ds(d * CUT, CUT)
        x = jnp.dot(take_in, latent[:, cols], preferred_element_type=F32)
        held[:, cols] = x
        square = square + jnp.sum(x * x, axis=1, keepdims=True)
    inverse = lax.rsqrt(square * (1.0 / D) + EPS)
    for d in range(D // CUT):
        cols = pl.ds(d * CUT, CUT)
        y = jnp.dot(take_dy, dout[:, cols], preferred_element_type=F32)
        value = held[:, cols] * inverse * gain[:, cols] + y * factor
        for e in range(GROUPS):
            out[2 * e + d % 2, :, pl.ds(d // 2 * CUT, CUT)] = value[8 * e : 8 * e + 8].astype(BF16)


def send_rows(routes, gate_w, latent, dout, gain):
    return pl.pallas_call(
        send_kernel,
        out_shape=shape((Z, 8, HALF), BF16),
        scratch_shapes=[pltpu.VMEM((2 * GROUPS * CAP, D), F32)],
        name="send_rows",
    )(routes, gate_w, latent, dout, gain)


def home_kernel(routes, latent, gain, home, out, grad):
    n = routes.shape[1]
    where_to = placing(routes[...])
    take = jnp.where(iota((GROUPS * CAP, n), 0) == where_to, 1.0, 0.0).astype(BF16)
    for z in range(Z):
        for y in range(Y):
            cols = pl.ds((2 * y + z % 2) * CUT, CUT)
            grad[pl.ds(z // 2 * CAP, CAP), cols] = home[z, :, pl.ds(y * CUT, CUT)].astype(F32)
    x = jnp.dot(take, latent[...], preferred_element_type=F32)
    inverse = lax.rsqrt(jnp.sum(x * x, axis=1, keepdims=True) * (1.0 / D) + EPS)
    scaled = x * inverse
    g = grad[...] * gain[...]
    mean = jnp.sum(g * scaled, axis=1, keepdims=True) * (1.0 / D)
    value = (inverse * (g - scaled * mean)).astype(BF16)
    out[...] = lax.dot_general(
        take, value, (((0,), (0,)), ((), ())), preferred_element_type=F32
    ).astype(BF16)


def home_rows(routes, latent, gain, home):
    return pl.pallas_call(
        home_kernel,
        out_shape=shape(latent.shape, BF16),
        scratch_shapes=[pltpu.VMEM((GROUPS * CAP, D), F32)],
        name="home_rows",
    )(routes, latent, gain, home)


def split_rows(both):
    n = both.shape[1]
    turns = both.reshape(ROWS // 16, 2, 8, n)
    first = turns[:, 0].reshape(ROWS // 2, n)
    second = turns[:, 1].reshape(ROWS // 2, n)
    low = iota((ROWS // 2, n), 0) % 8 < 4
    return first, second, low


def turned(value):
    n = value.shape[1]
    tiles = value.reshape(-1, 8, n)
    return pltpu.roll(tiles, 4, 1).reshape(-1, n)


def mix_kernel(place, own, left, right, far_a, far_b, weights, mine, other, total):
    step = pl.program_id(0)
    rows = jnp.concatenate([own[...], left[...], right[...], far_a[...], far_b[...]], axis=0)
    for g in range(2):
        part = jnp.dot(rows, weights[g], preferred_element_type=F32)

        @pl.when(step == 0)
        def _():
            total[g] = part

        @pl.when(step > 0)
        def _():
            total[g] = total[g] + part

    def packed(both):
        first, second, low = split_rows(both)
        pre = jnp.where(
            low[:, : 2 * HID], first[:, : 2 * HID], turned(second[:, : 2 * HID])
        )
        dh = jnp.where(low[:, :HID], turned(first[:, 2 * HID :]), second[:, 2 * HID :])
        return pre, dh

    @pl.when(step == pl.num_programs(0) - 1)
    def _():
        p = place[0]
        pre, dh = packed(total[p])
        mine[:, : 2 * HID] = pre
        mine[:, 2 * HID :] = dh
        pre, dh = packed(total[1 - p])
        other[:, : 2 * HID] = pre.astype(BF16)
        other[:, 2 * HID :] = dh.astype(BF16)


def row_specs():
    return [
        pl.BlockSpec((n, CUT), lambda i, *_: (0, i))
        for n in (ROWS // 4, ROWS // 4, ROWS // 4, ROWS // 8, ROWS // 8)
    ]


def weight_spec():
    return pl.BlockSpec((2, CUT, 3 * HID), lambda i, *_: (0, i, 0))


def whole(dims):
    return pl.BlockSpec(dims, lambda i, *_: (0,) * len(dims))


def mix(place, blocks, weights):
    dims = (ROWS // 2, 3 * HID)
    return pl.pallas_call(
        mix_kernel,
        grid_spec=pltpu.PrefetchScalarGridSpec(
            num_scalar_prefetch=1,
            grid=(HALF // CUT,),
            in_specs=[*row_specs(), weight_spec()],
            out_specs=[whole(dims), whole(dims)],
            scratch_shapes=[pltpu.VMEM((2, ROWS, 3 * HID), F32)],
        ),
        out_shape=[shape(dims, F32), shape(dims, BF16)],
        name="mix",
    )(place, *blocks, weights)


def gates_kernel(mine, got, out):
    total = mine[...] + got[...].astype(F32)
    gate = total[:, :HID]
    up = total[:, HID : 2 * HID]
    dh = total[:, 2 * HID :]
    sig = jax.nn.sigmoid(gate)
    act = gate * sig
    out[:, :HID] = (dh * up * sig * (1.0 + gate * (1.0 - sig))).astype(BF16)
    out[:, HID : 2 * HID] = (dh * act).astype(BF16)
    out[:, 2 * HID :] = (act * up).astype(BF16)


def gates(mine, got):
    return pl.pallas_call(
        gates_kernel, out_shape=shape(mine.shape, BF16), name="gates"
    )(mine, got)


def back_kernel(place, mine, other, weights, out, inner):
    @pl.when(pl.program_id(0) == 0)
    def _():
        inner[place[0]] = mine[...]
        inner[1 - place[0]] = other[...]

    total = sum(
        lax.dot_general(
            inner[g, :, : 2 * HID],
            weights[g, :, : 2 * HID],
            (((1,), (1,)), ((), ())),
            preferred_element_type=F32,
        )
        for g in range(2)
    ).astype(BF16)
    n = ROWS // 8
    for k, off in enumerate(ORDER):
        out[lax.rem(place[1] + off, X)] = total[n * k : n * k + n]


def back(place, mine, other, weights):
    dims = (ROWS // 2, 3 * HID)
    return pl.pallas_call(
        back_kernel,
        grid_spec=pltpu.PrefetchScalarGridSpec(
            num_scalar_prefetch=1,
            grid=(HALF // CUT,),
            in_specs=[whole(dims), whole(dims), weight_spec()],
            out_specs=pl.BlockSpec((X, ROWS // 8, CUT), lambda i, *_: (0, 0, i)),
            scratch_shapes=[pltpu.VMEM((2, *dims), BF16)],
        ),
        out_shape=shape((X, ROWS // 8, HALF), BF16),
        name="back",
    )(place, mine, other, weights)


def grads_kernel(place, mine, other, own, left, right, far_a, far_b, out, inner):
    @pl.when(pl.program_id(0) == 0)
    def _():
        def spread(value, g):
            value = value.astype(F32)
            n = ROWS // 2
            low = iota((n, 2 * HID), 0) % 8 < 4
            pre = value[:, : 2 * HID]
            hid = value[:, 2 * HID :]
            zero = F32(0.0)
            first = jnp.where(low, pre, zero), jnp.where(low[:, :HID], zero, turned(hid))
            second = jnp.where(low, turned(pre), zero), jnp.where(low[:, :HID], zero, hid)
            for k, cols in ((0, pl.ds(0, 2 * HID)), (1, pl.ds(2 * HID, HID))):
                width = first[k].shape[1]
                pair = jnp.stack(
                    [first[k].reshape(-1, 8, width), second[k].reshape(-1, 8, width)], axis=1
                )
                inner[g, :, cols] = pair.reshape(ROWS, width).astype(BF16)

        spread(mine[...], place[0])
        spread(other[...], 1 - place[0])

    rows = jnp.concatenate([own[...], left[...], right[...], far_a[...], far_b[...]], axis=0)
    for g in range(2):
        out[g, 0] = lax.dot_general(
            rows, inner[g], (((0,), (0,)), ((), ())), preferred_element_type=F32
        ).astype(BF16)


def grads(place, mine, other, blocks):
    dims = (ROWS // 2, 3 * HID)
    return pl.pallas_call(
        grads_kernel,
        grid_spec=pltpu.PrefetchScalarGridSpec(
            num_scalar_prefetch=1,
            grid=(HALF // CUT,),
            in_specs=[whole(dims), whole(dims), *row_specs()],
            out_specs=pl.BlockSpec((2, 1, CUT, 3 * HID), lambda i, *_: (0, i, 0, 0)),
            scratch_shapes=[pltpu.VMEM((2, ROWS, 3 * HID), BF16)],
        ),
        out_shape=shape((2, HALF // CUT, CUT, 3 * HID), BF16),
        name="grads",
    )(place, mine, other, *blocks)


def gather_x(own):
    half = own.shape[0] // 2
    left = lax.ppermute(own, "x", PLUS)
    right = lax.ppermute(own, "x", MINUS)
    far_a = lax.ppermute(left[:half], "x", PLUS)
    far_b = lax.ppermute(right[half:], "x", MINUS)
    return own, left, right, far_a, far_b


def work(latent, dout, routes, gate_w, norm_gain, w_gate_up, w_down):
    place = jnp.stack([lax.axis_index("z") % 2, lax.axis_index("x")]).astype(jnp.int32)
    gain = norm_gain[None, :]
    routes = routes.T

    send = send_rows(routes, gate_w.T, latent, dout, gain)
    piece = jnp.concatenate([w_gate_up[0], w_down[0].T], axis=1)
    got = lax.all_to_all(send, "z", 0, 0, tiled=True)
    piece = lax.ppermute(piece, ("c", "z"), SWAP)
    weights = lax.all_gather(piece, ("c", "y"), axis=0, tiled=True)
    weights = weights.reshape(2, HALF, 3 * HID)

    blocks = gather_x(got.reshape(ROWS // 4, HALF))
    mine, other = mix(place, blocks, weights)
    inner = gates(mine, lax.ppermute(other, "z", FLIP))
    outer = lax.ppermute(inner, "z", FLIP)

    grad = grads(place, inner, outer, blocks).reshape(2 * HALF, 3 * HID)
    grad = lax.psum_scatter(grad, ("c", "y"), scatter_dimension=0, tiled=True)
    grad = lax.ppermute(grad, ("c", "z"), SWAP)
    grad_gu = grad[:, : 2 * HID][None]
    grad_d = grad[:, 2 * HID :].T[None]

    part = lax.all_to_all(back(place, inner, outer, weights), "x", 0, 0, tiled=True)
    summed = jnp.sum(part.astype(F32), axis=0).astype(BF16)
    home = lax.all_to_all(summed.reshape(Z, CAP, HALF), "z", 0, 0, tiled=True)
    return home_rows(routes, latent, gain, home), grad_gu, grad_d


def solution(mesh):
    fine = Mesh(mesh.devices.reshape(Y, C, Z, X), ("y", "c", "z", "x"))
    rows = P(("y", "c", "z", "x"), None)
    gate_up = P(("z", "x"), ("y", "c"), None)
    down = P(("z", "x"), None, ("y", "c"))
    return jax.shard_map(
        work,
        mesh=fine,
        in_specs=(rows, rows, rows, rows, P(), gate_up, down),
        out_specs=(rows, gate_up, down),
        check_vma=False,
    )
```

time: 217 us -> 195 us (0.90)
  the two profiles are of different devices: /device:TPU:23 before, /device:TPU:1 now
where the time goes in v2:
time: 195 us; the launch traced here: 194 us
  blocking collectives  50.3 us (26%)
  waiting for transfers between devices  48.6 us (25%)
  starting transfers between devices  44.2 us (23%)
  Pallas kernels  27.7 us (14%)
  between operations  14.2 us (7%)
  local copies, waits for them, and re-layouts  6.88 us (4%)
    all_to_all x1, blocking collectives, work(): got = lax.all_to_all(send, 'z', 0, 0, tiled=True)  37.1 us
    reduce_scatter x1, waiting for transfers between devices, work(): grad = lax.psum_scatter(grad, ('c', 'y'), scatter_dimension=0, tiled=True)  21.2 us
    all_to_all x1, starting transfers between devices, work(): home = lax.all_to_all(summed.reshape(Z, CAP, HALF), 'z', 0, 0, tiled=True)  14.1 us
    all_to_all x1, blocking collectives, work(): lax.all_to_all(back(place, inner, outer, weights), 'x', 0, 0, tiled=True)  13.2 us
    pallas_call x1, Pallas kernels, mix(): pl.pallas_call(mix_kernel, grid_spec=pltpu.PrefetchScalarGridSpec(num_sca...  7.5 us
    pallas_call x1, Pallas kernels, grads(): pl.pallas_call(grads_kernel, grid_spec=pltpu.PrefetchScalarGridSpec(num_s...  6.71 us
    ppermute x1, waiting for transfers between devices, work(): piece = lax.ppermute(piece, ('c', 'z'), SWAP)  5.45 us
    ppermute x1, waiting for transfers between devices, gather_x(): far_a = lax.ppermute(left[:half], 'x', PLUS)  5.31 us
  transfers between devices with their start and end apart: 11, of which 8 were waited for; matrix products, arithmetic and copies ran while one was open for 1% of the time, Pallas kernels for 6%

profile of v2, /device:TPU:1, one launch (start us, length us, event | category | flops | bytes accessed | tf_op | source)
XLA Modules:
  0.0 193.7 jit_solution(729536112400541418)
XLA Ops:
  7.2 0.0 all-gather.2.cloned.1.call-start
  7.2 1.0 copy.12
  8.2 1.0 pad_maximum_fusion
  9.2 4.9 %collective-permute-start.4 = (bf16[512,384]{1,0:T(8,128)(2,1)S(1)}, bf16[512,384]{1,0:T(8,128)(2,1)S(1)}, u32[]{:S(2)}, u32[]{:S(2)}) collective-permute-start(bf16[512,384]{1,0:T(8,128)(2,1)S(1)} %pad_maximum_fusion), channel_id=1, source_target_pairs={{0,0},{4,64},{8,8},{12,72},{16,16},{20,80},{24,24},{28,88},{32,32}... | collective-permute-start | bytes 1179656 | tf_op jit(solution)/shard_map/ppermute | solution.py:310
  14.2 5.4 %collective-permute-done.4 = bf16[512,384]{1,0:T(8,128)(2,1)S(1)} collective-permute-done((bf16[512,384]{1,0:T(8,128)(2,1)S(1)}, bf16[512,384]{1,0:T(8,128)(2,1)S(1)}, u32[]{:S(2)}, u32[]{:S(2)}) %collective-permute-start.4) | collective-permute-done | bytes 393248 | tf_op jit(solution)/shard_map/ppermute | solution.py:310
  19.6 0.8 copy-done.7
  20.4 0.0 all-gather.2.cloned.1.call-update
  20.4 0.0 reduce-scatter.2.cloned.1.call-start
  20.5 3.1 %send_rows.1 = bf16[16,8,2048]{2,1,0:T(8,128)(2,1)} custom-call(s32[2,128]{1,0:T(2,128)} %bitcast.29, f32[2,128]{1,0:T(2,128)} %bitcast.31, bf16[128,4096]{1,0:T(8,128)(2,1)} %latent.3, bf16[128,4096]{1,0:T(8,128)(2,1)} %dout.1, f32[1,4096]{1,0:T(1,128)} %bitcast.27), custom_call_target="tpu_custom_call" | custom-call | tf_op jit(solution)/shard_map/send_rows/pallas_call | solution.py:79
  23.5 37.1 %all_to_all.15 = bf16[16,8,2048]{2,1,0:T(8,128)(2,1)S(1)} all-to-all(bf16[16,8,2048]{2,1,0:T(8,128)(2,1)} %send_rows.1), channel_id=1, replica_groups=mesh['y'=4,'c'=2,'z'=16,'x'=4] {'z'}, dimensions={0} | all-to-all | bytes 1048576 | tf_op jit(solution)/shard_map/all_to_all | solution.py:309
  60.6 4.4 %collective-permute-start.1 = (bf16[128,2048]{1,0:T(8,128)(2,1)S(1)}, bf16[128,2048]{1,0:T(8,128)(2,1)S(1)}, u32[]{:S(2)}, u32[]{:S(2)}) collective-permute-start(bf16[128,2048]{1,0:T(8,128)(2,1)S(1)} %bitcast.21), channel_id=1, source_target_pairs={{0,3},{1,0},{2,1},{3,2},{4,7},{5,4},{6,5},{7,6},{8,11},{9,8},{10,9... | collective-permute-start | bytes 1572872 | tf_op jit(solution)/shard_map/ppermute | solution.py:296
  65.0 1.9 collective-permute-start
  67.0 4.2 %collective-permute-done.1.right = bf16[128,2048]{1,0:T(8,128)(2,1)S(1)} collective-permute-done((bf16[128,2048]{1,0:T(8,128)(2,1)S(1)}, bf16[128,2048]{1,0:T(8,128)(2,1)S(1)}, u32[]{:S(2)}, u32[]{:S(2)}) %collective-permute-start.1) | collective-permute-done | bytes 524320 | tf_op jit(solution)/shard_map/ppermute | solution.py:296
  71.2 5.0 %collective-permute-start.3 = (bf16[64,2048]{1,0:T(8,128)(2,1)S(1)}, bf16[64,2048]{1,0:T(8,128)(2,1)S(1)}, u32[]{:S(2)}, u32[]{:S(2)}) collective-permute-start(bf16[64,2048]{1,0:T(8,128)(2,1)S(1)} %slice.17), channel_id=1, source_target_pairs={{0,3},{1,0},{2,1},{3,2},{4,7},{5,4},{6,5},{7,6},{8,11},{9,8},{10,9... | collective-permute-start | bytes 786440 | tf_op jit(solution)/shard_map/ppermute | solution.py:298
  76.2 0.0 collective-permute-done.left
  76.2 0.0 copy-start.2
  76.2 1.9 collective-permute-start.2
  78.2 0.6 pad_add_fusion.place
  78.8 2.7 %collective-permute-done.3.far_b = bf16[64,2048]{1,0:T(8,128)(2,1)S(1)} collective-permute-done((bf16[64,2048]{1,0:T(8,128)(2,1)S(1)}, bf16[64,2048]{1,0:T(8,128)(2,1)S(1)}, u32[]{:S(2)}, u32[]{:S(2)}) %collective-permute-start.3) | collective-permute-done | bytes 262176 | tf_op jit(solution)/shard_map/ppermute | solution.py:298
  81.5 5.3 %collective-permute-done.2.far_a = bf16[64,2048]{1,0:T(8,128)(2,1)S(1)} collective-permute-done((bf16[64,2048]{1,0:T(8,128)(2,1)S(1)}, bf16[64,2048]{1,0:T(8,128)(2,1)S(1)}, u32[]{:S(2)}, u32[]{:S(2)}) %collective-permute-start.2) | collective-permute-done | bytes 262176 | tf_op jit(solution)/shard_map/ppermute | solution.py:297
  86.9 0.0 copy-done
  86.9 0.0 copy-done.1
  86.9 0.0 copy-done.2
  86.9 0.7 copy-done.5
  87.6 7.5 %mix.1 = (f32[256,384]{1,0:T(8,128)}, bf16[256,384]{1,0:T(8,128)(2,1)}) custom-call(s32[2]{0:T(128)} %pad_add_fusion.place, bf16[128,2048]{1,0:T(8,128)(2,1)} %bitcast.23, bf16[128,2048]{1,0:T(8,128)(2,1)} %copy-done.2, bf16[128,2048]{1,0:T(8,128)(2,1)} %copy-done.1, bf16[64,2048]{1,0:T(8,128)(2,1)} %copy-done.5, bf16[64,2048]{1,0:T(8,128)(2,1)} %copy-done.4, ...), custom_call_target="tpu_custom_call" | custom-call | tf_op jit(solution)/shard_map/mix/pallas_call | solution.py:180
  95.1 5.0 %collective-permute-start.5 = (bf16[256,384]{1,0:T(8,128)(2,1)}, bf16[256,384]{1,0:T(8,128)(2,1)S(1)}, u32[]{:S(2)}, u32[]{:S(2)}) collective-permute-start(bf16[256,384]{1,0:T(8,128)(2,1)} %get-tuple-element.6), channel_id=1, source_target_pairs={{0,4},{4,0},{8,12},{12,8},{16,20},{20,16},{24,28},{28,24},{32,36},... | collective-permute-start | bytes 589832 | tf_op jit(solution)/shard_map/ppermute | solution.py:316
  100.1 3.3 %collective-permute-done.5.got = bf16[256,384]{1,0:T(8,128)(2,1)S(1)} collective-permute-done((bf16[256,384]{1,0:T(8,128)(2,1)}, bf16[256,384]{1,0:T(8,128)(2,1)S(1)}, u32[]{:S(2)}, u32[]{:S(2)}) %collective-permute-start.5) | collective-permute-done | bytes 196640 | tf_op jit(solution)/shard_map/ppermute | solution.py:316
  103.4 0.7 copy-done.8
  104.0 1.8 gates.1.mine
  105.9 3.3 %collective-permute-start.6 = (bf16[256,384]{1,0:T(8,128)(2,1)}, bf16[256,384]{1,0:T(8,128)(2,1)S(1)}, u32[]{:S(2)}, u32[]{:S(2)}) collective-permute-start(bf16[256,384]{1,0:T(8,128)(2,1)} %gates.1.mine), channel_id=1, source_target_pairs={{0,4},{4,0},{8,12},{12,8},{16,20},{20,16},{24,28},{28,24},{32,36},... | collective-permute-start | bytes 589832 | tf_op jit(solution)/shard_map/ppermute | solution.py:317
  109.2 4.7 %collective-permute-done.6.other = bf16[256,384]{1,0:T(8,128)(2,1)S(1)} collective-permute-done((bf16[256,384]{1,0:T(8,128)(2,1)}, bf16[256,384]{1,0:T(8,128)(2,1)S(1)}, u32[]{:S(2)}, u32[]{:S(2)}) %collective-permute-start.6) | collective-permute-done | bytes 196640 | tf_op jit(solution)/shard_map/ppermute | solution.py:317
  113.9 0.7 copy-done.6
  114.6 6.7 %grads.1 = bf16[2,4,512,384]{3,2,1,0:T(8,128)(2,1)} custom-call(s32[2]{0:T(128)} %pad_add_fusion.place, bf16[256,384]{1,0:T(8,128)(2,1)} %gates.1.mine, bf16[256,384]{1,0:T(8,128)(2,1)} %copy-done.6, bf16[128,2048]{1,0:T(8,128)(2,1)} %bitcast.24, bf16[128,2048]{1,0:T(8,128)(2,1)} %copy-done.2, bf16[128,2048]{1,0:T(8,128)(2,1)} %copy-done.1, ...), custom_call_target="tpu_custom_call" | custom-call | tf_op jit(solution)/shard_map/grads/pallas_call | solution.py:279
  121.3 0.0 reduce-scatter.2.cloned.1.call-update
  121.3 5.2 %back.1 = bf16[4,64,2048]{2,1,0:T(8,128)(2,1)} custom-call(s32[2]{0:T(128)} %pad_add_fusion.place, bf16[256,384]{1,0:T(8,128)(2,1)} %gates.1.mine, bf16[256,384]{1,0:T(8,128)(2,1)} %copy-done.6, bf16[2,2048,384]{2,1,0:T(8,128)(2,1)} %bitcast.20), custom_call_target="tpu_custom_call" | custom-call | tf_op jit(solution)/shard_map/back/pallas_call | solution.py:234
  126.5 13.2 %all_to_all.16 = bf16[4,64,2048]{2,1,0:T(8,128)(2,1)S(1)} all-to-all(bf16[4,64,2048]{2,1,0:T(8,128)(2,1)} %back.1), channel_id=1, replica_groups=mesh['y'=4,'c'=2,'z'=16,'x'=4] {'x'}, dimensions={0} | all-to-all | bytes 2097152 | tf_op jit(solution)/shard_map/all_to_all | solution.py:325
  139.7 0.2 reduce_sum.12
  139.9 0.8 reshape.20
  140.8 14.1 %all-to-all-start.2 = ((bf16[16,4,2048]{2,1,0:T(4,128)(2,1)}), bf16[16,4,2048]{2,1,0:T(4,128)(2,1)S(1)}, u32[]{:S(2)}, u32[]{:S(2)}) async-start(bf16[16,4,2048]{2,1,0:T(4,128)(2,1)} %reshape.20), calls=%async_computation.2 | async-start | bytes 524288 | tf_op jit(solution)/shard_map/all_to_all | solution.py:327
  154.9 21.2 %reduce-scatter.2.cloned.1.call-done = bf16[512,384]{1,0:T(8,128)(2,1)} async-done(((bf16[4096,384]{1,0:T(8,128)(2,1)}), bf16[512,384]{1,0:T(8,128)(2,1)}) %reduce-scatter.2.cloned.1.call-update) | async-done | bytes 393232 | tf_op jit(solution)/shard_map/reduce_scatter | solution.py:320
  176.1 3.4 %collective-permute-start.7 = (bf16[512,384]{1,0:T(8,128)(2,1)}, bf16[512,384]{1,0:T(8,128)(2,1)S(1)}, u32[]{:S(2)}, u32[]{:S(2)}) collective-permute-start(bf16[512,384]{1,0:T(8,128)(2,1)} %reduce-scatter.2.cloned.1.call-done), channel_id=1, source_target_pairs={{0,0},{4,64},{8,8},{12,72},{16,16},{20,80},{24,24},{28,88},{32,32}... | collective-permute-start | bytes 1179656 | tf_op jit(solution)/shard_map/ppermute | solution.py:321
  179.5 0.0 all-to-all-done.2.home
  179.5 0.0 copy-start.3
  179.5 0.7 copy-done.3
  180.2 3.3 %home_rows.1 = bf16[128,4096]{1,0:T(8,128)(2,1)} custom-call(s32[2,128]{1,0:T(2,128)} %bitcast.30, bf16[128,4096]{1,0:T(8,128)(2,1)} %latent.3, f32[1,4096]{1,0:T(1,128)} %bitcast.28, bf16[16,4,2048]{2,1,0:T(4,128)(2,1)} %copy-done.3), custom_call_target="tpu_custom_call" | custom-call | tf_op jit(solution)/shard_map/home_rows/pallas_call | solution.py:107
  183.6 1.8 collective-permute-done.7
  185.4 0.8 copy.13
  186.2 0.7 slice_bitcast_fusion
  (12 shorter events, 0.1 us)
Async XLA Ops:
  7.2 79.7 %all-gather.2.cloned.1.call-start = ((), (), s32[]{:S(2)}) async-start(), calls=%async_computation.4 | async-start | bytes 3538944 | tf_op jit(solution)/shard_map/all_gather | solution.py:311
  9.2 10.4 %collective-permute-start.4 = (bf16[512,384]{1,0:T(8,128)(2,1)S(1)}, bf16[512,384]{1,0:T(8,128)(2,1)S(1)}, u32[]{:S(2)}, u32[]{:S(2)}) collective-permute-start(bf16[512,384]{1,0:T(8,128)(2,1)S(1)} %pad_maximum_fusion), channel_id=1, source_target_pairs={{0,0},{4,64},{8,8},{12,72},{16,16},{20,80},{24,24},{28,88},{32,32}... | collective-permute-start | bytes 1179656 | tf_op jit(solution)/shard_map/ppermute | solution.py:310
  19.6 0.8 copy-start.7
  20.4 155.7 %reduce-scatter.2.cloned.1.call-start = ((), (), s32[]{:S(2)}) async-start(), calls=%async_computation.5 | async-start | bytes 3538944 | tf_op jit(solution)/shard_map/reduce_scatter | solution.py:320
  60.6 26.2 %copy-start = (bf16[16,8,2048]{2,1,0:T(8,128)(2,1)}, bf16[16,8,2048]{2,1,0:T(8,128)(2,1)S(1)}, u32[]{:S(2)}) copy-start(bf16[16,8,2048]{2,1,0:T(8,128)(2,1)S(1)} %all_to_all.15) | copy-start | bytes 1572868
  60.6 10.5 %collective-permute-start.1 = (bf16[128,2048]{1,0:T(8,128)(2,1)S(1)}, bf16[128,2048]{1,0:T(8,128)(2,1)S(1)}, u32[]{:S(2)}, u32[]{:S(2)}) collective-permute-start(bf16[128,2048]{1,0:T(8,128)(2,1)S(1)} %bitcast.21), channel_id=1, source_target_pairs={{0,3},{1,0},{2,1},{3,2},{4,7},{5,4},{6,5},{7,6},{8,11},{9,8},{10,9... | collective-permute-start | bytes 1572872 | tf_op jit(solution)/shard_map/ppermute | solution.py:296
  65.0 11.2 %collective-permute-start = (bf16[128,2048]{1,0:T(8,128)(2,1)S(1)}, bf16[128,2048]{1,0:T(8,128)(2,1)S(1)}, u32[]{:S(2)}, u32[]{:S(2)}) collective-permute-start(bf16[128,2048]{1,0:T(8,128)(2,1)S(1)} %bitcast.22), channel_id=1, source_target_pairs={{0,1},{1,2},{2,3},{3,0},{4,5},{5,6},{6,7},{7,4},{8,9},{9,10},{10,1... | collective-permute-start | bytes 1572872 | tf_op jit(solution)/shard_map/ppermute | solution.py:295
  71.1 15.7 %copy-start.1 = (bf16[128,2048]{1,0:T(8,128)(2,1)}, bf16[128,2048]{1,0:T(8,128)(2,1)S(1)}, u32[]{:S(2)}) copy-start(bf16[128,2048]{1,0:T(8,128)(2,1)S(1)} %collective-permute-done.1.right) | copy-start | bytes 1572868
  71.2 10.4 %collective-permute-start.3 = (bf16[64,2048]{1,0:T(8,128)(2,1)S(1)}, bf16[64,2048]{1,0:T(8,128)(2,1)S(1)}, u32[]{:S(2)}, u32[]{:S(2)}) collective-permute-start(bf16[64,2048]{1,0:T(8,128)(2,1)S(1)} %slice.17), channel_id=1, source_target_pairs={{0,3},{1,0},{2,1},{3,2},{4,7},{5,4},{6,5},{7,6},{8,11},{9,8},{10,9... | collective-permute-start | bytes 786440 | tf_op jit(solution)/shard_map/ppermute | solution.py:298
  76.2 10.7 %copy-start.2 = (bf16[128,2048]{1,0:T(8,128)(2,1)}, bf16[128,2048]{1,0:T(8,128)(2,1)S(1)}, u32[]{:S(2)}) copy-start(bf16[128,2048]{1,0:T(8,128)(2,1)S(1)} %collective-permute-done.left) | copy-start | bytes 1572868
  76.2 10.6 %collective-permute-start.2 = (bf16[64,2048]{1,0:T(8,128)(2,1)S(1)}, bf16[64,2048]{1,0:T(8,128)(2,1)S(1)}, u32[]{:S(2)}, u32[]{:S(2)}) collective-permute-start(bf16[64,2048]{1,0:T(8,128)(2,1)S(1)} %slice.16), channel_id=1, source_target_pairs={{0,1},{1,2},{2,3},{3,0},{4,5},{5,6},{6,7},{7,4},{8,9},{9,10},{10,1... | collective-permute-start | bytes 786440 | tf_op jit(solution)/shard_map/ppermute | solution.py:297
  81.5 5.3 %copy-start.4 = (bf16[64,2048]{1,0:T(8,128)(2,1)}, bf16[64,2048]{1,0:T(8,128)(2,1)S(1)}, u32[]{:S(2)}) copy-start(bf16[64,2048]{1,0:T(8,128)(2,1)S(1)} %collective-permute-done.3.far_b) | copy-start | bytes 786436
  86.9 0.7 copy-start.5
  95.1 8.3 %collective-permute-start.5 = (bf16[256,384]{1,0:T(8,128)(2,1)}, bf16[256,384]{1,0:T(8,128)(2,1)S(1)}, u32[]{:S(2)}, u32[]{:S(2)}) collective-permute-start(bf16[256,384]{1,0:T(8,128)(2,1)} %get-tuple-element.6), channel_id=1, source_target_pairs={{0,4},{4,0},{8,12},{12,8},{16,20},{20,16},{24,28},{28,24},{32,36},... | collective-permute-start | bytes 589832 | tf_op jit(solution)/shard_map/ppermute | solution.py:316
  103.4 0.7 copy-start.8
  105.9 8.0 %collective-permute-start.6 = (bf16[256,384]{1,0:T(8,128)(2,1)}, bf16[256,384]{1,0:T(8,128)(2,1)S(1)}, u32[]{:S(2)}, u32[]{:S(2)}) collective-permute-start(bf16[256,384]{1,0:T(8,128)(2,1)} %gates.1.mine), channel_id=1, source_target_pairs={{0,4},{4,0},{8,12},{12,8},{16,20},{20,16},{24,28},{28,24},{32,36},... | collective-permute-start | bytes 589832 | tf_op jit(solution)/shard_map/ppermute | solution.py:317
  113.9 0.7 copy-start.6
  140.8 38.8 %all-to-all-start.2 = ((bf16[16,4,2048]{2,1,0:T(4,128)(2,1)}), bf16[16,4,2048]{2,1,0:T(4,128)(2,1)S(1)}, u32[]{:S(2)}, u32[]{:S(2)}) async-start(bf16[16,4,2048]{2,1,0:T(4,128)(2,1)} %reshape.20), calls=%async_computation.2 | async-start | bytes 524288 | tf_op jit(solution)/shard_map/all_to_all | solution.py:327
  176.1 9.3 %collective-permute-start.7 = (bf16[512,384]{1,0:T(8,128)(2,1)}, bf16[512,384]{1,0:T(8,128)(2,1)S(1)}, u32[]{:S(2)}, u32[]{:S(2)}) collective-permute-start(bf16[512,384]{1,0:T(8,128)(2,1)} %reduce-scatter.2.cloned.1.call-done), channel_id=1, source_target_pairs={{0,0},{4,64},{8,8},{12,72},{16,16},{20,80},{24,24},{28,88},{32,32}... | collective-permute-start | bytes 1179656 | tf_op jit(solution)/shard_map/ppermute | solution.py:321
  179.5 0.7 copy-start.3
Sparse Core Ops, SparseCore 0:
  20.5 39.3 all-gather.1
  121.4 54.6 reduce-scatter.1

commit v3 on v2

--- a/solution.py
+++ b/solution.py
@@ -1,3 +1,5 @@
+import functools
+
 import jax
 import jax.numpy as jnp
 from jax import lax
@@ -47,7 +49,9 @@
     return jnp.where(present, chosen * CAP + slot, -1)
 
 
-def send_kernel(routes, gate_w, latent, dout, gain, out, held):
+def send_kernel(routes, gate_w, latent, dout, gain, gate_up, down, out, piece, held):
+    piece[:, : 2 * HID] = gate_up[0]
+    piece[:, 2 * HID :] = down[0].astype(F32).T.astype(BF16)
     n = routes.shape[1]
     where_to = placing(routes[...])
     weight = jnp.sum(
@@ -75,13 +79,21 @@
             out[2 * e + d % 2, :, pl.ds(d // 2 * CUT, CUT)] = value[8 * e : 8 * e + 8].astype(BF16)
 
 
-def send_rows(routes, gate_w, latent, dout, gain):
+def send_rows(*args):
     return pl.pallas_call(
         send_kernel,
-        out_shape=shape((Z, 8, HALF), BF16),
+        out_shape=[shape((Z, 8, HALF), BF16), shape((CUT, 3 * HID), BF16)],
         scratch_shapes=[pltpu.VMEM((2 * GROUPS * CAP, D), F32)],
         name="send_rows",
-    )(routes, gate_w, latent, dout, gain)
+    )(*args)
+
+
+def hold_kernel(piece, out):
+    out[...] = piece[...]
+
+
+def hold(piece):
+    return pl.pallas_call(hold_kernel, out_shape=shape(piece.shape, BF16), name="hold")(piece)
 
 
 def home_kernel(routes, latent, gain, home, out, grad):
@@ -112,24 +124,19 @@
     )(routes, latent, gain, home)
 
 
-def split_rows(both):
-    n = both.shape[1]
-    turns = both.reshape(ROWS // 16, 2, 8, n)
-    first = turns[:, 0].reshape(ROWS // 2, n)
-    second = turns[:, 1].reshape(ROWS // 2, n)
-    low = iota((ROWS // 2, n), 0) % 8 < 4
-    return first, second, low
-
-
 def turned(value):
     n = value.shape[1]
     tiles = value.reshape(-1, 8, n)
     return pltpu.roll(tiles, 4, 1).reshape(-1, n)
 
 
-def mix_kernel(place, own, left, right, far_a, far_b, weights, mine, other, total):
+def mix_kernel(count, place, *refs):
+    blocks, weights = refs[:count], refs[count]
+    mine, other, total = refs[-3:]
     step = pl.program_id(0)
-    rows = jnp.concatenate([own[...], left[...], right[...], far_a[...], far_b[...]], axis=0)
+    rows = blocks[0][...]
+    if count > 1:
+        rows = jnp.concatenate([block[...] for block in blocks], axis=0)
     for g in range(2):
         part = jnp.dot(rows, weights[g], preferred_element_type=F32)
 
@@ -142,20 +149,20 @@
             total[g] = total[g] + part
 
     def packed(both):
-        first, second, low = split_rows(both)
-        pre = jnp.where(
-            low[:, : 2 * HID], first[:, : 2 * HID], turned(second[:, : 2 * HID])
-        )
+        turns = both.reshape(-1, 2, 8, 3 * HID)
+        first = turns[:, 0].reshape(-1, 3 * HID)
+        second = turns[:, 1].reshape(-1, 3 * HID)
+        low = iota((first.shape[0], 2 * HID), 0) % 8 < 4
+        pre = jnp.where(low, first[:, : 2 * HID], turned(second[:, : 2 * HID]))
         dh = jnp.where(low[:, :HID], turned(first[:, 2 * HID :]), second[:, 2 * HID :])
         return pre, dh
 
     @pl.when(step == pl.num_programs(0) - 1)
     def _():
-        p = place[0]
-        pre, dh = packed(total[p])
+        pre, dh = packed(total[place[0]])
         mine[:, : 2 * HID] = pre
         mine[:, 2 * HID :] = dh
-        pre, dh = packed(total[1 - p])
+        pre, dh = packed(total[1 - place[0]])
         other[:, : 2 * HID] = pre.astype(BF16)
         other[:, 2 * HID :] = dh.astype(BF16)
 
@@ -175,20 +182,28 @@
     return pl.BlockSpec(dims, lambda i, *_: (0,) * len(dims))
 
 
-def mix(place, blocks, weights):
+def mix(place, at, blocks, weights, so_far):
+    rows = sum(block.shape[0] for block in blocks)
+    part = pl.BlockSpec((rows // 2, 3 * HID), lambda i, *_: (at, 0))
     dims = (ROWS // 2, 3 * HID)
-    return pl.pallas_call(
-        mix_kernel,
+    hold = [pl.BlockSpec(memory_space=pl.ANY)] * len(so_far)
+    first = 2 + len(blocks)
+    return pl.pallas_call(
+        functools.partial(mix_kernel, len(blocks)),
         grid_spec=pltpu.PrefetchScalarGridSpec(
             num_scalar_prefetch=1,
             grid=(HALF // CUT,),
-            in_specs=[*row_specs(), weight_spec()],
-            out_specs=[whole(dims), whole(dims)],
-            scratch_shapes=[pltpu.VMEM((2, ROWS, 3 * HID), F32)],
+            in_specs=[
+                *[pl.BlockSpec((b.shape[0], CUT), lambda i, *_: (0, i)) for b in blocks],
+                weight_spec(),
+                *hold,
+            ],
+            out_specs=[part, part],
+            scratch_shapes=[pltpu.VMEM((2, rows, 3 * HID), F32)],
         ),
         out_shape=[shape(dims, F32), shape(dims, BF16)],
-        name="mix",
-    )(place, *blocks, weights)
+        input_output_aliases={first + k: k for k in range(len(so_far))},
+    )(place, *blocks, weights, *so_far)
 
 
 def gates_kernel(mine, got, out):
@@ -245,84 +260,91 @@
     )(place, mine, other, weights)
 
 
-def grads_kernel(place, mine, other, own, left, right, far_a, far_b, out, inner):
+def grads_kernel(place, value, own, left, right, far_a, far_b, *refs):
+    out, inner = refs[-2:]
+
     @pl.when(pl.program_id(0) == 0)
     def _():
-        def spread(value, g):
-            value = value.astype(F32)
-            n = ROWS // 2
-            low = iota((n, 2 * HID), 0) % 8 < 4
-            pre = value[:, : 2 * HID]
-            hid = value[:, 2 * HID :]
-            zero = F32(0.0)
-            first = jnp.where(low, pre, zero), jnp.where(low[:, :HID], zero, turned(hid))
-            second = jnp.where(low, turned(pre), zero), jnp.where(low[:, :HID], zero, hid)
-            for k, cols in ((0, pl.ds(0, 2 * HID)), (1, pl.ds(2 * HID, HID))):
-                width = first[k].shape[1]
-                pair = jnp.stack(
-                    [first[k].reshape(-1, 8, width), second[k].reshape(-1, 8, width)], axis=1
-                )
-                inner[g, :, cols] = pair.reshape(ROWS, width).astype(BF16)
-
-        spread(mine[...], place[0])
-        spread(other[...], 1 - place[0])
+        both = value[...].astype(F32)
+        low = iota((ROWS // 2, 2 * HID), 0) % 8 < 4
+        pre = both[:, : 2 * HID]
+        hid = both[:, 2 * HID :]
+        zero = F32(0.0)
+        first = jnp.where(low, pre, zero), jnp.where(low[:, :HID], zero, turned(hid))
+        second = jnp.where(low, turned(pre), zero), jnp.where(low[:, :HID], zero, hid)
+        for k, cols in ((0, pl.ds(0, 2 * HID)), (1, pl.ds(2 * HID, HID))):
+            width = first[k].shape[1]
+            pair = jnp.stack(
+                [first[k].reshape(-1, 8, width), second[k].reshape(-1, 8, width)], axis=1
+            )
+            inner[:, cols] = pair.reshape(ROWS, width).astype(BF16)
 
     rows = jnp.concatenate([own[...], left[...], right[...], far_a[...], far_b[...]], axis=0)
-    for g in range(2):
-        out[g, 0] = lax.dot_general(
-            rows, inner[g], (((0,), (0,)), ((), ())), preferred_element_type=F32
-        ).astype(BF16)
-
-
-def grads(place, mine, other, blocks):
-    dims = (ROWS // 2, 3 * HID)
+    out[0, 0] = lax.dot_general(
+        rows, inner[...], (((0,), (0,)), ((), ())), preferred_element_type=F32
+    ).astype(BF16)
+
+
+def grads(place, turn, value, blocks, so_far):
+    hold = [pl.BlockSpec(memory_space=pl.ANY)] * len(so_far)
+
+    def at(i, place):
+        slot = place[2]
+        return (slot if turn == 0 else 1 - slot), i, 0, 0
+
     return pl.pallas_call(
         grads_kernel,
         grid_spec=pltpu.PrefetchScalarGridSpec(
             num_scalar_prefetch=1,
             grid=(HALF // CUT,),
-            in_specs=[whole(dims), whole(dims), *row_specs()],
-            out_specs=pl.BlockSpec((2, 1, CUT, 3 * HID), lambda i, *_: (0, i, 0, 0)),
-            scratch_shapes=[pltpu.VMEM((2, ROWS, 3 * HID), BF16)],
+            in_specs=[whole((ROWS // 2, 3 * HID)), *row_specs(), *hold],
+            out_specs=pl.BlockSpec((1, 1, CUT, 3 * HID), at),
+            scratch_shapes=[pltpu.VMEM((ROWS, 3 * HID), BF16)],
         ),
         out_shape=shape((2, HALF // CUT, CUT, 3 * HID), BF16),
-        name="grads",
-    )(place, mine, other, *blocks)
-
-
-def gather_x(own):
+        input_output_aliases={2 + len(blocks): 0} if so_far else {},
+    )(place, value, *blocks, *so_far)
+
+
+def work(latent, dout, routes, gate_w, norm_gain, w_gate_up, w_down):
+    zp = lax.axis_index("z") % 2
+    core = lax.axis_index("c")
+    place = jnp.stack([zp, lax.axis_index("x"), (zp + core) % 2]).astype(jnp.int32)
+    gain = norm_gain[None, :]
+    routes = routes.T
+
+    send, piece = send_rows(routes, gate_w.T, latent, dout, gain, w_gate_up, w_down)
+    piece = lax.ppermute(piece, ("c", "z"), SWAP)
+    got = lax.all_to_all(send, "z", 0, 0, tiled=True)
+    weights = lax.all_gather(hold(piece), ("c", "y"), axis=0, tiled=True)
+    weights = weights.reshape(2, HALF, 3 * HID)
+
+    own = got.reshape(ROWS // 4, HALF)
     half = own.shape[0] // 2
     left = lax.ppermute(own, "x", PLUS)
     right = lax.ppermute(own, "x", MINUS)
     far_a = lax.ppermute(left[:half], "x", PLUS)
     far_b = lax.ppermute(right[half:], "x", MINUS)
-    return own, left, right, far_a, far_b
-
-
-def work(latent, dout, routes, gate_w, norm_gain, w_gate_up, w_down):
-    place = jnp.stack([lax.axis_index("z") % 2, lax.axis_index("x")]).astype(jnp.int32)
-    gain = norm_gain[None, :]
-    routes = routes.T
-
-    send = send_rows(routes, gate_w.T, latent, dout, gain)
-    piece = jnp.concatenate([w_gate_up[0], w_down[0].T], axis=1)
-    got = lax.all_to_all(send, "z", 0, 0, tiled=True)
-    piece = lax.ppermute(piece, ("c", "z"), SWAP)
-    weights = lax.all_gather(piece, ("c", "y"), axis=0, tiled=True)
-    weights = weights.reshape(2, HALF, 3 * HID)
-
-    blocks = gather_x(got.reshape(ROWS // 4, HALF))
-    mine, other = mix(place, blocks, weights)
+    blocks = own, left, right, far_a, far_b
+
+    parts = ()
+    for at, some in enumerate(((own,), (left,), (right,), (far_a, far_b))):
+        parts = mix(place, at, some, weights, parts)
+    mine, other = parts
     inner = gates(mine, lax.ppermute(other, "z", FLIP))
     outer = lax.ppermute(inner, "z", FLIP)
 
-    grad = grads(place, inner, outer, blocks).reshape(2 * HALF, 3 * HID)
-    grad = lax.psum_scatter(grad, ("c", "y"), scatter_dimension=0, tiled=True)
+    grad = grads(place, 0, inner, blocks, ())
+    part = back(place, inner, outer, weights)
+    part = lax.all_to_all(part, "x", 0, 0, tiled=True)
+    grad = grads(place, 1, outer, blocks, (grad,))
+    partner = lax.ppermute(grad[1], "c", [(0, 1), (1, 0)])
+    grad = (grad[0].astype(F32) + partner.astype(F32)).astype(BF16).reshape(HALF, 3 * HID)
+    grad = lax.psum_scatter(grad, "y", scatter_dimension=0, tiled=True)
     grad = lax.ppermute(grad, ("c", "z"), SWAP)
     grad_gu = grad[:, : 2 * HID][None]
     grad_d = grad[:, 2 * HID :].T[None]
 
-    part = lax.all_to_all(back(place, inner, outer, weights), "x", 0, 0, tiled=True)
     summed = jnp.sum(part.astype(F32), axis=0).astype(BF16)
     home = lax.all_to_all(summed.reshape(Z, CAP, HALF), "z", 0, 0, tiled=True)
     return home_rows(routes, latent, gain, home), grad_gu, grad_d

time: 195 us -> 210 us (1.077)
  the two profiles are of different devices: /device:TPU:1 before, /device:TPU:24 now
where the time goes in v3:
time: 210 us; the launch traced here: 208 us
  blocking collectives  71.7 us (34%)
  Pallas kernels  47.7 us (23%)
  starting transfers between devices  32.8 us (16%)
  waiting for transfers between devices  31.9 us (15%)
  between operations  14.2 us (7%)
  local copies, waits for them, and re-layouts  7.7 us (4%)
  other arithmetic  2.36 us (1%)
    all_to_all x1, blocking collectives, work(): got = lax.all_to_all(send, 'z', 0, 0, tiled=True)  51.7 us
    pallas_call x4, Pallas kernels, mix(): pl.pallas_call(functools.partial(mix_kernel, len(blocks)), grid_spec=pltp...  21.2 us
    all_to_all x1, blocking collectives, work(): part = lax.all_to_all(part, 'x', 0, 0, tiled=True)  20 us
    all_to_all x1, waiting for transfers between devices, work(): home = lax.all_to_all(summed.reshape(Z, CAP, HALF), 'z', 0, 0, tiled=True)  15.7 us
    pallas_call x2, Pallas kernels, grads(): pl.pallas_call(grads_kernel, grid_spec=pltpu.PrefetchScalarGridSpec(num_s...  11.1 us
    all_to_all x1, starting transfers between devices, work(): home = lax.all_to_all(summed.reshape(Z, CAP, HALF), 'z', 0, 0, tiled=True)  8.8 us
    ppermute x1, waiting for transfers between devices, work(): right = lax.ppermute(own, 'x', MINUS)  7.15 us
    ppermute x1, waiting for transfers between devices, work(): inner = gates(mine, lax.ppermute(other, 'z', FLIP))  5.41 us
  transfers between devices with their start and end apart: 12, of which 5 were waited for; matrix products, arithmetic and copies ran while one was open for 1% of the time, Pallas kernels for 14%

profile of v3, /device:TPU:24, one launch (start us, length us, event | category | flops | bytes accessed | tf_op | source)
XLA Modules:
  0.0 208.4 jit_solution(8741241105061043236)
XLA Ops:
  7.2 0.0 all-gather.2.cloned.1.call-start
  7.2 3.2 %send_rows.1 = (bf16[16,8,2048]{2,1,0:T(8,128)(2,1)}, bf16[512,384]{1,0:T(8,128)(2,1)}) custom-call(s32[2,128]{1,0:T(2,128)} %bitcast.35, f32[2,128]{1,0:T(2,128)} %bitcast.37, bf16[128,4096]{1,0:T(8,128)(2,1)} %latent.3, bf16[128,4096]{1,0:T(8,128)(2,1)} %dout.1, f32[1,4096]{1,0:T(1,128)} %bitcast.33, bf16[1,512,256]{2,1,0:T(8,128)(2,1)} %gate_up.1, ...), custom_call_target="tpu_custom_call" | custom-call | tf_op jit(solution)/shard_map/send_rows/pallas_call | solution.py:83
  10.4 1.6 collective-permute-start.4
  12.1 0.7 copy-done.8
  12.8 1.8 hold.1
  14.6 0.0 all-gather.2.cloned.1.call-update
  14.6 0.0 reduce-scatter.2.cloned.1.call-start
  14.7 51.7 %all_to_all.15 = bf16[16,8,2048]{2,1,0:T(8,128)(2,1)S(1)} all-to-all(bf16[16,8,2048]{2,1,0:T(8,128)(2,1)} %get-tuple-element.13), channel_id=1, replica_groups=mesh['y'=4,'c'=2,'z'=16,'x'=4] {'z'}, dimensions={0} | all-to-all | bytes 1048576 | tf_op jit(solution)/shard_map/all_to_all | solution.py:318
  66.4 4.7 %collective-permute-start.2 = (bf16[128,2048]{1,0:T(8,128)(2,1)S(1)}, bf16[128,2048]{1,0:T(8,128)(2,1)S(1)}, u32[]{:S(2)}, u32[]{:S(2)}) collective-permute-start(bf16[128,2048]{1,0:T(8,128)(2,1)S(1)} %bitcast.27), channel_id=1, source_target_pairs={{0,3},{1,0},{2,1},{3,2},{4,7},{5,4},{6,5},{7,6},{8,11},{9,8},{10,9... | collective-permute-start | bytes 1572872 | tf_op jit(solution)/shard_map/ppermute | solution.py:325
  71.0 1.9 collective-permute-start
  73.0 7.2 %collective-permute-done.2.refs_0_.right = bf16[128,2048]{1,0:T(8,128)(2,1)S(1)} collective-permute-done((bf16[128,2048]{1,0:T(8,128)(2,1)S(1)}, bf16[128,2048]{1,0:T(8,128)(2,1)S(1)}, u32[]{:S(2)}, u32[]{:S(2)}) %collective-permute-start.2) | collective-permute-done | bytes 524320 | tf_op jit(solution)/shard_map/ppermute | solution.py:325
  80.2 5.2 %collective-permute-start.3 = (bf16[64,2048]{1,0:T(8,128)(2,1)S(1)}, bf16[64,2048]{1,0:T(8,128)(2,1)S(1)}, u32[]{:S(2)}, u32[]{:S(2)}) collective-permute-start(bf16[64,2048]{1,0:T(8,128)(2,1)S(1)} %slice.25), channel_id=1, source_target_pairs={{0,3},{1,0},{2,1},{3,2},{4,7},{5,4},{6,5},{7,6},{8,11},{9,8},{10,9... | collective-permute-start | bytes 786440 | tf_op jit(solution)/shard_map/ppermute | solution.py:327
  85.4 0.2 collective-permute-done.refs_0_.left
  85.6 1.9 collective-permute-start.1
  87.6 0.6 pad_add_fusion.place
  88.2 5.3 %shard_map.94 = (f32[256,384]{1,0:T(8,128)}, bf16[256,384]{1,0:T(8,128)(2,1)}) custom-call(s32[3]{0:T(128)} %pad_add_fusion.place, bf16[128,2048]{1,0:T(8,128)(2,1)} %bitcast.29, bf16[2,2048,384]{2,1,0:T(8,128)(2,1)} %bitcast.22), custom_call_target="tpu_custom_call" | custom-call | tf_op jit(solution)/shard_map/pallas_call | solution.py:191
  93.5 5.3 %shard_map.95 = (f32[256,384]{1,0:T(8,128)}, bf16[256,384]{1,0:T(8,128)(2,1)}) custom-call(s32[3]{0:T(128)} %pad_add_fusion.place, bf16[128,2048]{1,0:T(8,128)(2,1)} %copy-done.3, bf16[2,2048,384]{2,1,0:T(8,128)(2,1)} %bitcast.23, f32[256,384]{1,0:T(8,128)} %get-tuple-element.15.refs_2_, ...), custom_call_target="tpu_custom_call", output_to_operand_aliasing={{0}: (3, {}), {1}: (4, {})} | custom-call | tf_op jit(solution)/shard_map/pallas_call | solution.py:191
  98.8 5.3 %shard_map.96 = (f32[256,384]{1,0:T(8,128)}, bf16[256,384]{1,0:T(8,128)(2,1)}) custom-call(s32[3]{0:T(128)} %pad_add_fusion.place, bf16[128,2048]{1,0:T(8,128)(2,1)} %copy-done.2, bf16[2,2048,384]{2,1,0:T(8,128)(2,1)} %bitcast.24, f32[256,384]{1,0:T(8,128)} %get-tuple-element.17.refs_2_, ...), custom_call_target="tpu_custom_call", output_to_operand_aliasing={{0}: (3, {}), {1}: (4, {})} | custom-call | tf_op jit(solution)/shard_map/pallas_call | solution.py:191
  104.1 0.0 collective-permute-done.3.refs_1_.far_b
  104.1 0.0 copy-start.5
  104.1 0.7 copy-done.4
  104.8 0.1 copy-done.5
  104.9 5.3 %shard_map.97 = (f32[256,384]{1,0:T(8,128)}, bf16[256,384]{1,0:T(8,128)(2,1)}) custom-call(s32[3]{0:T(128)} %pad_add_fusion.place, bf16[64,2048]{1,0:T(8,128)(2,1)} %copy-done.5, bf16[64,2048]{1,0:T(8,128)(2,1)} %copy-done.4, bf16[2,2048,384]{2,1,0:T(8,128)(2,1)} %bitcast.25, ...), custom_call_target="tpu_custom_call", output_to_operand_aliasing={{0}: (4, {}), {1}: (5, {})} | custom-call | tf_op jit(solution)/shard_map/pallas_call | solution.py:191
  110.2 2.6 %collective-permute-start.5 = (bf16[256,384]{1,0:T(8,128)(2,1)}, bf16[256,384]{1,0:T(8,128)(2,1)S(1)}, u32[]{:S(2)}, u32[]{:S(2)}) collective-permute-start(bf16[256,384]{1,0:T(8,128)(2,1)} %get-tuple-element.22), channel_id=1, source_target_pairs={{0,4},{4,0},{8,12},{12,8},{16,20},{20,16},{24,28},{28,24},{32,36},... | collective-permute-start | bytes 589832 | tf_op jit(solution)/shard_map/ppermute | solution.py:334
  112.8 5.4 %collective-permute-done.5.got = bf16[256,384]{1,0:T(8,128)(2,1)S(1)} collective-permute-done((bf16[256,384]{1,0:T(8,128)(2,1)}, bf16[256,384]{1,0:T(8,128)(2,1)S(1)}, u32[]{:S(2)}, u32[]{:S(2)}) %collective-permute-start.5) | collective-permute-done | bytes 196640 | tf_op jit(solution)/shard_map/ppermute | solution.py:334
  118.2 0.7 copy-done.9
  118.9 1.8 gates.1.mine.value
  120.8 2.3 %collective-permute-start.6 = (bf16[256,384]{1,0:T(8,128)(2,1)}, bf16[256,384]{1,0:T(8,128)(2,1)S(1)}, u32[]{:S(2)}, u32[]{:S(2)}) collective-permute-start(bf16[256,384]{1,0:T(8,128)(2,1)} %gates.1.mine.value), channel_id=1, source_target_pairs={{0,4},{4,0},{8,12},{12,8},{16,20},{20,16},{24,28},{28,24},{32,36},... | collective-permute-start | bytes 589832 | tf_op jit(solution)/shard_map/ppermute | solution.py:335
  123.1 5.5 %shard_map.98.refs_0_ = bf16[2,4,512,384]{3,2,1,0:T(8,128)(2,1)} custom-call(s32[3]{0:T(128)} %pad_add_fusion.place, bf16[256,384]{1,0:T(8,128)(2,1)} %gates.1.mine.value, bf16[128,2048]{1,0:T(8,128)(2,1)} %bitcast.30, bf16[128,2048]{1,0:T(8,128)(2,1)} %copy-done.3, bf16[128,2048]{1,0:T(8,128)(2,1)} %copy-done.2, bf16[64,2048]{1,0:T(8,128)(2,1)} %copy-done.5, ...), custom_call_target="tpu_custom_call" | custom-call | tf_op jit(solution)/shard_map/pallas_call | solution.py:295
  128.7 0.7 copy-done.7
  129.4 5.5 %shard_map.99 = bf16[2,4,512,384]{3,2,1,0:T(8,128)(2,1)} custom-call(s32[3]{0:T(128)} %pad_add_fusion.place, bf16[256,384]{1,0:T(8,128)(2,1)} %copy-done.7, bf16[128,2048]{1,0:T(8,128)(2,1)} %bitcast.31, bf16[128,2048]{1,0:T(8,128)(2,1)} %copy-done.3, bf16[128,2048]{1,0:T(8,128)(2,1)} %copy-done.2, ...), custom_call_target="tpu_custom_call", output_to_operand_aliasing={{}: (7, {})} | custom-call | tf_op jit(solution)/shard_map/pallas_call | solution.py:295
  134.9 1.7 slice_bitcast_fusion
  136.6 1.9 collective-permute-start.7
  138.6 3.4 %collective-permute-done.7 = bf16[4,512,384]{2,1,0:T(8,128)(2,1)S(1)} collective-permute-done((bf16[4,512,384]{2,1,0:T(8,128)(2,1)S(1)}, bf16[4,512,384]{2,1,0:T(8,128)(2,1)S(1)}, u32[]{:S(2)}, u32[]{:S(2)}) %collective-permute-start.7) | collective-permute-done | bytes 1572896 | tf_op jit(solution)/shard_map/ppermute | solution.py:341
  141.9 1.6 fusion
  143.5 0.0 reduce-scatter.2.cloned.1.call-update
  143.5 5.2 %back.1 = bf16[4,64,2048]{2,1,0:T(8,128)(2,1)} custom-call(s32[3]{0:T(128)} %pad_add_fusion.place, bf16[256,384]{1,0:T(8,128)(2,1)} %gates.1.mine.value, bf16[256,384]{1,0:T(8,128)(2,1)} %copy-done.7, bf16[2,2048,384]{2,1,0:T(8,128)(2,1)} %bitcast.26), custom_call_target="tpu_custom_call" | custom-call | tf_op jit(solution)/shard_map/back/pallas_call | solution.py:249
  148.7 20.0 %all_to_all.16 = bf16[4,64,2048]{2,1,0:T(8,128)(2,1)S(1)} all-to-all(bf16[4,64,2048]{2,1,0:T(8,128)(2,1)} %back.1), channel_id=1, replica_groups=mesh['y'=4,'c'=2,'z'=16,'x'=4] {'x'}, dimensions={0} | all-to-all | bytes 2097152 | tf_op jit(solution)/shard_map/all_to_all | solution.py:339
  168.8 0.2 reduce_sum.12
  169.0 0.8 reshape.22
  169.8 8.8 %all-to-all-start.2 = ((bf16[16,4,2048]{2,1,0:T(4,128)(2,1)}), bf16[16,4,2048]{2,1,0:T(4,128)(2,1)S(1)}, u32[]{:S(2)}, u32[]{:S(2)}) async-start(bf16[16,4,2048]{2,1,0:T(4,128)(2,1)} %reshape.22), calls=%async_computation.2 | async-start | bytes 524288 | tf_op jit(solution)/shard_map/all_to_all | solution.py:349
  178.6 0.0 reduce-scatter.2.cloned.1.call-done
  178.6 1.7 collective-permute-start.8
  180.3 15.7 %all-to-all-done.2.home = bf16[16,4,2048]{2,1,0:T(4,128)(2,1)S(1)} async-done(((bf16[16,4,2048]{2,1,0:T(4,128)(2,1)}), bf16[16,4,2048]{2,1,0:T(4,128)(2,1)S(1)}, u32[]{:S(2)}, u32[]{:S(2)}) %all-to-all-start.2) | async-done | bytes 262176 | tf_op jit(solution)/shard_map/all_to_all | solution.py:349
  196.0 0.7 copy-done.6
  196.7 3.3 %home_rows.1 = bf16[128,4096]{1,0:T(8,128)(2,1)} custom-call(s32[2,128]{1,0:T(2,128)} %bitcast.36, bf16[128,4096]{1,0:T(8,128)(2,1)} %latent.3, f32[1,4096]{1,0:T(1,128)} %bitcast.34, bf16[16,4,2048]{2,1,0:T(4,128)(2,1)} %copy-done.6), custom_call_target="tpu_custom_call" | custom-call | tf_op jit(solution)/shard_map/home_rows/pallas_call | solution.py:119
  200.1 0.8 copy.18
  200.8 0.7 slice_bitcast_fusion.2
  (21 shorter events, 0.1 us)
Async XLA Ops:
  7.2 81.0 %all-gather.2.cloned.1.call-start = ((), (), s32[]{:S(2)}) async-start(), calls=%async_computation.4 | async-start | bytes 3538944 | tf_op jit(solution)/shard_map/all_gather | solution.py:319
  10.4 1.6 collective-permute-start.4
  12.1 0.7 copy-start.8
  14.6 164.0 %reduce-scatter.2.cloned.1.call-start = ((), (), s32[]{:S(2)}) async-start(), calls=%async_computation.5 | async-start | bytes 1966080 | tf_op jit(solution)/shard_map/reduce_scatter | solution.py:343
  66.4 21.8 %copy-start.1 = (bf16[16,8,2048]{2,1,0:T(8,128)(2,1)}, bf16[16,8,2048]{2,1,0:T(8,128)(2,1)S(1)}, u32[]{:S(2)}) copy-start(bf16[16,8,2048]{2,1,0:T(8,128)(2,1)S(1)} %all_to_all.15) | copy-start | bytes 1572868
  66.4 13.7 %collective-permute-start.2 = (bf16[128,2048]{1,0:T(8,128)(2,1)S(1)}, bf16[128,2048]{1,0:T(8,128)(2,1)S(1)}, u32[]{:S(2)}, u32[]{:S(2)}) collective-permute-start(bf16[128,2048]{1,0:T(8,128)(2,1)S(1)} %bitcast.27), channel_id=1, source_target_pairs={{0,3},{1,0},{2,1},{3,2},{4,7},{5,4},{6,5},{7,6},{8,11},{9,8},{10,9... | collective-permute-start | bytes 1572872 | tf_op jit(solution)/shard_map/ppermute | solution.py:325
  71.0 14.6 %collective-permute-start = (bf16[128,2048]{1,0:T(8,128)(2,1)S(1)}, bf16[128,2048]{1,0:T(8,128)(2,1)S(1)}, u32[]{:S(2)}, u32[]{:S(2)}) collective-permute-start(bf16[128,2048]{1,0:T(8,128)(2,1)S(1)} %bitcast.28), channel_id=1, source_target_pairs={{0,1},{1,2},{2,3},{3,0},{4,5},{5,6},{6,7},{7,4},{8,9},{9,10},{10,1... | collective-permute-start | bytes 1572872 | tf_op jit(solution)/shard_map/ppermute | solution.py:324
  80.1 18.7 %copy-start.2 = (bf16[128,2048]{1,0:T(8,128)(2,1)}, bf16[128,2048]{1,0:T(8,128)(2,1)S(1)}, u32[]{:S(2)}) copy-start(bf16[128,2048]{1,0:T(8,128)(2,1)S(1)} %collective-permute-done.2.refs_0_.right) | copy-start | bytes 1572868
  80.2 24.0 %collective-permute-start.3 = (bf16[64,2048]{1,0:T(8,128)(2,1)S(1)}, bf16[64,2048]{1,0:T(8,128)(2,1)S(1)}, u32[]{:S(2)}, u32[]{:S(2)}) collective-permute-start(bf16[64,2048]{1,0:T(8,128)(2,1)S(1)} %slice.25), channel_id=1, source_target_pairs={{0,3},{1,0},{2,1},{3,2},{4,7},{5,4},{6,5},{7,6},{8,11},{9,8},{10,9... | collective-permute-start | bytes 786440 | tf_op jit(solution)/shard_map/ppermute | solution.py:327
  85.6 7.9 %copy-start.3 = (bf16[128,2048]{1,0:T(8,128)(2,1)}, bf16[128,2048]{1,0:T(8,128)(2,1)S(1)}, u32[]{:S(2)}) copy-start(bf16[128,2048]{1,0:T(8,128)(2,1)S(1)} %collective-permute-done.refs_0_.left) | copy-start | bytes 1572868
  85.6 18.5 %collective-permute-start.1 = (bf16[64,2048]{1,0:T(8,128)(2,1)S(1)}, bf16[64,2048]{1,0:T(8,128)(2,1)S(1)}, u32[]{:S(2)}, u32[]{:S(2)}) collective-permute-start(bf16[64,2048]{1,0:T(8,128)(2,1)S(1)} %slice.24), channel_id=1, source_target_pairs={{0,1},{1,2},{2,3},{3,0},{4,5},{5,6},{6,7},{7,4},{8,9},{9,10},{10,1... | collective-permute-start | bytes 786440 | tf_op jit(solution)/shard_map/ppermute | solution.py:326
  104.1 0.7 copy-start.4
  104.1 0.8 copy-start.5
  110.2 8.0 %collective-permute-start.5 = (bf16[256,384]{1,0:T(8,128)(2,1)}, bf16[256,384]{1,0:T(8,128)(2,1)S(1)}, u32[]{:S(2)}, u32[]{:S(2)}) collective-permute-start(bf16[256,384]{1,0:T(8,128)(2,1)} %get-tuple-element.22), channel_id=1, source_target_pairs={{0,4},{4,0},{8,12},{12,8},{16,20},{20,16},{24,28},{28,24},{32,36},... | collective-permute-start | bytes 589832 | tf_op jit(solution)/shard_map/ppermute | solution.py:334
  118.2 0.7 copy-start.9
  120.8 7.9 %collective-permute-start.6 = (bf16[256,384]{1,0:T(8,128)(2,1)}, bf16[256,384]{1,0:T(8,128)(2,1)S(1)}, u32[]{:S(2)}, u32[]{:S(2)}) collective-permute-start(bf16[256,384]{1,0:T(8,128)(2,1)} %gates.1.mine.value), channel_id=1, source_target_pairs={{0,4},{4,0},{8,12},{12,8},{16,20},{20,16},{24,28},{28,24},{32,36},... | collective-permute-start | bytes 589832 | tf_op jit(solution)/shard_map/ppermute | solution.py:335
  128.7 0.7 copy-start.7
  134.9 7.0 %copy-start = (bf16[2,4,512,384]{3,2,1,0:T(8,128)(2,1)S(1)}, bf16[2,4,512,384]{3,2,1,0:T(8,128)(2,1)}, u32[]{:S(2)}) copy-start(bf16[2,4,512,384]{3,2,1,0:T(8,128)(2,1)} %shard_map.99) | copy-start | bytes 9437188
  136.6 5.3 %collective-permute-start.7 = (bf16[4,512,384]{2,1,0:T(8,128)(2,1)S(1)}, bf16[4,512,384]{2,1,0:T(8,128)(2,1)S(1)}, u32[]{:S(2)}, u32[]{:S(2)}) collective-permute-start(bf16[4,512,384]{2,1,0:T(8,128)(2,1)S(1)} %slice_bitcast_fusion), channel_id=1, source_target_pairs={{0,64},{64,0},{1,65},{65,1},{2,66},{66,2},{3,67},{67,3},{4,68},{68... | collective-permute-start | bytes 4718600 | tf_op jit(solution)/shard_map/ppermute | solution.py:341
  169.8 26.2 %all-to-all-start.2 = ((bf16[16,4,2048]{2,1,0:T(4,128)(2,1)}), bf16[16,4,2048]{2,1,0:T(4,128)(2,1)S(1)}, u32[]{:S(2)}, u32[]{:S(2)}) async-start(bf16[16,4,2048]{2,1,0:T(4,128)(2,1)} %reshape.22), calls=%async_computation.2 | async-start | bytes 524288 | tf_op jit(solution)/shard_map/all_to_all | solution.py:349
  178.6 21.4 %collective-permute-start.8 = (bf16[512,384]{1,0:T(8,128)(2,1)}, bf16[512,384]{1,0:T(8,128)(2,1)S(1)}, u32[]{:S(2)}, u32[]{:S(2)}) collective-permute-start(bf16[512,384]{1,0:T(8,128)(2,1)} %reduce-scatter.2.cloned.1.call-done), channel_id=1, source_target_pairs={{0,0},{4,64},{8,8},{12,72},{16,16},{20,80},{24,24},{28,88},{32,32}... | collective-permute-start | bytes 1179656 | tf_op jit(solution)/shard_map/ppermute | solution.py:344
  196.0 0.7 copy-start.6
Sparse Core Ops, SparseCore 0:
  14.8 45.7 all-gather.1
  143.6 30.5 reduce-scatter.1

commit v4 on v3

--- a/solution.py
+++ b/solution.py
@@ -26,6 +26,7 @@
 FLIP = [(i, i ^ 1) for i in range(Z)]
 PLUS = [(i, (i + 1) % X) for i in range(X)]
 MINUS = [(i, (i - 1) % X) for i in range(X)]
+TURN = [(0, 1), (1, 0)]
 ORDER = (0, 3, 1, 2)
 
 
@@ -88,12 +89,18 @@
     )(*args)
 
 
-def hold_kernel(piece, out):
-    out[...] = piece[...]
-
-
-def hold(piece):
-    return pl.pallas_call(hold_kernel, out_shape=shape(piece.shape, BF16), name="hold")(piece)
+def join_kernel(own, left, right, far_a, far_b, out):
+    out[pl.ds(0, CUT), :] = own[...]
+    out[pl.ds(CUT, CUT), :] = left[...]
+    out[pl.ds(2 * CUT, CUT), :] = right[...]
+    out[pl.ds(3 * CUT, CUT // 2), :] = far_a[...]
+    out[pl.ds(3 * CUT + CUT // 2, CUT // 2), :] = far_b[...]
+
+
+def join(*blocks):
+    return pl.pallas_call(
+        join_kernel, out_shape=shape((HALF, 3 * HID), BF16), name="join"
+    )(*blocks)
 
 
 def home_kernel(routes, latent, gain, home, out, grad):
@@ -131,14 +138,14 @@
 
 
 def mix_kernel(count, place, *refs):
-    blocks, weights = refs[:count], refs[count]
+    blocks, weights = refs[:count], refs[count : count + 2]
     mine, other, total = refs[-3:]
     step = pl.program_id(0)
     rows = blocks[0][...]
     if count > 1:
         rows = jnp.concatenate([block[...] for block in blocks], axis=0)
     for g in range(2):
-        part = jnp.dot(rows, weights[g], preferred_element_type=F32)
+        part = jnp.dot(rows, weights[g][...], preferred_element_type=F32)
 
         @pl.when(step == 0)
         def _():
@@ -159,23 +166,23 @@
 
     @pl.when(step == pl.num_programs(0) - 1)
     def _():
-        pre, dh = packed(total[place[0]])
+        pre, dh = packed(total[place[2]])
         mine[:, : 2 * HID] = pre
         mine[:, 2 * HID :] = dh
-        pre, dh = packed(total[1 - place[0]])
+        pre, dh = packed(total[1 - place[2]])
         other[:, : 2 * HID] = pre.astype(BF16)
         other[:, 2 * HID :] = dh.astype(BF16)
 
 
 def row_specs():
     return [
-        pl.BlockSpec((n, CUT), lambda i, *_: (0, i))
+        pl.BlockSpec((n, CUT), lambda i, place: (0, place[3 + i]))
         for n in (ROWS // 4, ROWS // 4, ROWS // 4, ROWS // 8, ROWS // 8)
     ]
 
 
-def weight_spec():
-    return pl.BlockSpec((2, CUT, 3 * HID), lambda i, *_: (0, i, 0))
+def weight_specs():
+    return [pl.BlockSpec((CUT, 3 * HID), lambda i, *_: (i, 0))] * 2
 
 
 def whole(dims):
@@ -187,15 +194,18 @@
     part = pl.BlockSpec((rows // 2, 3 * HID), lambda i, *_: (at, 0))
     dims = (ROWS // 2, 3 * HID)
     hold = [pl.BlockSpec(memory_space=pl.ANY)] * len(so_far)
-    first = 2 + len(blocks)
+    first = 3 + len(blocks)
     return pl.pallas_call(
         functools.partial(mix_kernel, len(blocks)),
         grid_spec=pltpu.PrefetchScalarGridSpec(
             num_scalar_prefetch=1,
             grid=(HALF // CUT,),
             in_specs=[
-                *[pl.BlockSpec((b.shape[0], CUT), lambda i, *_: (0, i)) for b in blocks],
-                weight_spec(),
+                *[
+                    pl.BlockSpec((b.shape[0], CUT), lambda i, place: (0, place[3 + i]))
+                    for b in blocks
+                ],
+                *weight_specs(),
                 *hold,
             ],
             out_specs=[part, part],
@@ -203,7 +213,7 @@
         ),
         out_shape=[shape(dims, F32), shape(dims, BF16)],
         input_output_aliases={first + k: k for k in range(len(so_far))},
-    )(place, *blocks, weights, *so_far)
+    )(place, *blocks, *weights, *so_far)
 
 
 def gates_kernel(mine, got, out):
@@ -224,16 +234,18 @@
     )(mine, got)
 
 
-def back_kernel(place, mine, other, weights, out, inner):
+def back_kernel(place, mine, other, weights_a, weights_b, out, inner):
+    weights = weights_a, weights_b
+
     @pl.when(pl.program_id(0) == 0)
     def _():
-        inner[place[0]] = mine[...]
-        inner[1 - place[0]] = other[...]
+        inner[place[2]] = mine[...]
+        inner[1 - place[2]] = other[...]
 
     total = sum(
         lax.dot_general(
             inner[g, :, : 2 * HID],
-            weights[g, :, : 2 * HID],
+            weights[g][:, : 2 * HID],
             (((1,), (1,)), ((), ())),
             preferred_element_type=F32,
         )
@@ -251,13 +263,13 @@
         grid_spec=pltpu.PrefetchScalarGridSpec(
             num_scalar_prefetch=1,
             grid=(HALF // CUT,),
-            in_specs=[whole(dims), whole(dims), weight_spec()],
-            out_specs=pl.BlockSpec((X, ROWS // 8, CUT), lambda i, *_: (0, 0, i)),
+            in_specs=[whole(dims), whole(dims), *weight_specs()],
+            out_specs=pl.BlockSpec((X, ROWS // 8, CUT), lambda i, place: (0, 0, place[3 + i])),
             scratch_shapes=[pltpu.VMEM((2, *dims), BF16)],
         ),
         out_shape=shape((X, ROWS // 8, HALF), BF16),
         name="back",
-    )(place, mine, other, weights)
+    )(place, mine, other, *weights)
 
 
 def grads_kernel(place, value, own, left, right, far_a, far_b, *refs):
@@ -306,31 +318,47 @@
     )(place, value, *blocks, *so_far)
 
 
+def gathered(own, axis):
+    half = own.shape[0] // 2
+    left = lax.ppermute(own, axis, PLUS)
+    right = lax.ppermute(own, axis, MINUS)
+    far_a = lax.ppermute(left[:half], axis, PLUS)
+    far_b = lax.ppermute(right[half:], axis, MINUS)
+    return own, left, right, far_a, far_b
+
+
+def scattered(parts):
+    own, left, right, far = parts
+    half = own.shape[0] // 2
+    far = far.astype(BF16)
+    got_a = lax.ppermute(far[:half], "y", MINUS).astype(F32)
+    got_b = lax.ppermute(far[half:], "y", PLUS).astype(F32)
+    left = jnp.concatenate([left[:half] + got_a, left[half:]], axis=0).astype(BF16)
+    right = jnp.concatenate([right[:half], right[half:] + got_b], axis=0).astype(BF16)
+    left = lax.ppermute(left, "y", MINUS)
+    right = lax.ppermute(right, "y", PLUS)
+    return (own + left.astype(F32) + right.astype(F32)).astype(BF16)
+
+
 def work(latent, dout, routes, gate_w, norm_gain, w_gate_up, w_down):
     zp = lax.axis_index("z") % 2
     core = lax.axis_index("c")
-    place = jnp.stack([zp, lax.axis_index("x"), (zp + core) % 2]).astype(jnp.int32)
+    y = lax.axis_index("y")
+    place = jnp.stack(
+        [zp, lax.axis_index("x"), (zp + core) % 2, *[(y + off) % Y for off in ORDER]]
+    ).astype(jnp.int32)
     gain = norm_gain[None, :]
     routes = routes.T
 
     send, piece = send_rows(routes, gate_w.T, latent, dout, gain, w_gate_up, w_down)
     piece = lax.ppermute(piece, ("c", "z"), SWAP)
     got = lax.all_to_all(send, "z", 0, 0, tiled=True)
-    weights = lax.all_gather(hold(piece), ("c", "y"), axis=0, tiled=True)
-    weights = weights.reshape(2, HALF, 3 * HID)
-
-    own = got.reshape(ROWS // 4, HALF)
-    half = own.shape[0] // 2
-    left = lax.ppermute(own, "x", PLUS)
-    right = lax.ppermute(own, "x", MINUS)
-    far_a = lax.ppermute(left[:half], "x", PLUS)
-    far_b = lax.ppermute(right[half:], "x", MINUS)
-    blocks = own, left, right, far_a, far_b
-
-    parts = ()
-    for at, some in enumerate(((own,), (left,), (right,), (far_a, far_b))):
-        parts = mix(place, at, some, weights, parts)
-    mine, other = parts
+    mine = join(*gathered(piece, "y"))
+    weights = mine, lax.ppermute(mine, "c", TURN)
+
+    blocks = gathered(got.reshape(ROWS // 4, HALF), "x")
+    parts = mix(place, 0, blocks[:3], weights, ())
+    mine, other = mix(place, 3, blocks[3:], weights, parts)
     inner = gates(mine, lax.ppermute(other, "z", FLIP))
     outer = lax.ppermute(inner, "z", FLIP)
 
@@ -338,9 +366,8 @@
     part = back(place, inner, outer, weights)
     part = lax.all_to_all(part, "x", 0, 0, tiled=True)
     grad = grads(place, 1, outer, blocks, (grad,))
-    partner = lax.ppermute(grad[1], "c", [(0, 1), (1, 0)])
-    grad = (grad[0].astype(F32) + partner.astype(F32)).astype(BF16).reshape(HALF, 3 * HID)
-    grad = lax.psum_scatter(grad, "y", scatter_dimension=0, tiled=True)
+    partner = lax.ppermute(grad[1], "c", TURN)
+    grad = scattered([grad[0, k].astype(F32) + partner[k].astype(F32) for k in range(Y)])
     grad = lax.ppermute(grad, ("c", "z"), SWAP)
     grad_gu = grad[:, : 2 * HID][None]
     grad_d = grad[:, 2 * HID :].T[None]

time: 210 us -> 220 us (1.048); the launches traced: 208 us -> 216 us
  starting transfers between devices: 32.8 us -> 115 us
  blocking collectives: 71.7 us -> 0 us
  between operations: 14.2 us -> 1.04 us
  Pallas kernels: 47.7 us -> 39.4 us
  waiting for transfers between devices: 31.9 us -> 39.9 us
  other arithmetic: 2.36 us -> 7.93 us
  local copies, waits for them, and re-layouts: 7.7 us -> 13.1 us
    all_to_all x2 -> x0, blocking collectives: 71.7 us -> none  [the longest x1 51.7 us: work(): got = lax.all_to_all(send, 'z', 0, 0, tiled=True)]
    ppermute x5 -> x14, starting transfers between devices: 15.7 us -> 71.7 us  [the longest x1 27.1 us: work(): weights = (mine, lax.ppermute(mine, 'c', TURN))]
    all_to_all x0 -> x2, starting transfers between devices: none -> 19.4 us  [the longest x1 15.2 us: work(): got = lax.all_to_all(send, 'z', 0, 0, tiled=True)]
    ppermute x5 -> x14, waiting for transfers between devices: 10.7 us -> 20.6 us  [the longest x2 13.2 us: gathered(): right = lax.ppermute(own, axis, MINUS)]
    pallas_call x4 -> x2, Pallas kernels: 21.2 us -> 12 us  [mix(): pl.pallas_call(functools.partial(mix_kernel, len(blocks)), grid_spec=pltp...]
    slice x2 -> x7, local copies, waits for them, and re-layouts: 0.04 us -> 3.73 us  [the longest x1 1.09 us: scattered(): left[half:]]
    all_to_all x1, starting transfers between devices: 8.8 us -> 12.2 us  [work(): home = lax.all_to_all(summed.reshape(Z, CAP, HALF), 'z', 0, 0, tiled=True)]
    unnamed x21 -> x33, local copies, waits for them, and re-layouts: 4.42 us -> 5.48 us
  transfers between devices with their start and end apart: 12 -> 21, of which waited for: 5 -> 9; matrix products, arithmetic and copies ran while one was open for 1% -> 5% of each run, Pallas kernels for 14% -> 11%
where the time goes in v4:
time: 220 us; the launch traced here: 216 us
  starting transfers between devices  115 us (52%)
  waiting for transfers between devices  39.9 us (18%)
  Pallas kernels  39.4 us (18%)
  local copies, waits for them, and re-layouts  13.1 us (6%)
  other arithmetic  7.93 us (4%)
    ppermute x1, starting transfers between devices, work(): weights = (mine, lax.ppermute(mine, 'c', TURN))  27.1 us
    all_to_all x1, starting transfers between devices, work(): got = lax.all_to_all(send, 'z', 0, 0, tiled=True)  15.2 us
    all_to_all x1, waiting for transfers between devices, work(): home = lax.all_to_all(summed.reshape(Z, CAP, HALF), 'z', 0, 0, tiled=True)  13.9 us
    ppermute x2, waiting for transfers between devices, gathered(): right = lax.ppermute(own, axis, MINUS)  13.2 us
    all_to_all x1, starting transfers between devices, work(): home = lax.all_to_all(summed.reshape(Z, CAP, HALF), 'z', 0, 0, tiled=True)  12.2 us
    pallas_call x2, Pallas kernels, mix(): pl.pallas_call(functools.partial(mix_kernel, len(blocks)), grid_spec=pltp...  12 us
    pallas_call x2, Pallas kernels, grads(): pl.pallas_call(grads_kernel, grid_spec=pltpu.PrefetchScalarGridSpec(num_s...  11.2 us
    ppermute x2, starting transfers between devices, gathered(): far_b = lax.ppermute(right[half:], axis, MINUS)  7.51 us
  transfers between devices with their start and end apart: 21, of which 9 were waited for; matrix products, arithmetic and copies ran while one was open for 5% of the time, Pallas kernels for 11%

profile of v4, /device:TPU:24, one launch (start us, length us, event | category | flops | bytes accessed | tf_op | source)
XLA Modules:
  0.0 216.0 jit_solution(4094562083468714196)
XLA Ops:
  0.6 3.2 %send_rows.1 = (bf16[16,8,2048]{2,1,0:T(8,128)(2,1)}, bf16[512,384]{1,0:T(8,128)(2,1)}) custom-call(s32[2,128]{1,0:T(2,128)} %bitcast.66, f32[2,128]{1,0:T(2,128)} %bitcast.68, bf16[128,4096]{1,0:T(8,128)(2,1)} %latent.3, bf16[128,4096]{1,0:T(8,128)(2,1)} %dout.1, f32[1,4096]{1,0:T(1,128)} %bitcast.64, bf16[1,512,256]{2,1,0:T(8,128)(2,1)} %gate_up.1, ...), custom_call_target="tpu_custom_call" | custom-call | tf_op jit(solution)/shard_map/send_rows/pallas_call | solution.py:84
  3.9 15.2 %all-to-all-start = ((bf16[16,8,2048]{2,1,0:T(8,128)(2,1)}), bf16[16,8,2048]{2,1,0:T(8,128)(2,1)S(1)}, u32[]{:S(2)}, u32[]{:S(2)}) async-start(bf16[16,8,2048]{2,1,0:T(8,128)(2,1)} %get-tuple-element.9), calls=%async_computation | async-start | bytes 1048576 | tf_op jit(solution)/shard_map/all_to_all | solution.py:355
  19.1 1.7 collective-permute-start.4
  20.7 2.6 %collective-permute-start.6 = (bf16[512,384]{1,0:T(8,128)(2,1)S(1)}, bf16[512,384]{1,0:T(8,128)(2,1)S(1)}, u32[]{:S(2)}, u32[]{:S(2)}) collective-permute-start(bf16[512,384]{1,0:T(8,128)(2,1)S(1)} %collective-permute-done.4.own), channel_id=1, source_target_pairs={{0,384},{128,0},{256,128},{384,256},{1,385},{129,1},{257,129},{385... | collective-permute-start | bytes 1179656 | tf_op jit(solution)/shard_map/ppermute | solution.py:324
  23.4 4.4 %collective-permute-start.5 = (bf16[512,384]{1,0:T(8,128)(2,1)S(1)}, bf16[512,384]{1,0:T(8,128)(2,1)S(1)}, u32[]{:S(2)}, u32[]{:S(2)}) collective-permute-start(bf16[512,384]{1,0:T(8,128)(2,1)S(1)} %collective-permute-done.4.own), channel_id=1, source_target_pairs={{0,128},{128,256},{256,384},{384,0},{1,129},{129,257},{257,385},{3... | collective-permute-start | bytes 1179656 | tf_op jit(solution)/shard_map/ppermute | solution.py:323
  27.8 3.8 %collective-permute-done.6.right = bf16[512,384]{1,0:T(8,128)(2,1)S(1)} collective-permute-done((bf16[512,384]{1,0:T(8,128)(2,1)S(1)}, bf16[512,384]{1,0:T(8,128)(2,1)S(1)}, u32[]{:S(2)}, u32[]{:S(2)}) %collective-permute-start.6) | collective-permute-done | bytes 393248 | tf_op jit(solution)/shard_map/ppermute | solution.py:324
  31.6 1.9 collective-permute-start.8
  33.6 5.1 %collective-permute-start.7 = (bf16[256,384]{1,0:T(8,128)(2,1)S(1)}, bf16[256,384]{1,0:T(8,128)(2,1)S(1)}, u32[]{:S(2)}, u32[]{:S(2)}) collective-permute-start(bf16[256,384]{1,0:T(8,128)(2,1)S(1)} %slice.88), channel_id=1, source_target_pairs={{0,128},{128,256},{256,384},{384,0},{1,129},{129,257},{257,385},{3... | collective-permute-start | bytes 589832 | tf_op jit(solution)/shard_map/ppermute | solution.py:325
  38.7 1.7 collective-permute-done.8.far_b
  40.4 1.5 collective-permute-done.7.far_a
  42.6 2.6 %join.1.refs_3_.refs_2_.weights_a = bf16[2048,384]{1,0:T(8,128)(2,1)} custom-call(bf16[512,384]{1,0:T(8,128)(2,1)} %copy-done.12, bf16[512,384]{1,0:T(8,128)(2,1)} %copy-done.10, bf16[512,384]{1,0:T(8,128)(2,1)} %copy-done.9, bf16[256,384]{1,0:T(8,128)(2,1)} %copy-done.14, bf16[256,384]{1,0:T(8,128)(2,1)} %copy-done.13), custom_call_target="tpu_custom_call" | custom-call | tf_op jit(solution)/shard_map/join/pallas_call | solution.py:101
  45.2 27.1 %collective-permute-start.9 = (bf16[2048,384]{1,0:T(8,128)(2,1)}, bf16[2048,384]{1,0:T(8,128)(2,1)S(1)}, u32[]{:S(2)}, u32[]{:S(2)}) collective-permute-start(bf16[2048,384]{1,0:T(8,128)(2,1)} %join.1.refs_3_.refs_2_.weights_a), channel_id=1, source_target_pairs={{0,64},{64,0},{1,65},{65,1},{2,66},{66,2},{3,67},{67,3},{4,68},{68... | collective-permute-start | bytes 4718600 | tf_op jit(solution)/shard_map/ppermute | solution.py:357
  72.3 4.7 %collective-permute-start.2 = (bf16[128,2048]{1,0:T(8,128)(2,1)S(1)}, bf16[128,2048]{1,0:T(8,128)(2,1)S(1)}, u32[]{:S(2)}, u32[]{:S(2)}) collective-permute-start(bf16[128,2048]{1,0:T(8,128)(2,1)S(1)} %bitcast.59), channel_id=1, source_target_pairs={{0,3},{1,0},{2,1},{3,2},{4,7},{5,4},{6,5},{7,6},{8,11},{9,8},{10,9... | collective-permute-start | bytes 1572872 | tf_op jit(solution)/shard_map/ppermute | solution.py:324
  77.0 1.9 collective-permute-start
  78.9 9.4 %collective-permute-done.2.refs_2_.right = bf16[128,2048]{1,0:T(8,128)(2,1)S(1)} collective-permute-done((bf16[128,2048]{1,0:T(8,128)(2,1)S(1)}, bf16[128,2048]{1,0:T(8,128)(2,1)S(1)}, u32[]{:S(2)}, u32[]{:S(2)}) %collective-permute-start.2) | collective-permute-done | bytes 524320 | tf_op jit(solution)/shard_map/ppermute | solution.py:324
  89.1 5.6 %collective-permute-start.3 = (bf16[64,2048]{1,0:T(8,128)(2,1)}, bf16[64,2048]{1,0:T(8,128)(2,1)S(1)}, u32[]{:S(2)}, u32[]{:S(2)}) collective-permute-start(bf16[64,2048]{1,0:T(8,128)(2,1)} %slice.87), channel_id=1, source_target_pairs={{0,3},{1,0},{2,1},{3,2},{4,7},{5,4},{6,5},{7,6},{8,11},{9,8},{10,9... | collective-permute-start | bytes 786440 | tf_op jit(solution)/shard_map/ppermute | solution.py:326
  95.5 1.9 collective-permute-start.1
  98.1 1.2 copy-done.1
  99.3 6.7 %shard_map.94 = (f32[256,384]{1,0:T(8,128)}, bf16[256,384]{1,0:T(8,128)(2,1)}) custom-call(s32[7]{0:T(128)} %stack.31.place, bf16[128,2048]{1,0:T(8,128)(2,1)} %bitcast.61, bf16[128,2048]{1,0:T(8,128)(2,1)} %copy-done.4, bf16[128,2048]{1,0:T(8,128)(2,1)} %copy-done.3, bf16[2048,384]{1,0:T(8,128)(2,1)} %join.1.refs_3_.refs_2_.weights_a, ...), custom_call_target="tpu_custom_call" | custom-call | tf_op jit(solution)/shard_map/pallas_call | solution.py:198
  106.7 5.3 %shard_map.95 = (f32[256,384]{1,0:T(8,128)}, bf16[256,384]{1,0:T(8,128)(2,1)}) custom-call(s32[7]{0:T(128)} %stack.31.place, bf16[64,2048]{1,0:T(8,128)(2,1)} %collective-permute-done.1.refs_0_.far_a, bf16[64,2048]{1,0:T(8,128)(2,1)} %copy-done.6, bf16[2048,384]{1,0:T(8,128)(2,1)} %join.1.refs_3_.refs_2_.weights_a, ...), custom_call_target="tpu_custom_call", output_to_operand_aliasing={{0}: (5, {}), {1}: (6, {})} | custom-call | tf_op jit(solution)/shard_map/pallas_call | solution.py:198
  112.0 4.5 %collective-permute-start.10 = (bf16[256,384]{1,0:T(8,128)(2,1)}, bf16[256,384]{1,0:T(8,128)(2,1)S(1)}, u32[]{:S(2)}, u32[]{:S(2)}) collective-permute-start(bf16[256,384]{1,0:T(8,128)(2,1)} %get-tuple-element.14), channel_id=1, source_target_pairs={{0,4},{4,0},{8,12},{12,8},{16,20},{20,16},{24,28},{28,24},{32,36},... | collective-permute-start | bytes 589832 | tf_op jit(solution)/shard_map/ppermute | solution.py:362
  116.5 4.6 %collective-permute-done.10.got = bf16[256,384]{1,0:T(8,128)(2,1)S(1)} collective-permute-done((bf16[256,384]{1,0:T(8,128)(2,1)}, bf16[256,384]{1,0:T(8,128)(2,1)S(1)}, u32[]{:S(2)}, u32[]{:S(2)}) %collective-permute-start.10) | collective-permute-done | bytes 196640 | tf_op jit(solution)/shard_map/ppermute | solution.py:362
  121.8 1.8 gates.1.mine.value
  123.6 3.6 %collective-permute-start.11 = (bf16[256,384]{1,0:T(8,128)(2,1)}, bf16[256,384]{1,0:T(8,128)(2,1)S(1)}, u32[]{:S(2)}, u32[]{:S(2)}) collective-permute-start(bf16[256,384]{1,0:T(8,128)(2,1)} %gates.1.mine.value), channel_id=1, source_target_pairs={{0,4},{4,0},{8,12},{12,8},{16,20},{20,16},{24,28},{28,24},{32,36},... | collective-permute-start | bytes 589832 | tf_op jit(solution)/shard_map/ppermute | solution.py:363
  127.3 5.6 %shard_map.96.refs_0_ = bf16[2,4,512,384]{3,2,1,0:T(8,128)(2,1)} custom-call(s32[7]{0:T(128)} %stack.31.place, bf16[256,384]{1,0:T(8,128)(2,1)} %gates.1.mine.value, bf16[128,2048]{1,0:T(8,128)(2,1)} %bitcast.62, bf16[128,2048]{1,0:T(8,128)(2,1)} %copy-done.4, bf16[128,2048]{1,0:T(8,128)(2,1)} %copy-done.3, ...), custom_call_target="tpu_custom_call" | custom-call | tf_op jit(solution)/shard_map/pallas_call | solution.py:307
  133.5 5.6 %shard_map.97 = bf16[2,4,512,384]{3,2,1,0:T(8,128)(2,1)} custom-call(s32[7]{0:T(128)} %stack.31.place, bf16[256,384]{1,0:T(8,128)(2,1)} %copy-done.11, bf16[128,2048]{1,0:T(8,128)(2,1)} %bitcast.63, bf16[128,2048]{1,0:T(8,128)(2,1)} %copy-done.4, bf16[128,2048]{1,0:T(8,128)(2,1)} %copy-done.3, ...), custom_call_target="tpu_custom_call", output_to_operand_aliasing={{}: (7, {})} | custom-call | tf_op jit(solution)/shard_map/pallas_call | solution.py:307
  139.1 1.7 slice_bitcast_fusion
  140.8 1.9 collective-permute-start.12
  142.7 3.4 %collective-permute-done.12 = bf16[4,512,384]{2,1,0:T(8,128)(2,1)S(1)} collective-permute-done((bf16[4,512,384]{2,1,0:T(8,128)(2,1)S(1)}, bf16[4,512,384]{2,1,0:T(8,128)(2,1)S(1)}, u32[]{:S(2)}, u32[]{:S(2)}) %collective-permute-start.12) | collective-permute-done | bytes 1572896 | tf_op jit(solution)/shard_map/ppermute | solution.py:369
  146.1 1.6 convert_add_fusion.2
  147.8 5.6 %collective-permute-start.15 = (bf16[256,384]{1,0:T(8,128)(2,1)S(1)}, bf16[256,384]{1,0:T(8,128)(2,1)}, u32[]{:S(2)}, u32[]{:S(2)}) collective-permute-start(bf16[256,384]{1,0:T(8,128)(2,1)S(1)} %get-tuple-element.22), channel_id=1, source_target_pairs={{0,128},{128,256},{256,384},{384,0},{1,129},{129,257},{257,385},{3... | collective-permute-start | bytes 589832 | tf_op jit(solution)/shard_map/ppermute | solution.py:335
  153.5 5.2 %back.1 = bf16[4,64,2048]{2,1,0:T(8,128)(2,1)} custom-call(s32[7]{0:T(128)} %stack.31.place, bf16[256,384]{1,0:T(8,128)(2,1)} %gates.1.mine.value, bf16[256,384]{1,0:T(8,128)(2,1)} %copy-done.11, bf16[2048,384]{1,0:T(8,128)(2,1)} %join.1.refs_3_.refs_2_.weights_a, bf16[2048,384]{1,0:T(8,128)(2,1)} %copy-done.1), custom_call_target="tpu_custom_call" | custom-call | tf_op jit(solution)/shard_map/back/pallas_call | solution.py:261
  158.7 4.2 %all-to-all-start.1 = ((bf16[4,64,2048]{2,1,0:T(8,128)(2,1)}), bf16[4,64,2048]{2,1,0:T(8,128)(2,1)}, u32[]{:S(2)}, u32[]{:S(2)}) async-start(bf16[4,64,2048]{2,1,0:T(8,128)(2,1)} %back.1), calls=%async_computation.1 | async-start | bytes 2097152 | tf_op jit(solution)/shard_map/all_to_all | solution.py:367
  162.9 1.1 slice.143
  164.0 1.0 slice.142
  165.0 1.9 collective-permute-start.13
  167.0 1.1 fusion.4
  168.9 5.1 %collective-permute-start.16 = (bf16[512,384]{1,0:T(8,128)(2,1)}, bf16[512,384]{1,0:T(8,128)(2,1)}, u32[]{:S(2)}, u32[]{:S(2)}) collective-permute-start(bf16[512,384]{1,0:T(8,128)(2,1)} %pad_maximum_fusion.1), channel_id=1, source_target_pairs={{0,128},{128,256},{256,384},{384,0},{1,129},{129,257},{257,385},{3... | collective-permute-start | bytes 1179656 | tf_op jit(solution)/shard_map/ppermute | solution.py:339
  174.0 0.8 collective-permute-done.13
  174.9 0.8 pad_maximum_fusion
  175.7 1.9 collective-permute-start.14
  178.4 1.4 reduce_sum.12
  179.8 0.8 reshape.29
  180.6 12.2 %all-to-all-start.2 = ((bf16[16,4,2048]{2,1,0:T(4,128)(2,1)}), bf16[16,4,2048]{2,1,0:T(4,128)(2,1)S(1)}, u32[]{:S(2)}, u32[]{:S(2)}) async-start(bf16[16,4,2048]{2,1,0:T(4,128)(2,1)} %reshape.29), calls=%async_computation.2 | async-start | bytes 524288 | tf_op jit(solution)/shard_map/all_to_all | solution.py:376
  192.8 2.2 %fusion.3 = bf16[512,384]{1,0:T(8,128)(2,1)} fusion(bf16[512,384]{1,0:T(8,128)(2,1)} %collective-permute-done.16, bf16[512,384]{1,0:T(8,128)(2,1)} %collective-permute-done.14, bf16[4,512,384]{2,1,0:T(8,128)(2,1)} %copy-done.7, bf16[2,4,512,384]{3,2,1,0:T(8,128)(2,1)S(1)} %copy-done), kind=kLoop, calls=%fused_computation.8 | loop fusion | flops 1572864 | bytes 1966080 | tf_op jit(solution)/shard_map/convert_element_type | solution.py:340
  195.0 1.6 collective-permute-start.17
  196.6 13.9 %all-to-all-done.2.home = bf16[16,4,2048]{2,1,0:T(4,128)(2,1)S(1)} async-done(((bf16[16,4,2048]{2,1,0:T(4,128)(2,1)}), bf16[16,4,2048]{2,1,0:T(4,128)(2,1)S(1)}, u32[]{:S(2)}, u32[]{:S(2)}) %all-to-all-start.2) | async-done | bytes 262176 | tf_op jit(solution)/shard_map/all_to_all | solution.py:376
  211.2 3.3 %home_rows.1 = bf16[128,4096]{1,0:T(8,128)(2,1)} custom-call(s32[2,128]{1,0:T(2,128)} %bitcast.67, bf16[128,4096]{1,0:T(8,128)(2,1)} %latent.3, f32[1,4096]{1,0:T(1,128)} %bitcast.65, bf16[16,4,2048]{2,1,0:T(4,128)(2,1)} %copy-done.8), custom_call_target="tpu_custom_call" | custom-call | tf_op jit(solution)/shard_map/home_rows/pallas_call | solution.py:126
  (55 shorter events, 8.9 us)
Async XLA Ops:
  3.9 68.4 %all-to-all-start = ((bf16[16,8,2048]{2,1,0:T(8,128)(2,1)}), bf16[16,8,2048]{2,1,0:T(8,128)(2,1)S(1)}, u32[]{:S(2)}, u32[]{:S(2)}) async-start(bf16[16,8,2048]{2,1,0:T(8,128)(2,1)} %get-tuple-element.9), calls=%async_computation | async-start | bytes 1048576 | tf_op jit(solution)/shard_map/all_to_all | solution.py:355
  19.1 1.7 collective-permute-start.4
  20.7 21.2 %copy-start.12 = (bf16[512,384]{1,0:T(8,128)(2,1)}, bf16[512,384]{1,0:T(8,128)(2,1)S(1)}, u32[]{:S(2)}) copy-start(bf16[512,384]{1,0:T(8,128)(2,1)S(1)} %collective-permute-done.4.own) | copy-start | bytes 1179652
  20.7 10.9 %collective-permute-start.6 = (bf16[512,384]{1,0:T(8,128)(2,1)S(1)}, bf16[512,384]{1,0:T(8,128)(2,1)S(1)}, u32[]{:S(2)}, u32[]{:S(2)}) collective-permute-start(bf16[512,384]{1,0:T(8,128)(2,1)S(1)} %collective-permute-done.4.own), channel_id=1, source_target_pairs={{0,384},{128,0},{256,128},{384,256},{1,385},{129,1},{257,129},{385... | collective-permute-start | bytes 1179656 | tf_op jit(solution)/shard_map/ppermute | solution.py:324
  23.4 10.2 %collective-permute-start.5 = (bf16[512,384]{1,0:T(8,128)(2,1)S(1)}, bf16[512,384]{1,0:T(8,128)(2,1)S(1)}, u32[]{:S(2)}, u32[]{:S(2)}) collective-permute-start(bf16[512,384]{1,0:T(8,128)(2,1)S(1)} %collective-permute-done.4.own), channel_id=1, source_target_pairs={{0,128},{128,256},{256,384},{384,0},{1,129},{129,257},{257,385},{3... | collective-permute-start | bytes 1179656 | tf_op jit(solution)/shard_map/ppermute | solution.py:323
  31.6 10.3 %copy-start.9 = (bf16[512,384]{1,0:T(8,128)(2,1)}, bf16[512,384]{1,0:T(8,128)(2,1)S(1)}, u32[]{:S(2)}) copy-start(bf16[512,384]{1,0:T(8,128)(2,1)S(1)} %collective-permute-done.6.right) | copy-start | bytes 1179652
  31.6 8.8 %collective-permute-start.8 = (bf16[256,384]{1,0:T(8,128)(2,1)S(1)}, bf16[256,384]{1,0:T(8,128)(2,1)S(1)}, u32[]{:S(2)}, u32[]{:S(2)}) collective-permute-start(bf16[256,384]{1,0:T(8,128)(2,1)S(1)} %slice.89), channel_id=1, source_target_pairs={{0,384},{128,0},{256,128},{384,256},{1,385},{129,1},{257,129},{385... | collective-permute-start | bytes 589832 | tf_op jit(solution)/shard_map/ppermute | solution.py:326
  33.6 8.4 %copy-start.10 = (bf16[512,384]{1,0:T(8,128)(2,1)}, bf16[512,384]{1,0:T(8,128)(2,1)S(1)}, u32[]{:S(2)}) copy-start(bf16[512,384]{1,0:T(8,128)(2,1)S(1)} %collective-permute-done.5.left) | copy-start | bytes 1179652
  33.6 8.3 %collective-permute-start.7 = (bf16[256,384]{1,0:T(8,128)(2,1)S(1)}, bf16[256,384]{1,0:T(8,128)(2,1)S(1)}, u32[]{:S(2)}, u32[]{:S(2)}) collective-permute-start(bf16[256,384]{1,0:T(8,128)(2,1)S(1)} %slice.88), channel_id=1, source_target_pairs={{0,128},{128,256},{256,384},{384,0},{1,129},{129,257},{257,385},{3... | collective-permute-start | bytes 589832 | tf_op jit(solution)/shard_map/ppermute | solution.py:325
  40.4 1.5 copy-start.13
  41.9 0.7 copy-start.14
  45.2 52.8 %collective-permute-start.9 = (bf16[2048,384]{1,0:T(8,128)(2,1)}, bf16[2048,384]{1,0:T(8,128)(2,1)S(1)}, u32[]{:S(2)}, u32[]{:S(2)}) collective-permute-start(bf16[2048,384]{1,0:T(8,128)(2,1)} %join.1.refs_3_.refs_2_.weights_a), channel_id=1, source_target_pairs={{0,64},{64,0},{1,65},{65,1},{2,66},{66,2},{3,67},{67,3},{4,68},{68... | collective-permute-start | bytes 4718600 | tf_op jit(solution)/shard_map/ppermute | solution.py:357
  72.3 25.8 %copy-start.2 = (bf16[16,8,2048]{2,1,0:T(8,128)(2,1)}, bf16[16,8,2048]{2,1,0:T(8,128)(2,1)S(1)}, u32[]{:S(2)}) copy-start(bf16[16,8,2048]{2,1,0:T(8,128)(2,1)S(1)} %all-to-all-done) | copy-start | bytes 1572868
  72.3 16.0 %collective-permute-start.2 = (bf16[128,2048]{1,0:T(8,128)(2,1)S(1)}, bf16[128,2048]{1,0:T(8,128)(2,1)S(1)}, u32[]{:S(2)}, u32[]{:S(2)}) collective-permute-start(bf16[128,2048]{1,0:T(8,128)(2,1)S(1)} %bitcast.59), channel_id=1, source_target_pairs={{0,3},{1,0},{2,1},{3,2},{4,7},{5,4},{6,5},{7,6},{8,11},{9,8},{10,9... | collective-permute-start | bytes 1572872 | tf_op jit(solution)/shard_map/ppermute | solution.py:324
  77.0 17.7 %collective-permute-start = (bf16[128,2048]{1,0:T(8,128)(2,1)S(1)}, bf16[128,2048]{1,0:T(8,128)(2,1)S(1)}, u32[]{:S(2)}, u32[]{:S(2)}) collective-permute-start(bf16[128,2048]{1,0:T(8,128)(2,1)S(1)} %bitcast.60), channel_id=1, source_target_pairs={{0,1},{1,2},{2,3},{3,0},{4,5},{5,6},{6,7},{7,4},{8,9},{9,10},{10,1... | collective-permute-start | bytes 1572872 | tf_op jit(solution)/shard_map/ppermute | solution.py:323
  88.3 9.7 %copy-start.3 = (bf16[128,2048]{1,0:T(8,128)(2,1)}, bf16[128,2048]{1,0:T(8,128)(2,1)S(1)}, u32[]{:S(2)}) copy-start(bf16[128,2048]{1,0:T(8,128)(2,1)S(1)} %collective-permute-done.2.refs_2_.right) | copy-start | bytes 1572868
  89.1 16.9 %collective-permute-start.3 = (bf16[64,2048]{1,0:T(8,128)(2,1)}, bf16[64,2048]{1,0:T(8,128)(2,1)S(1)}, u32[]{:S(2)}, u32[]{:S(2)}) collective-permute-start(bf16[64,2048]{1,0:T(8,128)(2,1)} %slice.87), channel_id=1, source_target_pairs={{0,3},{1,0},{2,1},{3,2},{4,7},{5,4},{6,5},{7,6},{8,11},{9,8},{10,9... | collective-permute-start | bytes 786440 | tf_op jit(solution)/shard_map/ppermute | solution.py:326
  94.7 3.4 %copy-start.4 = (bf16[128,2048]{1,0:T(8,128)(2,1)}, bf16[128,2048]{1,0:T(8,128)(2,1)S(1)}, u32[]{:S(2)}) copy-start(bf16[128,2048]{1,0:T(8,128)(2,1)S(1)} %collective-permute-done.refs_1_.left) | copy-start | bytes 1572868
  95.5 10.5 %collective-permute-start.1 = (bf16[64,2048]{1,0:T(8,128)(2,1)}, bf16[64,2048]{1,0:T(8,128)(2,1)}, u32[]{:S(2)}, u32[]{:S(2)}) collective-permute-start(bf16[64,2048]{1,0:T(8,128)(2,1)} %slice.86), channel_id=1, source_target_pairs={{0,1},{1,2},{2,3},{3,0},{4,5},{5,6},{6,7},{7,4},{8,9},{9,10},{10,1... | collective-permute-start | bytes 786440 | tf_op jit(solution)/shard_map/ppermute | solution.py:325
  98.1 1.2 copy-start.1
  106.0 0.7 copy-start.6
  112.0 9.1 %collective-permute-start.10 = (bf16[256,384]{1,0:T(8,128)(2,1)}, bf16[256,384]{1,0:T(8,128)(2,1)S(1)}, u32[]{:S(2)}, u32[]{:S(2)}) collective-permute-start(bf16[256,384]{1,0:T(8,128)(2,1)} %get-tuple-element.14), channel_id=1, source_target_pairs={{0,4},{4,0},{8,12},{12,8},{16,20},{20,16},{24,28},{28,24},{32,36},... | collective-permute-start | bytes 589832 | tf_op jit(solution)/shard_map/ppermute | solution.py:362
  121.1 0.7 copy-start.15
  123.6 9.2 %collective-permute-start.11 = (bf16[256,384]{1,0:T(8,128)(2,1)}, bf16[256,384]{1,0:T(8,128)(2,1)S(1)}, u32[]{:S(2)}, u32[]{:S(2)}) collective-permute-start(bf16[256,384]{1,0:T(8,128)(2,1)} %gates.1.mine.value), channel_id=1, source_target_pairs={{0,4},{4,0},{8,12},{12,8},{16,20},{20,16},{24,28},{28,24},{32,36},... | collective-permute-start | bytes 589832 | tf_op jit(solution)/shard_map/ppermute | solution.py:363
  132.8 0.7 copy-start.11
  139.1 7.0 %copy-start = (bf16[2,4,512,384]{3,2,1,0:T(8,128)(2,1)S(1)}, bf16[2,4,512,384]{3,2,1,0:T(8,128)(2,1)}, u32[]{:S(2)}) copy-start(bf16[2,4,512,384]{3,2,1,0:T(8,128)(2,1)} %shard_map.97) | copy-start | bytes 9437188
  140.8 5.3 %collective-permute-start.12 = (bf16[4,512,384]{2,1,0:T(8,128)(2,1)S(1)}, bf16[4,512,384]{2,1,0:T(8,128)(2,1)S(1)}, u32[]{:S(2)}, u32[]{:S(2)}) collective-permute-start(bf16[4,512,384]{2,1,0:T(8,128)(2,1)S(1)} %slice_bitcast_fusion), channel_id=1, source_target_pairs={{0,64},{64,0},{1,65},{65,1},{2,66},{66,2},{3,67},{67,3},{4,68},{68... | collective-permute-start | bytes 4718600 | tf_op jit(solution)/shard_map/ppermute | solution.py:369
  146.1 1.7 copy-start.7
  147.8 19.1 %collective-permute-start.15 = (bf16[256,384]{1,0:T(8,128)(2,1)S(1)}, bf16[256,384]{1,0:T(8,128)(2,1)}, u32[]{:S(2)}, u32[]{:S(2)}) collective-permute-start(bf16[256,384]{1,0:T(8,128)(2,1)S(1)} %get-tuple-element.22), channel_id=1, source_target_pairs={{0,128},{128,256},{256,384},{384,0},{1,129},{129,257},{257,385},{3... | collective-permute-start | bytes 589832 | tf_op jit(solution)/shard_map/ppermute | solution.py:335
  158.7 19.7 %all-to-all-start.1 = ((bf16[4,64,2048]{2,1,0:T(8,128)(2,1)}), bf16[4,64,2048]{2,1,0:T(8,128)(2,1)}, u32[]{:S(2)}, u32[]{:S(2)}) async-start(bf16[4,64,2048]{2,1,0:T(8,128)(2,1)} %back.1), calls=%async_computation.1 | async-start | bytes 2097152 | tf_op jit(solution)/shard_map/all_to_all | solution.py:367
  162.9 11.9 %copy-start.5 = (f32[512,384]{1,0:T(8,128)S(1)}, f32[512,384]{1,0:T(8,128)}, u32[]{:S(2)}) copy-start(f32[512,384]{1,0:T(8,128)} %get-tuple-element.18) | copy-start | bytes 2359300
  165.0 9.8 %collective-permute-start.13 = (bf16[256,384]{1,0:T(8,128)(2,1)S(1)}, bf16[256,384]{1,0:T(8,128)(2,1)S(1)}, u32[]{:S(2)}, u32[]{:S(2)}) collective-permute-start(bf16[256,384]{1,0:T(8,128)(2,1)S(1)} %get-tuple-element.21), channel_id=1, source_target_pairs={{0,384},{128,0},{256,128},{384,256},{1,385},{129,1},{257,129},{385... | collective-permute-start | bytes 589832 | tf_op jit(solution)/shard_map/ppermute | solution.py:334
  168.9 23.9 %collective-permute-start.16 = (bf16[512,384]{1,0:T(8,128)(2,1)}, bf16[512,384]{1,0:T(8,128)(2,1)}, u32[]{:S(2)}, u32[]{:S(2)}) collective-permute-start(bf16[512,384]{1,0:T(8,128)(2,1)} %pad_maximum_fusion.1), channel_id=1, source_target_pairs={{0,128},{128,256},{256,384},{384,0},{1,129},{129,257},{257,385},{3... | collective-permute-start | bytes 1179656 | tf_op jit(solution)/shard_map/ppermute | solution.py:339
  175.7 17.1 %collective-permute-start.14 = (bf16[512,384]{1,0:T(8,128)(2,1)}, bf16[512,384]{1,0:T(8,128)(2,1)}, u32[]{:S(2)}, u32[]{:S(2)}) collective-permute-start(bf16[512,384]{1,0:T(8,128)(2,1)} %pad_maximum_fusion), channel_id=1, source_target_pairs={{0,384},{128,0},{256,128},{384,256},{1,385},{129,1},{257,129},{385... | collective-permute-start | bytes 1179656 | tf_op jit(solution)/shard_map/ppermute | solution.py:338
  180.6 29.9 %all-to-all-start.2 = ((bf16[16,4,2048]{2,1,0:T(4,128)(2,1)}), bf16[16,4,2048]{2,1,0:T(4,128)(2,1)S(1)}, u32[]{:S(2)}, u32[]{:S(2)}) async-start(bf16[16,4,2048]{2,1,0:T(4,128)(2,1)} %reshape.29), calls=%async_computation.2 | async-start | bytes 524288 | tf_op jit(solution)/shard_map/all_to_all | solution.py:376
  195.0 19.5 %collective-permute-start.17 = (bf16[512,384]{1,0:T(8,128)(2,1)}, bf16[512,384]{1,0:T(8,128)(2,1)S(1)}, u32[]{:S(2)}, u32[]{:S(2)}) collective-permute-start(bf16[512,384]{1,0:T(8,128)(2,1)} %fusion.3), channel_id=1, source_target_pairs={{0,0},{4,64},{8,8},{12,72},{16,16},{20,80},{24,24},{28,88},{32,32}... | collective-permute-start | bytes 1179656 | tf_op jit(solution)/shard_map/ppermute | solution.py:371
  210.5 0.7 copy-start.8

commit v5 on v3

--- a/solution.py
+++ b/solution.py
@@ -16,6 +16,7 @@
 D = 4096
 HALF = D // 2
 CUT = 512
+WIDE = 2 * CUT
 ROWS = 2 * Z * X * CAP
 F32 = jnp.float32
 BF16 = jnp.bfloat16
@@ -169,59 +170,46 @@
 
 def row_specs():
     return [
-        pl.BlockSpec((n, CUT), lambda i, *_: (0, i))
+        pl.BlockSpec((n, WIDE), lambda i, *_: (0, i))
         for n in (ROWS // 4, ROWS // 4, ROWS // 4, ROWS // 8, ROWS // 8)
     ]
 
 
 def weight_spec():
-    return pl.BlockSpec((2, CUT, 3 * HID), lambda i, *_: (0, i, 0))
+    return pl.BlockSpec((2, WIDE, 3 * HID), lambda i, *_: (0, i, 0))
 
 
 def whole(dims):
     return pl.BlockSpec(dims, lambda i, *_: (0,) * len(dims))
 
 
-def mix(place, at, blocks, weights, so_far):
+def mix(place, blocks, weights):
     rows = sum(block.shape[0] for block in blocks)
-    part = pl.BlockSpec((rows // 2, 3 * HID), lambda i, *_: (at, 0))
-    dims = (ROWS // 2, 3 * HID)
-    hold = [pl.BlockSpec(memory_space=pl.ANY)] * len(so_far)
-    first = 2 + len(blocks)
+    dims = (rows // 2, 3 * HID)
     return pl.pallas_call(
         functools.partial(mix_kernel, len(blocks)),
         grid_spec=pltpu.PrefetchScalarGridSpec(
             num_scalar_prefetch=1,
-            grid=(HALF // CUT,),
+            grid=(HALF // WIDE,),
             in_specs=[
-                *[pl.BlockSpec((b.shape[0], CUT), lambda i, *_: (0, i)) for b in blocks],
+                *[pl.BlockSpec((b.shape[0], WIDE), lambda i, *_: (0, i)) for b in blocks],
                 weight_spec(),
-                *hold,
             ],
-            out_specs=[part, part],
+            out_specs=[whole(dims), whole(dims)],
             scratch_shapes=[pltpu.VMEM((2, rows, 3 * HID), F32)],
         ),
         out_shape=[shape(dims, F32), shape(dims, BF16)],
-        input_output_aliases={first + k: k for k in range(len(so_far))},
-    )(place, *blocks, weights, *so_far)
-
-
-def gates_kernel(mine, got, out):
-    total = mine[...] + got[...].astype(F32)
+    )(place, *blocks, weights)
+
+
+def gates(total):
     gate = total[:, :HID]
     up = total[:, HID : 2 * HID]
     dh = total[:, 2 * HID :]
     sig = jax.nn.sigmoid(gate)
     act = gate * sig
-    out[:, :HID] = (dh * up * sig * (1.0 + gate * (1.0 - sig))).astype(BF16)
-    out[:, HID : 2 * HID] = (dh * act).astype(BF16)
-    out[:, 2 * HID :] = (act * up).astype(BF16)
-
-
-def gates(mine, got):
-    return pl.pallas_call(
-        gates_kernel, out_shape=shape(mine.shape, BF16), name="gates"
-    )(mine, got)
+    d_gate = dh * up * sig * (1.0 + gate * (1.0 - sig))
+    return jnp.concatenate([d_gate, dh * act, act * up], axis=1).astype(BF16)
 
 
 def back_kernel(place, mine, other, weights, out, inner):
@@ -250,9 +238,9 @@
         back_kernel,
         grid_spec=pltpu.PrefetchScalarGridSpec(
             num_scalar_prefetch=1,
-            grid=(HALF // CUT,),
+            grid=(HALF // WIDE,),
             in_specs=[whole(dims), whole(dims), weight_spec()],
-            out_specs=pl.BlockSpec((X, ROWS // 8, CUT), lambda i, *_: (0, 0, i)),
+            out_specs=pl.BlockSpec((X, ROWS // 8, WIDE), lambda i, *_: (0, 0, i)),
             scratch_shapes=[pltpu.VMEM((2, *dims), BF16)],
         ),
         out_shape=shape((X, ROWS // 8, HALF), BF16),
@@ -280,9 +268,11 @@
             inner[:, cols] = pair.reshape(ROWS, width).astype(BF16)
 
     rows = jnp.concatenate([own[...], left[...], right[...], far_a[...], far_b[...]], axis=0)
-    out[0, 0] = lax.dot_general(
+    total = lax.dot_general(
         rows, inner[...], (((0,), (0,)), ((), ())), preferred_element_type=F32
     ).astype(BF16)
+    for k in range(WIDE // CUT):
+        out[0, k] = total[k * CUT : (k + 1) * CUT]
 
 
 def grads(place, turn, value, blocks, so_far):
@@ -296,9 +286,9 @@
         grads_kernel,
         grid_spec=pltpu.PrefetchScalarGridSpec(
             num_scalar_prefetch=1,
-            grid=(HALF // CUT,),
+            grid=(HALF // WIDE,),
             in_specs=[whole((ROWS // 2, 3 * HID)), *row_specs(), *hold],
-            out_specs=pl.BlockSpec((1, 1, CUT, 3 * HID), at),
+            out_specs=pl.BlockSpec((1, WIDE // CUT, CUT, 3 * HID), at),
             scratch_shapes=[pltpu.VMEM((ROWS, 3 * HID), BF16)],
         ),
         out_shape=shape((2, HALF // CUT, CUT, 3 * HID), BF16),
@@ -327,18 +317,19 @@
     far_b = lax.ppermute(right[half:], "x", MINUS)
     blocks = own, left, right, far_a, far_b
 
-    parts = ()
-    for at, some in enumerate(((own,), (left,), (right,), (far_a, far_b))):
-        parts = mix(place, at, some, weights, parts)
-    mine, other = parts
-    inner = gates(mine, lax.ppermute(other, "z", FLIP))
+    totals = []
+    for some in (blocks[:3], blocks[3:]):
+        mine, other = mix(place, some, weights)
+        got = lax.ppermute(other, "z", FLIP)
+        totals.append(mine + got.astype(F32))
+    inner = gates(jnp.concatenate(totals, axis=0))
     outer = lax.ppermute(inner, "z", FLIP)
 
     grad = grads(place, 0, inner, blocks, ())
+    grad = grads(place, 1, outer, blocks, (grad,))
+    partner = lax.ppermute(grad[1], "c", [(0, 1), (1, 0)])
     part = back(place, inner, outer, weights)
     part = lax.all_to_all(part, "x", 0, 0, tiled=True)
-    grad = grads(place, 1, outer, blocks, (grad,))
-    partner = lax.ppermute(grad[1], "c", [(0, 1), (1, 0)])
     grad = (grad[0].astype(F32) + partner.astype(F32)).astype(BF16).reshape(HALF, 3 * HID)
     grad = lax.psum_scatter(grad, "y", scatter_dimension=0, tiled=True)
     grad = lax.ppermute(grad, ("c", "z"), SWAP)

time: 210 us -> 204 us (0.971)
  Pallas kernels: 47.7 us -> 31.3 us
  waiting for transfers between devices: 31.9 us -> 39.9 us
  starting transfers between devices: 32.8 us -> 35.9 us
    pallas_call x4 -> x2, Pallas kernels: 21.2 us -> 9.84 us  [mix(): pl.pallas_call(functools.partial(mix_kernel, len(blocks)), grid_spec=pltp...]
    ppermute x1, waiting for transfers between devices: 0.01 us -> 5.84 us  [work(): far_a = lax.ppermute(left[:half], 'x', PLUS)]
    ppermute x1 -> x2, starting transfers between devices: 2.58 us -> 5.95 us  [work(): got = lax.ppermute(other, 'z', FLIP)]
    unnamed x21 -> x23, local copies, waits for them, and re-layouts: 4.42 us -> 3.68 us
    ppermute x1 -> x2, waiting for transfers between devices: 5.41 us -> 5.49 us  [work(): got = lax.ppermute(other, 'z', FLIP)]
  transfers between devices with their start and end apart: 12 -> 13, of which waited for: 5 -> 8; matrix products, arithmetic and copies ran while one was open for 1% -> 1% of each run, Pallas kernels for 14% -> 9%
where the time goes in v5:
time: 204 us; the launch traced here: 203 us
  blocking collectives  70.9 us (35%)
  waiting for transfers between devices  39.9 us (20%)
  starting transfers between devices  35.9 us (18%)
  Pallas kernels  31.3 us (15%)
  between operations  14.3 us (7%)
  local copies, waits for them, and re-layouts  6.97 us (3%)
  other arithmetic  3.58 us (2%)
    all_to_all x1, blocking collectives, work(): got = lax.all_to_all(send, 'z', 0, 0, tiled=True)  51.7 us
    all_to_all x1, blocking collectives, work(): part = lax.all_to_all(part, 'x', 0, 0, tiled=True)  19.2 us
    all_to_all x1, waiting for transfers between devices, work(): home = lax.all_to_all(summed.reshape(Z, CAP, HALF), 'z', 0, 0, tiled=True)  16.3 us
    pallas_call x2, Pallas kernels, mix(): pl.pallas_call(functools.partial(mix_kernel, len(blocks)), grid_spec=pltp...  9.84 us
    pallas_call x2, Pallas kernels, grads(): pl.pallas_call(grads_kernel, grid_spec=pltpu.PrefetchScalarGridSpec(num_s...  9.18 us
    all_to_all x1, starting transfers between devices, work(): home = lax.all_to_all(summed.reshape(Z, CAP, HALF), 'z', 0, 0, tiled=True)  8.47 us
    ppermute x1, waiting for transfers between devices, work(): right = lax.ppermute(own, 'x', MINUS)  7.15 us
    ppermute x2, starting transfers between devices, work(): got = lax.ppermute(other, 'z', FLIP)  5.95 us
  transfers between devices with their start and end apart: 13, of which 8 were waited for; matrix products, arithmetic and copies ran while one was open for 1% of the time, Pallas kernels for 9%

profile of v5, /device:TPU:24, one launch (start us, length us, event | category | flops | bytes accessed | tf_op | source)
XLA Modules:
  0.0 202.8 jit_solution(10488928896867924333)
XLA Ops:
  7.2 0.0 all-gather.2.cloned.1.call-start
  7.2 3.2 %send_rows.1 = (bf16[16,8,2048]{2,1,0:T(8,128)(2,1)}, bf16[512,384]{1,0:T(8,128)(2,1)}) custom-call(s32[2,128]{1,0:T(2,128)} %bitcast.33, f32[2,128]{1,0:T(2,128)} %bitcast.35, bf16[128,4096]{1,0:T(8,128)(2,1)} %latent.3, bf16[128,4096]{1,0:T(8,128)(2,1)} %dout.1, f32[1,4096]{1,0:T(1,128)} %bitcast.31, bf16[1,512,256]{2,1,0:T(8,128)(2,1)} %gate_up.1, ...), custom_call_target="tpu_custom_call" | custom-call | tf_op jit(solution)/shard_map/send_rows/pallas_call | solution.py:84
  10.4 1.6 collective-permute-start.2
  12.1 0.8 copy-done.9
  12.8 1.8 hold.1
  14.6 0.0 all-gather.2.cloned.1.call-update
  14.6 0.0 reduce-scatter.2.cloned.1.call-start
  14.7 51.7 %all_to_all.15 = bf16[16,8,2048]{2,1,0:T(8,128)(2,1)S(1)} all-to-all(bf16[16,8,2048]{2,1,0:T(8,128)(2,1)} %get-tuple-element.9), channel_id=1, replica_groups=mesh['y'=4,'c'=2,'z'=16,'x'=4] {'z'}, dimensions={0} | all-to-all | bytes 1048576 | tf_op jit(solution)/shard_map/all_to_all | solution.py:308
  66.4 4.7 %collective-permute-start.1 = (bf16[128,2048]{1,0:T(8,128)(2,1)S(1)}, bf16[128,2048]{1,0:T(8,128)(2,1)S(1)}, u32[]{:S(2)}, u32[]{:S(2)}) collective-permute-start(bf16[128,2048]{1,0:T(8,128)(2,1)S(1)} %bitcast.25), channel_id=1, source_target_pairs={{0,3},{1,0},{2,1},{3,2},{4,7},{5,4},{6,5},{7,6},{8,11},{9,8},{10,9... | collective-permute-start | bytes 1572872 | tf_op jit(solution)/shard_map/ppermute | solution.py:315
  71.0 1.9 collective-permute-start
  73.0 7.2 %collective-permute-done.1.refs_2_.right = bf16[128,2048]{1,0:T(8,128)(2,1)S(1)} collective-permute-done((bf16[128,2048]{1,0:T(8,128)(2,1)S(1)}, bf16[128,2048]{1,0:T(8,128)(2,1)S(1)}, u32[]{:S(2)}, u32[]{:S(2)}) %collective-permute-start.1) | collective-permute-done | bytes 524320 | tf_op jit(solution)/shard_map/ppermute | solution.py:315
  80.2 5.2 %collective-permute-start.5 = (bf16[64,2048]{1,0:T(8,128)(2,1)S(1)}, bf16[64,2048]{1,0:T(8,128)(2,1)S(1)}, u32[]{:S(2)}, u32[]{:S(2)}) collective-permute-start(bf16[64,2048]{1,0:T(8,128)(2,1)S(1)} %slice.37), channel_id=1, source_target_pairs={{0,3},{1,0},{2,1},{3,2},{4,7},{5,4},{6,5},{7,6},{8,11},{9,8},{10,9... | collective-permute-start | bytes 786440 | tf_op jit(solution)/shard_map/ppermute | solution.py:317
  85.4 0.2 collective-permute-done.refs_1_.left
  85.6 1.9 collective-permute-start.4
  87.6 0.7 pad_add_fusion.place
  88.2 1.0 collective-permute-done.5.refs_1_.far_b
  89.3 5.8 %collective-permute-done.4.refs_0_.far_a = bf16[64,2048]{1,0:T(8,128)(2,1)S(1)} collective-permute-done((bf16[64,2048]{1,0:T(8,128)(2,1)S(1)}, bf16[64,2048]{1,0:T(8,128)(2,1)S(1)}, u32[]{:S(2)}, u32[]{:S(2)}) %collective-permute-start.4) | collective-permute-done | bytes 262176 | tf_op jit(solution)/shard_map/ppermute | solution.py:316
  95.1 0.7 copy-done.5
  95.8 4.2 %shard_map.95 = (f32[64,384]{1,0:T(8,128)}, bf16[64,384]{1,0:T(8,128)(2,1)}) custom-call(s32[3]{0:T(128)} %pad_add_fusion.place, bf16[64,2048]{1,0:T(8,128)(2,1)} %copy-done.5, bf16[64,2048]{1,0:T(8,128)(2,1)} %copy-done.4, bf16[2,2048,384]{2,1,0:T(8,128)(2,1)} %bitcast.22), custom_call_target="tpu_custom_call" | custom-call | tf_op jit(solution)/shard_map/pallas_call | solution.py:189
  100.0 2.7 %collective-permute-start.6 = (bf16[64,384]{1,0:T(8,128)(2,1)}, bf16[64,384]{1,0:T(8,128)(2,1)S(1)}, u32[]{:S(2)}, u32[]{:S(2)}) collective-permute-start(bf16[64,384]{1,0:T(8,128)(2,1)} %get-tuple-element.14), channel_id=1, source_target_pairs={{0,4},{4,0},{8,12},{12,8},{16,20},{20,16},{24,28},{28,24},{32,36},... | collective-permute-start | bytes 147464 | tf_op jit(solution)/shard_map/ppermute | solution.py:323
  102.7 5.6 %shard_map.94 = (f32[192,384]{1,0:T(8,128)}, bf16[192,384]{1,0:T(8,128)(2,1)}) custom-call(s32[3]{0:T(128)} %pad_add_fusion.place, bf16[128,2048]{1,0:T(8,128)(2,1)} %bitcast.27, bf16[128,2048]{1,0:T(8,128)(2,1)} %copy-done.3, bf16[128,2048]{1,0:T(8,128)(2,1)} %copy-done.2, bf16[2,2048,384]{2,1,0:T(8,128)(2,1)} %bitcast.23), custom_call_target="tpu_custom_call" | custom-call | tf_op jit(solution)/shard_map/pallas_call | solution.py:189
  108.4 3.2 %collective-permute-start.3 = (bf16[192,384]{1,0:T(8,128)(2,1)}, bf16[192,384]{1,0:T(8,128)(2,1)S(1)}, u32[]{:S(2)}, u32[]{:S(2)}) collective-permute-start(bf16[192,384]{1,0:T(8,128)(2,1)} %get-tuple-element.12), channel_id=1, source_target_pairs={{0,4},{4,0},{8,12},{12,8},{16,20},{20,16},{24,28},{28,24},{32,36},... | collective-permute-start | bytes 442376 | tf_op jit(solution)/shard_map/ppermute | solution.py:323
  111.7 5.5 %collective-permute-done.3 = bf16[192,384]{1,0:T(8,128)(2,1)S(1)} collective-permute-done((bf16[192,384]{1,0:T(8,128)(2,1)}, bf16[192,384]{1,0:T(8,128)(2,1)S(1)}, u32[]{:S(2)}, u32[]{:S(2)}) %collective-permute-start.3) | collective-permute-done | bytes 147488 | tf_op jit(solution)/shard_map/ppermute | solution.py:323
  117.2 1.0 convert_add_fusion.1
  118.2 0.1 multiply_convert_fusion.2
  118.2 0.1 multiply_convert_fusion.1
  118.3 2.5 %collective-permute-start.7 = (bf16[256,384]{1,0:T(8,128)(2,1)S(1)}, bf16[256,384]{1,0:T(8,128)(2,1)S(1)}, u32[]{:S(2)}, u32[]{:S(2)}) collective-permute-start(bf16[256,384]{1,0:T(8,128)(2,1)S(1)} %pad_maximum_fusion.mine.value), channel_id=1, source_target_pairs={{0,4},{4,0},{8,12},{12,8},{16,20},{20,16},{24,28},{28,24},{32,36},... | collective-permute-start | bytes 589832 | tf_op jit(solution)/shard_map/ppermute | solution.py:326
  120.9 4.6 %shard_map.96.refs_0_ = bf16[2,4,512,384]{3,2,1,0:T(8,128)(2,1)} custom-call(s32[3]{0:T(128)} %pad_add_fusion.place, bf16[256,384]{1,0:T(8,128)(2,1)} %copy-done.6, bf16[128,2048]{1,0:T(8,128)(2,1)} %bitcast.28, bf16[128,2048]{1,0:T(8,128)(2,1)} %copy-done.3, bf16[128,2048]{1,0:T(8,128)(2,1)} %copy-done.2, bf16[64,2048]{1,0:T(8,128)(2,1)} %copy-done.5, ...), custom_call_target="tpu_custom_call" | custom-call | tf_op jit(solution)/shard_map/pallas_call | solution.py:285
  125.5 0.5 collective-permute-done.7.other.value
  125.9 0.7 copy-done.8
  126.6 4.6 %shard_map.97 = bf16[2,4,512,384]{3,2,1,0:T(8,128)(2,1)} custom-call(s32[3]{0:T(128)} %pad_add_fusion.place, bf16[256,384]{1,0:T(8,128)(2,1)} %copy-done.8, bf16[128,2048]{1,0:T(8,128)(2,1)} %bitcast.29, bf16[128,2048]{1,0:T(8,128)(2,1)} %copy-done.3, bf16[128,2048]{1,0:T(8,128)(2,1)} %copy-done.2, ...), custom_call_target="tpu_custom_call", output_to_operand_aliasing={{}: (7, {})} | custom-call | tf_op jit(solution)/shard_map/pallas_call | solution.py:285
  131.2 1.7 slice_bitcast_fusion
  132.9 1.9 collective-permute-start.8
  134.9 3.4 %collective-permute-done.8 = bf16[4,512,384]{2,1,0:T(8,128)(2,1)S(1)} collective-permute-done((bf16[4,512,384]{2,1,0:T(8,128)(2,1)S(1)}, bf16[4,512,384]{2,1,0:T(8,128)(2,1)S(1)}, u32[]{:S(2)}, u32[]{:S(2)}) %collective-permute-start.8) | collective-permute-done | bytes 1572896 | tf_op jit(solution)/shard_map/ppermute | solution.py:330
  138.3 1.6 fusion
  139.8 0.0 reduce-scatter.2.cloned.1.call-update
  139.8 4.0 %back.1 = bf16[4,64,2048]{2,1,0:T(8,128)(2,1)} custom-call(s32[3]{0:T(128)} %pad_add_fusion.place, bf16[256,384]{1,0:T(8,128)(2,1)} %copy-done.6, bf16[256,384]{1,0:T(8,128)(2,1)} %copy-done.8, bf16[2,2048,384]{2,1,0:T(8,128)(2,1)} %bitcast.24), custom_call_target="tpu_custom_call" | custom-call | tf_op jit(solution)/shard_map/back/pallas_call | solution.py:237
  143.8 19.2 %all_to_all.16 = bf16[4,64,2048]{2,1,0:T(8,128)(2,1)S(1)} all-to-all(bf16[4,64,2048]{2,1,0:T(8,128)(2,1)} %back.1), channel_id=1, replica_groups=mesh['y'=4,'c'=2,'z'=16,'x'=4] {'x'}, dimensions={0} | all-to-all | bytes 2097152 | tf_op jit(solution)/shard_map/all_to_all | solution.py:332
  163.0 0.2 reduce_sum.12
  163.2 0.8 reshape.22
  164.0 8.5 %all-to-all-start.2 = ((bf16[16,4,2048]{2,1,0:T(4,128)(2,1)}), bf16[16,4,2048]{2,1,0:T(4,128)(2,1)S(1)}, u32[]{:S(2)}, u32[]{:S(2)}) async-start(bf16[16,4,2048]{2,1,0:T(4,128)(2,1)} %reshape.22), calls=%async_computation.2 | async-start | bytes 524288 | tf_op jit(solution)/shard_map/all_to_all | solution.py:340
  172.4 0.0 reduce-scatter.2.cloned.1.call-done
  172.5 1.7 collective-permute-start.9
  174.1 16.3 %all-to-all-done.2.home = bf16[16,4,2048]{2,1,0:T(4,128)(2,1)S(1)} async-done(((bf16[16,4,2048]{2,1,0:T(4,128)(2,1)}), bf16[16,4,2048]{2,1,0:T(4,128)(2,1)S(1)}, u32[]{:S(2)}, u32[]{:S(2)}) %all-to-all-start.2) | async-done | bytes 262176 | tf_op jit(solution)/shard_map/all_to_all | solution.py:340
  190.4 0.7 copy-done.7
  191.2 3.3 %home_rows.1 = bf16[128,4096]{1,0:T(8,128)(2,1)} custom-call(s32[2,128]{1,0:T(2,128)} %bitcast.34, bf16[128,4096]{1,0:T(8,128)(2,1)} %latent.3, f32[1,4096]{1,0:T(1,128)} %bitcast.32, bf16[16,4,2048]{2,1,0:T(4,128)(2,1)} %copy-done.7), custom_call_target="tpu_custom_call" | custom-call | tf_op jit(solution)/shard_map/home_rows/pallas_call | solution.py:120
  194.5 0.8 copy.12
  195.3 0.7 slice_bitcast_fusion.2
  (27 shorter events, 0.1 us)
Async XLA Ops:
  7.2 87.9 %all-gather.2.cloned.1.call-start = ((), (), s32[]{:S(2)}) async-start(), calls=%async_computation.4 | async-start | bytes 3538944 | tf_op jit(solution)/shard_map/all_gather | solution.py:309
  10.4 1.6 collective-permute-start.2
  12.1 0.8 copy-start.9
  14.6 157.8 %reduce-scatter.2.cloned.1.call-start = ((), (), s32[]{:S(2)}) async-start(), calls=%async_computation.5 | async-start | bytes 1966080 | tf_op jit(solution)/shard_map/reduce_scatter | solution.py:334
  66.4 36.3 %copy-start.1 = (bf16[16,8,2048]{2,1,0:T(8,128)(2,1)}, bf16[16,8,2048]{2,1,0:T(8,128)(2,1)S(1)}, u32[]{:S(2)}) copy-start(bf16[16,8,2048]{2,1,0:T(8,128)(2,1)S(1)} %all_to_all.15) | copy-start | bytes 1572868
  66.4 13.7 %collective-permute-start.1 = (bf16[128,2048]{1,0:T(8,128)(2,1)S(1)}, bf16[128,2048]{1,0:T(8,128)(2,1)S(1)}, u32[]{:S(2)}, u32[]{:S(2)}) collective-permute-start(bf16[128,2048]{1,0:T(8,128)(2,1)S(1)} %bitcast.25), channel_id=1, source_target_pairs={{0,3},{1,0},{2,1},{3,2},{4,7},{5,4},{6,5},{7,6},{8,11},{9,8},{10,9... | collective-permute-start | bytes 1572872 | tf_op jit(solution)/shard_map/ppermute | solution.py:315
  71.0 14.6 %collective-permute-start = (bf16[128,2048]{1,0:T(8,128)(2,1)S(1)}, bf16[128,2048]{1,0:T(8,128)(2,1)S(1)}, u32[]{:S(2)}, u32[]{:S(2)}) collective-permute-start(bf16[128,2048]{1,0:T(8,128)(2,1)S(1)} %bitcast.26), channel_id=1, source_target_pairs={{0,1},{1,2},{2,3},{3,0},{4,5},{5,6},{6,7},{7,4},{8,9},{9,10},{10,1... | collective-permute-start | bytes 1572872 | tf_op jit(solution)/shard_map/ppermute | solution.py:314
  80.1 22.6 %copy-start.2 = (bf16[128,2048]{1,0:T(8,128)(2,1)}, bf16[128,2048]{1,0:T(8,128)(2,1)S(1)}, u32[]{:S(2)}) copy-start(bf16[128,2048]{1,0:T(8,128)(2,1)S(1)} %collective-permute-done.1.refs_2_.right) | copy-start | bytes 1572868
  80.2 9.1 %collective-permute-start.5 = (bf16[64,2048]{1,0:T(8,128)(2,1)S(1)}, bf16[64,2048]{1,0:T(8,128)(2,1)S(1)}, u32[]{:S(2)}, u32[]{:S(2)}) collective-permute-start(bf16[64,2048]{1,0:T(8,128)(2,1)S(1)} %slice.37), channel_id=1, source_target_pairs={{0,3},{1,0},{2,1},{3,2},{4,7},{5,4},{6,5},{7,6},{8,11},{9,8},{10,9... | collective-permute-start | bytes 786440 | tf_op jit(solution)/shard_map/ppermute | solution.py:317
  85.6 17.1 %copy-start.3 = (bf16[128,2048]{1,0:T(8,128)(2,1)}, bf16[128,2048]{1,0:T(8,128)(2,1)S(1)}, u32[]{:S(2)}) copy-start(bf16[128,2048]{1,0:T(8,128)(2,1)S(1)} %collective-permute-done.refs_1_.left) | copy-start | bytes 1572868
  85.6 9.5 %collective-permute-start.4 = (bf16[64,2048]{1,0:T(8,128)(2,1)S(1)}, bf16[64,2048]{1,0:T(8,128)(2,1)S(1)}, u32[]{:S(2)}, u32[]{:S(2)}) collective-permute-start(bf16[64,2048]{1,0:T(8,128)(2,1)S(1)} %slice.36), channel_id=1, source_target_pairs={{0,1},{1,2},{2,3},{3,0},{4,5},{5,6},{6,7},{7,4},{8,9},{9,10},{10,1... | collective-permute-start | bytes 786440 | tf_op jit(solution)/shard_map/ppermute | solution.py:316
  89.3 5.8 %copy-start.4 = (bf16[64,2048]{1,0:T(8,128)(2,1)}, bf16[64,2048]{1,0:T(8,128)(2,1)S(1)}, u32[]{:S(2)}) copy-start(bf16[64,2048]{1,0:T(8,128)(2,1)S(1)} %collective-permute-done.5.refs_1_.far_b) | copy-start | bytes 786436
  95.1 0.7 copy-start.5
  100.0 11.7 %copy-start.10 = (f32[64,384]{1,0:T(8,128)S(1)}, f32[64,384]{1,0:T(8,128)}, u32[]{:S(2)}) copy-start(f32[64,384]{1,0:T(8,128)} %get-tuple-element.13) | copy-start | bytes 294916
  100.0 11.6 %collective-permute-start.6 = (bf16[64,384]{1,0:T(8,128)(2,1)}, bf16[64,384]{1,0:T(8,128)(2,1)S(1)}, u32[]{:S(2)}, u32[]{:S(2)}) collective-permute-start(bf16[64,384]{1,0:T(8,128)(2,1)} %get-tuple-element.14), channel_id=1, source_target_pairs={{0,4},{4,0},{8,12},{12,8},{16,20},{20,16},{24,28},{28,24},{32,36},... | collective-permute-start | bytes 147464 | tf_op jit(solution)/shard_map/ppermute | solution.py:323
  108.4 8.8 %collective-permute-start.3 = (bf16[192,384]{1,0:T(8,128)(2,1)}, bf16[192,384]{1,0:T(8,128)(2,1)S(1)}, u32[]{:S(2)}, u32[]{:S(2)}) collective-permute-start(bf16[192,384]{1,0:T(8,128)(2,1)} %get-tuple-element.12), channel_id=1, source_target_pairs={{0,4},{4,0},{8,12},{12,8},{16,20},{20,16},{24,28},{28,24},{32,36},... | collective-permute-start | bytes 442376 | tf_op jit(solution)/shard_map/ppermute | solution.py:323
  118.3 2.5 %copy-start.6 = (bf16[256,384]{1,0:T(8,128)(2,1)}, bf16[256,384]{1,0:T(8,128)(2,1)S(1)}, u32[]{:S(2)}) copy-start(bf16[256,384]{1,0:T(8,128)(2,1)S(1)} %pad_maximum_fusion.mine.value) | copy-start | bytes 589828
  118.3 7.6 %collective-permute-start.7 = (bf16[256,384]{1,0:T(8,128)(2,1)S(1)}, bf16[256,384]{1,0:T(8,128)(2,1)S(1)}, u32[]{:S(2)}, u32[]{:S(2)}) collective-permute-start(bf16[256,384]{1,0:T(8,128)(2,1)S(1)} %pad_maximum_fusion.mine.value), channel_id=1, source_target_pairs={{0,4},{4,0},{8,12},{12,8},{16,20},{20,16},{24,28},{28,24},{32,36},... | collective-permute-start | bytes 589832 | tf_op jit(solution)/shard_map/ppermute | solution.py:326
  125.9 0.7 copy-start.8
  131.2 7.0 %copy-start = (bf16[2,4,512,384]{3,2,1,0:T(8,128)(2,1)S(1)}, bf16[2,4,512,384]{3,2,1,0:T(8,128)(2,1)}, u32[]{:S(2)}) copy-start(bf16[2,4,512,384]{3,2,1,0:T(8,128)(2,1)} %shard_map.97) | copy-start | bytes 9437188
  132.9 5.3 %collective-permute-start.8 = (bf16[4,512,384]{2,1,0:T(8,128)(2,1)S(1)}, bf16[4,512,384]{2,1,0:T(8,128)(2,1)S(1)}, u32[]{:S(2)}, u32[]{:S(2)}) collective-permute-start(bf16[4,512,384]{2,1,0:T(8,128)(2,1)S(1)} %slice_bitcast_fusion), channel_id=1, source_target_pairs={{0,64},{64,0},{1,65},{65,1},{2,66},{66,2},{3,67},{67,3},{4,68},{68... | collective-permute-start | bytes 4718600 | tf_op jit(solution)/shard_map/ppermute | solution.py:330
  164.0 26.5 %all-to-all-start.2 = ((bf16[16,4,2048]{2,1,0:T(4,128)(2,1)}), bf16[16,4,2048]{2,1,0:T(4,128)(2,1)S(1)}, u32[]{:S(2)}, u32[]{:S(2)}) async-start(bf16[16,4,2048]{2,1,0:T(4,128)(2,1)} %reshape.22), calls=%async_computation.2 | async-start | bytes 524288 | tf_op jit(solution)/shard_map/all_to_all | solution.py:340
  172.5 22.0 %collective-permute-start.9 = (bf16[512,384]{1,0:T(8,128)(2,1)}, bf16[512,384]{1,0:T(8,128)(2,1)S(1)}, u32[]{:S(2)}, u32[]{:S(2)}) collective-permute-start(bf16[512,384]{1,0:T(8,128)(2,1)} %reduce-scatter.2.cloned.1.call-done), channel_id=1, source_target_pairs={{0,0},{4,64},{8,8},{12,72},{16,16},{20,80},{24,24},{28,88},{32,32}... | collective-permute-start | bytes 1179656 | tf_op jit(solution)/shard_map/ppermute | solution.py:335
  190.4 0.7 copy-start.7
Sparse Core Ops, SparseCore 0:
  14.8 45.7 all-gather.1
  140.0 27.4 reduce-scatter.1

commit v6 on v5

--- a/solution.py
+++ b/solution.py
@@ -248,12 +248,13 @@
     )(place, mine, other, weights)
 
 
-def grads_kernel(place, value, own, left, right, far_a, far_b, *refs):
+def grads_kernel(kept, place, mine, other, own, left, right, far_a, far_b, *refs):
     out, inner = refs[-2:]
 
     @pl.when(pl.program_id(0) == 0)
     def _():
-        both = value[...].astype(F32)
+        is_mine = place[2] == (0 if kept else 1)
+        both = jnp.where(is_mine, mine[...].astype(F32), other[...].astype(F32))
         low = iota((ROWS // 2, 2 * HID), 0) % 8 < 4
         pre = both[:, : 2 * HID]
         hid = both[:, 2 * HID :]
@@ -270,30 +271,28 @@
     rows = jnp.concatenate([own[...], left[...], right[...], far_a[...], far_b[...]], axis=0)
     total = lax.dot_general(
         rows, inner[...], (((0,), (0,)), ((), ())), preferred_element_type=F32
-    ).astype(BF16)
+    )
     for k in range(WIDE // CUT):
-        out[0, k] = total[k * CUT : (k + 1) * CUT]
-
-
-def grads(place, turn, value, blocks, so_far):
-    hold = [pl.BlockSpec(memory_space=pl.ANY)] * len(so_far)
-
-    def at(i, place):
-        slot = place[2]
-        return (slot if turn == 0 else 1 - slot), i, 0, 0
-
-    return pl.pallas_call(
-        grads_kernel,
+        part = total[k * CUT : (k + 1) * CUT]
+        if kept:
+            part = part + refs[0][k].astype(F32)
+        out[k] = part.astype(BF16)
+
+
+def grads(place, mine, other, blocks, received):
+    dims = (ROWS // 2, 3 * HID)
+    part = pl.BlockSpec((WIDE // CUT, CUT, 3 * HID), lambda i, *_: (i, 0, 0))
+    return pl.pallas_call(
+        functools.partial(grads_kernel, len(received)),
         grid_spec=pltpu.PrefetchScalarGridSpec(
             num_scalar_prefetch=1,
             grid=(HALF // WIDE,),
-            in_specs=[whole((ROWS // 2, 3 * HID)), *row_specs(), *hold],
-            out_specs=pl.BlockSpec((1, WIDE // CUT, CUT, 3 * HID), at),
+            in_specs=[whole(dims), whole(dims), *row_specs(), *[part for _ in received]],
+            out_specs=part,
             scratch_shapes=[pltpu.VMEM((ROWS, 3 * HID), BF16)],
         ),
-        out_shape=shape((2, HALF // CUT, CUT, 3 * HID), BF16),
-        input_output_aliases={2 + len(blocks): 0} if so_far else {},
-    )(place, value, *blocks, *so_far)
+        out_shape=shape((HALF // CUT, CUT, 3 * HID), BF16),
+    )(place, mine, other, *blocks, *received)
 
 
 def work(latent, dout, routes, gate_w, norm_gain, w_gate_up, w_down):
@@ -325,12 +324,10 @@
     inner = gates(jnp.concatenate(totals, axis=0))
     outer = lax.ppermute(inner, "z", FLIP)
 
-    grad = grads(place, 0, inner, blocks, ())
-    grad = grads(place, 1, outer, blocks, (grad,))
-    partner = lax.ppermute(grad[1], "c", [(0, 1), (1, 0)])
+    received = lax.ppermute(grads(place, inner, outer, blocks, ()), "c", [(0, 1), (1, 0)])
     part = back(place, inner, outer, weights)
     part = lax.all_to_all(part, "x", 0, 0, tiled=True)
-    grad = (grad[0].astype(F32) + partner.astype(F32)).astype(BF16).reshape(HALF, 3 * HID)
+    grad = grads(place, inner, outer, blocks, (received,)).reshape(HALF, 3 * HID)
     grad = lax.psum_scatter(grad, "y", scatter_dimension=0, tiled=True)
     grad = lax.ppermute(grad, ("c", "z"), SWAP)
     grad_gu = grad[:, : 2 * HID][None]

time: 204 us -> 207 us (1.015)
  waiting for transfers between devices: 39.9 us -> 44.7 us
    ppermute x1, waiting for transfers between devices: 0.45 us -> 5.03 us  [work(): outer = lax.ppermute(inner, 'z', FLIP)]
  transfers between devices with their start and end apart: 13 -> 13, of which waited for: 8 -> 8; matrix products, arithmetic and copies ran while one was open for 1% -> 1% of each run, Pallas kernels for 9% -> 6%
where the time goes in v6:
time: 207 us; the launch traced here: 206 us
  blocking collectives  70.9 us (34%)
  waiting for transfers between devices  44.7 us (22%)
  starting transfers between devices  35.5 us (17%)
  Pallas kernels  31.7 us (15%)
  between operations  14.2 us (7%)
  local copies, waits for them, and re-layouts  6.45 us (3%)
    all_to_all x1, blocking collectives, work(): got = lax.all_to_all(send, 'z', 0, 0, tiled=True)  51.7 us
    all_to_all x1, blocking collectives, work(): part = lax.all_to_all(part, 'x', 0, 0, tiled=True)  19.2 us
    all_to_all x1, waiting for transfers between devices, work(): home = lax.all_to_all(summed.reshape(Z, CAP, HALF), 'z', 0, 0, tiled=True)  16.3 us
    pallas_call x2, Pallas kernels, mix(): pl.pallas_call(functools.partial(mix_kernel, len(blocks)), grid_spec=pltp...  9.84 us
    pallas_call x2, Pallas kernels, grads(): pl.pallas_call(functools.partial(grads_kernel, len(received)), grid_spec=...  9.59 us
    all_to_all x1, starting transfers between devices, work(): home = lax.all_to_all(summed.reshape(Z, CAP, HALF), 'z', 0, 0, tiled=True)  8.05 us
    ppermute x1, waiting for transfers between devices, work(): right = lax.ppermute(own, 'x', MINUS)  7.15 us
    ppermute x2, starting transfers between devices, work(): got = lax.ppermute(other, 'z', FLIP)  5.96 us
  transfers between devices with their start and end apart: 13, of which 8 were waited for; matrix products, arithmetic and copies ran while one was open for 1% of the time, Pallas kernels for 6%

profile of v6, /device:TPU:24, one launch (start us, length us, event | category | flops | bytes accessed | tf_op | source)
XLA Modules:
  0.0 205.6 jit_solution(3821020965841417160)
XLA Ops:
  7.2 0.0 all-gather.2.cloned.1.call-start
  7.2 3.2 %send_rows.1 = (bf16[16,8,2048]{2,1,0:T(8,128)(2,1)}, bf16[512,384]{1,0:T(8,128)(2,1)}) custom-call(s32[2,128]{1,0:T(2,128)} %bitcast.26, f32[2,128]{1,0:T(2,128)} %bitcast.28, bf16[128,4096]{1,0:T(8,128)(2,1)} %latent.3, bf16[128,4096]{1,0:T(8,128)(2,1)} %dout.1, f32[1,4096]{1,0:T(1,128)} %bitcast.24, bf16[1,512,256]{2,1,0:T(8,128)(2,1)} %gate_up.1, ...), custom_call_target="tpu_custom_call" | custom-call | tf_op jit(solution)/shard_map/send_rows/pallas_call | solution.py:84
  10.4 1.6 collective-permute-start.2
  12.1 0.8 copy-done.9
  12.8 1.8 hold.1
  14.6 0.0 all-gather.2.cloned.1.call-update
  14.6 0.0 reduce-scatter.2.cloned.1.call-start
  14.7 51.7 %all_to_all.15 = bf16[16,8,2048]{2,1,0:T(8,128)(2,1)S(1)} all-to-all(bf16[16,8,2048]{2,1,0:T(8,128)(2,1)} %get-tuple-element.9), channel_id=1, replica_groups=mesh['y'=4,'c'=2,'z'=16,'x'=4] {'z'}, dimensions={0} | all-to-all | bytes 1048576 | tf_op jit(solution)/shard_map/all_to_all | solution.py:307
  66.4 4.7 %collective-permute-start.1 = (bf16[128,2048]{1,0:T(8,128)(2,1)S(1)}, bf16[128,2048]{1,0:T(8,128)(2,1)S(1)}, u32[]{:S(2)}, u32[]{:S(2)}) collective-permute-start(bf16[128,2048]{1,0:T(8,128)(2,1)S(1)} %bitcast.18), channel_id=1, source_target_pairs={{0,3},{1,0},{2,1},{3,2},{4,7},{5,4},{6,5},{7,6},{8,11},{9,8},{10,9... | collective-permute-start | bytes 1572872 | tf_op jit(solution)/shard_map/ppermute | solution.py:314
  71.0 1.9 collective-permute-start
  73.0 7.2 %collective-permute-done.1.refs_2_.right = bf16[128,2048]{1,0:T(8,128)(2,1)S(1)} collective-permute-done((bf16[128,2048]{1,0:T(8,128)(2,1)S(1)}, bf16[128,2048]{1,0:T(8,128)(2,1)S(1)}, u32[]{:S(2)}, u32[]{:S(2)}) %collective-permute-start.1) | collective-permute-done | bytes 524320 | tf_op jit(solution)/shard_map/ppermute | solution.py:314
  80.2 5.2 %collective-permute-start.5 = (bf16[64,2048]{1,0:T(8,128)(2,1)S(1)}, bf16[64,2048]{1,0:T(8,128)(2,1)S(1)}, u32[]{:S(2)}, u32[]{:S(2)}) collective-permute-start(bf16[64,2048]{1,0:T(8,128)(2,1)S(1)} %slice.29), channel_id=1, source_target_pairs={{0,3},{1,0},{2,1},{3,2},{4,7},{5,4},{6,5},{7,6},{8,11},{9,8},{10,9... | collective-permute-start | bytes 786440 | tf_op jit(solution)/shard_map/ppermute | solution.py:316
  85.4 0.2 collective-permute-done.refs_1_.left
  85.6 1.9 collective-permute-start.4
  87.6 0.7 pad_add_fusion.place
  88.2 1.0 collective-permute-done.5.refs_1_.far_b
  89.3 5.8 %collective-permute-done.4.refs_0_.far_a = bf16[64,2048]{1,0:T(8,128)(2,1)S(1)} collective-permute-done((bf16[64,2048]{1,0:T(8,128)(2,1)S(1)}, bf16[64,2048]{1,0:T(8,128)(2,1)S(1)}, u32[]{:S(2)}, u32[]{:S(2)}) %collective-permute-start.4) | collective-permute-done | bytes 262176 | tf_op jit(solution)/shard_map/ppermute | solution.py:315
  95.1 0.7 copy-done.5
  95.8 4.2 %shard_map.95 = (f32[64,384]{1,0:T(8,128)}, bf16[64,384]{1,0:T(8,128)(2,1)}) custom-call(s32[3]{0:T(128)} %pad_add_fusion.place, bf16[64,2048]{1,0:T(8,128)(2,1)} %copy-done.5, bf16[64,2048]{1,0:T(8,128)(2,1)} %copy-done.4, bf16[2,2048,384]{2,1,0:T(8,128)(2,1)} %bitcast.15), custom_call_target="tpu_custom_call" | custom-call | tf_op jit(solution)/shard_map/pallas_call | solution.py:189
  100.0 0.0 copy-start.10
  100.0 2.7 %collective-permute-start.6 = (bf16[64,384]{1,0:T(8,128)(2,1)}, bf16[64,384]{1,0:T(8,128)(2,1)S(1)}, u32[]{:S(2)}, u32[]{:S(2)}) collective-permute-start(bf16[64,384]{1,0:T(8,128)(2,1)} %get-tuple-element.14), channel_id=1, source_target_pairs={{0,4},{4,0},{8,12},{12,8},{16,20},{20,16},{24,28},{28,24},{32,36},... | collective-permute-start | bytes 147464 | tf_op jit(solution)/shard_map/ppermute | solution.py:322
  102.8 5.6 %shard_map.94 = (f32[192,384]{1,0:T(8,128)}, bf16[192,384]{1,0:T(8,128)(2,1)}) custom-call(s32[3]{0:T(128)} %pad_add_fusion.place, bf16[128,2048]{1,0:T(8,128)(2,1)} %bitcast.20, bf16[128,2048]{1,0:T(8,128)(2,1)} %copy-done.2, bf16[128,2048]{1,0:T(8,128)(2,1)} %copy-done.1, bf16[2,2048,384]{2,1,0:T(8,128)(2,1)} %bitcast.16), custom_call_target="tpu_custom_call" | custom-call | tf_op jit(solution)/shard_map/pallas_call | solution.py:189
  108.4 3.2 %collective-permute-start.3 = (bf16[192,384]{1,0:T(8,128)(2,1)}, bf16[192,384]{1,0:T(8,128)(2,1)S(1)}, u32[]{:S(2)}, u32[]{:S(2)}) collective-permute-start(bf16[192,384]{1,0:T(8,128)(2,1)} %get-tuple-element.12), channel_id=1, source_target_pairs={{0,4},{4,0},{8,12},{12,8},{16,20},{20,16},{24,28},{28,24},{32,36},... | collective-permute-start | bytes 442376 | tf_op jit(solution)/shard_map/ppermute | solution.py:322
  111.7 5.5 %collective-permute-done.3 = bf16[192,384]{1,0:T(8,128)(2,1)S(1)} collective-permute-done((bf16[192,384]{1,0:T(8,128)(2,1)}, bf16[192,384]{1,0:T(8,128)(2,1)S(1)}, u32[]{:S(2)}, u32[]{:S(2)}) %collective-permute-start.3) | collective-permute-done | bytes 147488 | tf_op jit(solution)/shard_map/ppermute | solution.py:322
  117.2 1.0 convert_add_fusion
  118.2 0.1 multiply_convert_fusion.2
  118.2 0.1 multiply_convert_fusion.1
  118.4 2.5 %collective-permute-start.7 = (bf16[256,384]{1,0:T(8,128)(2,1)S(1)}, bf16[256,384]{1,0:T(8,128)(2,1)S(1)}, u32[]{:S(2)}, u32[]{:S(2)}) collective-permute-start(bf16[256,384]{1,0:T(8,128)(2,1)S(1)} %pad_maximum_fusion.mine), channel_id=1, source_target_pairs={{0,4},{4,0},{8,12},{12,8},{16,20},{20,16},{24,28},{28,24},{32,36},... | collective-permute-start | bytes 589832 | tf_op jit(solution)/shard_map/ppermute | solution.py:325
  120.9 5.0 %collective-permute-done.7.other = bf16[256,384]{1,0:T(8,128)(2,1)S(1)} collective-permute-done((bf16[256,384]{1,0:T(8,128)(2,1)S(1)}, bf16[256,384]{1,0:T(8,128)(2,1)S(1)}, u32[]{:S(2)}, u32[]{:S(2)}) %collective-permute-start.7) | collective-permute-done | bytes 196640 | tf_op jit(solution)/shard_map/ppermute | solution.py:325
  125.9 0.7 copy-done.6
  126.6 4.7 %shard_map.96 = bf16[4,512,384]{2,1,0:T(8,128)(2,1)} custom-call(s32[3]{0:T(128)} %pad_add_fusion.place, bf16[256,384]{1,0:T(8,128)(2,1)} %copy-done.3, bf16[256,384]{1,0:T(8,128)(2,1)} %copy-done.6, bf16[128,2048]{1,0:T(8,128)(2,1)} %bitcast.21, bf16[128,2048]{1,0:T(8,128)(2,1)} %copy-done.2, bf16[128,2048]{1,0:T(8,128)(2,1)} %copy-done.1, ...), custom_call_target="tpu_custom_call" | custom-call | tf_op jit(solution)/shard_map/pallas_call | solution.py:285
  131.3 1.9 collective-permute-start.8
  133.2 3.6 %collective-permute-done.8.refs_0_ = bf16[4,512,384]{2,1,0:T(8,128)(2,1)S(1)} collective-permute-done((bf16[4,512,384]{2,1,0:T(8,128)(2,1)}, bf16[4,512,384]{2,1,0:T(8,128)(2,1)S(1)}, u32[]{:S(2)}, u32[]{:S(2)}) %collective-permute-start.8) | collective-permute-done | bytes 1572896 | tf_op jit(solution)/shard_map/ppermute | solution.py:327
  136.8 1.2 copy-done.7
  138.0 4.9 %shard_map.97 = bf16[4,512,384]{2,1,0:T(8,128)(2,1)} custom-call(s32[3]{0:T(128)} %pad_add_fusion.place, bf16[256,384]{1,0:T(8,128)(2,1)} %copy-done.3, bf16[256,384]{1,0:T(8,128)(2,1)} %copy-done.6, bf16[128,2048]{1,0:T(8,128)(2,1)} %bitcast.22, bf16[128,2048]{1,0:T(8,128)(2,1)} %copy-done.2, bf16[128,2048]{1,0:T(8,128)(2,1)} %copy-done.1, ...), custom_call_target="tpu_custom_call" | custom-call | tf_op jit(solution)/shard_map/pallas_call | solution.py:285
  142.9 0.0 reduce-scatter.2.cloned.1.call-update
  143.0 4.0 %back.1 = bf16[4,64,2048]{2,1,0:T(8,128)(2,1)} custom-call(s32[3]{0:T(128)} %pad_add_fusion.place, bf16[256,384]{1,0:T(8,128)(2,1)} %copy-done.3, bf16[256,384]{1,0:T(8,128)(2,1)} %copy-done.6, bf16[2,2048,384]{2,1,0:T(8,128)(2,1)} %bitcast.17), custom_call_target="tpu_custom_call" | custom-call | tf_op jit(solution)/shard_map/back/pallas_call | solution.py:237
  146.9 19.2 %all_to_all.16 = bf16[4,64,2048]{2,1,0:T(8,128)(2,1)S(1)} all-to-all(bf16[4,64,2048]{2,1,0:T(8,128)(2,1)} %back.1), channel_id=1, replica_groups=mesh['y'=4,'c'=2,'z'=16,'x'=4] {'x'}, dimensions={0} | all-to-all | bytes 2097152 | tf_op jit(solution)/shard_map/all_to_all | solution.py:329
  166.1 0.2 reduce_sum.12
  166.3 0.8 reshape.20
  167.1 8.0 %all-to-all-start.2 = ((bf16[16,4,2048]{2,1,0:T(4,128)(2,1)}), bf16[16,4,2048]{2,1,0:T(4,128)(2,1)S(1)}, u32[]{:S(2)}, u32[]{:S(2)}) async-start(bf16[16,4,2048]{2,1,0:T(4,128)(2,1)} %reshape.20), calls=%async_computation.2 | async-start | bytes 524288 | tf_op jit(solution)/shard_map/all_to_all | solution.py:337
  175.2 0.0 reduce-scatter.2.cloned.1.call-done
  175.2 1.7 collective-permute-start.9
  176.8 16.3 %all-to-all-done.2.home = bf16[16,4,2048]{2,1,0:T(4,128)(2,1)S(1)} async-done(((bf16[16,4,2048]{2,1,0:T(4,128)(2,1)}), bf16[16,4,2048]{2,1,0:T(4,128)(2,1)S(1)}, u32[]{:S(2)}, u32[]{:S(2)}) %all-to-all-start.2) | async-done | bytes 262176 | tf_op jit(solution)/shard_map/all_to_all | solution.py:337
  193.2 0.7 copy-done.8
  193.9 3.3 %home_rows.1 = bf16[128,4096]{1,0:T(8,128)(2,1)} custom-call(s32[2,128]{1,0:T(2,128)} %bitcast.27, bf16[128,4096]{1,0:T(8,128)(2,1)} %latent.3, f32[1,4096]{1,0:T(1,128)} %bitcast.25, bf16[16,4,2048]{2,1,0:T(4,128)(2,1)} %copy-done.8), custom_call_target="tpu_custom_call" | custom-call | tf_op jit(solution)/shard_map/home_rows/pallas_call | solution.py:120
  197.2 0.8 copy.11
  198.0 0.7 slice_bitcast_fusion
  (25 shorter events, 0.1 us)
Async XLA Ops:
  7.2 87.9 %all-gather.2.cloned.1.call-start = ((), (), s32[]{:S(2)}) async-start(), calls=%async_computation.4 | async-start | bytes 3538944 | tf_op jit(solution)/shard_map/all_gather | solution.py:308
  10.4 1.6 collective-permute-start.2
  12.1 0.8 copy-start.9
  14.6 160.5 %reduce-scatter.2.cloned.1.call-start = ((), (), s32[]{:S(2)}) async-start(), calls=%async_computation.5 | async-start | bytes 1966080 | tf_op jit(solution)/shard_map/reduce_scatter | solution.py:331
  66.4 33.6 %copy-start = (bf16[16,8,2048]{2,1,0:T(8,128)(2,1)}, bf16[16,8,2048]{2,1,0:T(8,128)(2,1)S(1)}, u32[]{:S(2)}) copy-start(bf16[16,8,2048]{2,1,0:T(8,128)(2,1)S(1)} %all_to_all.15) | copy-start | bytes 1572868
  66.4 13.7 %collective-permute-start.1 = (bf16[128,2048]{1,0:T(8,128)(2,1)S(1)}, bf16[128,2048]{1,0:T(8,128)(2,1)S(1)}, u32[]{:S(2)}, u32[]{:S(2)}) collective-permute-start(bf16[128,2048]{1,0:T(8,128)(2,1)S(1)} %bitcast.18), channel_id=1, source_target_pairs={{0,3},{1,0},{2,1},{3,2},{4,7},{5,4},{6,5},{7,6},{8,11},{9,8},{10,9... | collective-permute-start | bytes 1572872 | tf_op jit(solution)/shard_map/ppermute | solution.py:314
  71.0 14.6 %collective-permute-start = (bf16[128,2048]{1,0:T(8,128)(2,1)S(1)}, bf16[128,2048]{1,0:T(8,128)(2,1)S(1)}, u32[]{:S(2)}, u32[]{:S(2)}) collective-permute-start(bf16[128,2048]{1,0:T(8,128)(2,1)S(1)} %bitcast.19), channel_id=1, source_target_pairs={{0,1},{1,2},{2,3},{3,0},{4,5},{5,6},{6,7},{7,4},{8,9},{9,10},{10,1... | collective-permute-start | bytes 1572872 | tf_op jit(solution)/shard_map/ppermute | solution.py:313
  80.1 19.9 %copy-start.1 = (bf16[128,2048]{1,0:T(8,128)(2,1)}, bf16[128,2048]{1,0:T(8,128)(2,1)S(1)}, u32[]{:S(2)}) copy-start(bf16[128,2048]{1,0:T(8,128)(2,1)S(1)} %collective-permute-done.1.refs_2_.right) | copy-start | bytes 1572868
  80.2 9.1 %collective-permute-start.5 = (bf16[64,2048]{1,0:T(8,128)(2,1)S(1)}, bf16[64,2048]{1,0:T(8,128)(2,1)S(1)}, u32[]{:S(2)}, u32[]{:S(2)}) collective-permute-start(bf16[64,2048]{1,0:T(8,128)(2,1)S(1)} %slice.29), channel_id=1, source_target_pairs={{0,3},{1,0},{2,1},{3,2},{4,7},{5,4},{6,5},{7,6},{8,11},{9,8},{10,9... | collective-permute-start | bytes 786440 | tf_op jit(solution)/shard_map/ppermute | solution.py:316
  85.6 14.4 %copy-start.2 = (bf16[128,2048]{1,0:T(8,128)(2,1)}, bf16[128,2048]{1,0:T(8,128)(2,1)S(1)}, u32[]{:S(2)}) copy-start(bf16[128,2048]{1,0:T(8,128)(2,1)S(1)} %collective-permute-done.refs_1_.left) | copy-start | bytes 1572868
  85.6 9.5 %collective-permute-start.4 = (bf16[64,2048]{1,0:T(8,128)(2,1)S(1)}, bf16[64,2048]{1,0:T(8,128)(2,1)S(1)}, u32[]{:S(2)}, u32[]{:S(2)}) collective-permute-start(bf16[64,2048]{1,0:T(8,128)(2,1)S(1)} %slice.28), channel_id=1, source_target_pairs={{0,1},{1,2},{2,3},{3,0},{4,5},{5,6},{6,7},{7,4},{8,9},{9,10},{10,1... | collective-permute-start | bytes 786440 | tf_op jit(solution)/shard_map/ppermute | solution.py:315
  89.3 5.8 %copy-start.4 = (bf16[64,2048]{1,0:T(8,128)(2,1)}, bf16[64,2048]{1,0:T(8,128)(2,1)S(1)}, u32[]{:S(2)}) copy-start(bf16[64,2048]{1,0:T(8,128)(2,1)S(1)} %collective-permute-done.5.refs_1_.far_b) | copy-start | bytes 786436
  95.1 0.7 copy-start.5
  100.0 11.6 %copy-start.10 = (f32[64,384]{1,0:T(8,128)S(1)}, f32[64,384]{1,0:T(8,128)}, u32[]{:S(2)}) copy-start(f32[64,384]{1,0:T(8,128)} %get-tuple-element.13) | copy-start | bytes 294916
  100.0 11.6 %collective-permute-start.6 = (bf16[64,384]{1,0:T(8,128)(2,1)}, bf16[64,384]{1,0:T(8,128)(2,1)S(1)}, u32[]{:S(2)}, u32[]{:S(2)}) collective-permute-start(bf16[64,384]{1,0:T(8,128)(2,1)} %get-tuple-element.14), channel_id=1, source_target_pairs={{0,4},{4,0},{8,12},{12,8},{16,20},{20,16},{24,28},{28,24},{32,36},... | collective-permute-start | bytes 147464 | tf_op jit(solution)/shard_map/ppermute | solution.py:322
  108.4 8.8 %collective-permute-start.3 = (bf16[192,384]{1,0:T(8,128)(2,1)}, bf16[192,384]{1,0:T(8,128)(2,1)S(1)}, u32[]{:S(2)}, u32[]{:S(2)}) collective-permute-start(bf16[192,384]{1,0:T(8,128)(2,1)} %get-tuple-element.12), channel_id=1, source_target_pairs={{0,4},{4,0},{8,12},{12,8},{16,20},{20,16},{24,28},{28,24},{32,36},... | collective-permute-start | bytes 442376 | tf_op jit(solution)/shard_map/ppermute | solution.py:322
  118.3 7.6 %copy-start.3 = (bf16[256,384]{1,0:T(8,128)(2,1)}, bf16[256,384]{1,0:T(8,128)(2,1)S(1)}, u32[]{:S(2)}) copy-start(bf16[256,384]{1,0:T(8,128)(2,1)S(1)} %pad_maximum_fusion.mine) | copy-start | bytes 589828
  118.4 7.6 %collective-permute-start.7 = (bf16[256,384]{1,0:T(8,128)(2,1)S(1)}, bf16[256,384]{1,0:T(8,128)(2,1)S(1)}, u32[]{:S(2)}, u32[]{:S(2)}) collective-permute-start(bf16[256,384]{1,0:T(8,128)(2,1)S(1)} %pad_maximum_fusion.mine), channel_id=1, source_target_pairs={{0,4},{4,0},{8,12},{12,8},{16,20},{20,16},{24,28},{28,24},{32,36},... | collective-permute-start | bytes 589832 | tf_op jit(solution)/shard_map/ppermute | solution.py:325
  125.9 0.7 copy-start.6
  131.3 5.5 %collective-permute-start.8 = (bf16[4,512,384]{2,1,0:T(8,128)(2,1)}, bf16[4,512,384]{2,1,0:T(8,128)(2,1)S(1)}, u32[]{:S(2)}, u32[]{:S(2)}) collective-permute-start(bf16[4,512,384]{2,1,0:T(8,128)(2,1)} %shard_map.96), channel_id=1, source_target_pairs={{0,64},{64,0},{1,65},{65,1},{2,66},{66,2},{3,67},{67,3},{4,68},{68... | collective-permute-start | bytes 4718600 | tf_op jit(solution)/shard_map/ppermute | solution.py:327
  136.8 1.2 copy-start.7
  167.1 26.1 %all-to-all-start.2 = ((bf16[16,4,2048]{2,1,0:T(4,128)(2,1)}), bf16[16,4,2048]{2,1,0:T(4,128)(2,1)S(1)}, u32[]{:S(2)}, u32[]{:S(2)}) async-start(bf16[16,4,2048]{2,1,0:T(4,128)(2,1)} %reshape.20), calls=%async_computation.2 | async-start | bytes 524288 | tf_op jit(solution)/shard_map/all_to_all | solution.py:337
  175.2 22.0 %collective-permute-start.9 = (bf16[512,384]{1,0:T(8,128)(2,1)}, bf16[512,384]{1,0:T(8,128)(2,1)S(1)}, u32[]{:S(2)}, u32[]{:S(2)}) collective-permute-start(bf16[512,384]{1,0:T(8,128)(2,1)} %reduce-scatter.2.cloned.1.call-done), channel_id=1, source_target_pairs={{0,0},{4,64},{8,8},{12,72},{16,16},{20,80},{24,24},{28,88},{32,32}... | collective-permute-start | bytes 1179656 | tf_op jit(solution)/shard_map/ppermute | solution.py:332
  193.2 0.7 copy-start.8
Sparse Core Ops, SparseCore 0:
  14.8 45.7 all-gather.1
  143.1 27.0 reduce-scatter.1

commit v7 on v6

--- a/solution.py
+++ b/solution.py
@@ -27,6 +27,7 @@
 FLIP = [(i, i ^ 1) for i in range(Z)]
 PLUS = [(i, (i + 1) % X) for i in range(X)]
 MINUS = [(i, (i - 1) % X) for i in range(X)]
+TURN = [(0, 1), (1, 0)]
 ORDER = (0, 3, 1, 2)
 
 
@@ -89,12 +90,25 @@
     )(*args)
 
 
-def hold_kernel(piece, out):
-    out[...] = piece[...]
-
-
-def hold(piece):
-    return pl.pallas_call(hold_kernel, out_shape=shape(piece.shape, BF16), name="hold")(piece)
+def join_kernel(place, own, left, right, far_a, far_b, out):
+    half = CUT // 2
+    for block, k, first in ((own, 0, 0), (left, 1, 0), (right, 2, 0), (far_a, 3, 0), (far_b, 3, half)):
+        at = pl.multiple_of(place[7 + k] * CUT + first, half)
+        out[pl.ds(at, block.shape[0]), :] = block[...]
+
+
+def join(place, blocks):
+    return pl.pallas_call(
+        join_kernel,
+        grid_spec=pltpu.PrefetchScalarGridSpec(
+            num_scalar_prefetch=1,
+            grid=(1,),
+            in_specs=[whole(block.shape) for block in blocks],
+            out_specs=whole((HALF, 3 * HID)),
+        ),
+        out_shape=shape((HALF, 3 * HID), BF16),
+        name="join",
+    )(place, *blocks)
 
 
 def home_kernel(routes, latent, gain, home, out, grad):
@@ -132,14 +146,14 @@
 
 
 def mix_kernel(count, place, *refs):
-    blocks, weights = refs[:count], refs[count]
+    blocks, weights = refs[:count], refs[count : count + 2]
     mine, other, total = refs[-3:]
     step = pl.program_id(0)
     rows = blocks[0][...]
     if count > 1:
         rows = jnp.concatenate([block[...] for block in blocks], axis=0)
     for g in range(2):
-        part = jnp.dot(rows, weights[g], preferred_element_type=F32)
+        part = jnp.dot(rows, weights[g][...], preferred_element_type=F32)
 
         @pl.when(step == 0)
         def _():
@@ -160,10 +174,10 @@
 
     @pl.when(step == pl.num_programs(0) - 1)
     def _():
-        pre, dh = packed(total[place[0]])
+        pre, dh = packed(total[place[2]])
         mine[:, : 2 * HID] = pre
         mine[:, 2 * HID :] = dh
-        pre, dh = packed(total[1 - place[0]])
+        pre, dh = packed(total[1 - place[2]])
         other[:, : 2 * HID] = pre.astype(BF16)
         other[:, 2 * HID :] = dh.astype(BF16)
 
@@ -175,8 +189,8 @@
     ]
 
 
-def weight_spec():
-    return pl.BlockSpec((2, WIDE, 3 * HID), lambda i, *_: (0, i, 0))
+def weight_specs():
+    return [pl.BlockSpec((WIDE, 3 * HID), lambda i, *_: (i, 0))] * 2
 
 
 def whole(dims):
@@ -193,13 +207,13 @@
             grid=(HALF // WIDE,),
             in_specs=[
                 *[pl.BlockSpec((b.shape[0], WIDE), lambda i, *_: (0, i)) for b in blocks],
-                weight_spec(),
+                *weight_specs(),
             ],
             out_specs=[whole(dims), whole(dims)],
             scratch_shapes=[pltpu.VMEM((2, rows, 3 * HID), F32)],
         ),
         out_shape=[shape(dims, F32), shape(dims, BF16)],
-    )(place, *blocks, weights)
+    )(place, *blocks, *weights)
 
 
 def gates(total):
@@ -212,16 +226,18 @@
     return jnp.concatenate([d_gate, dh * act, act * up], axis=1).astype(BF16)
 
 
-def back_kernel(place, mine, other, weights, out, inner):
+def back_kernel(place, mine, other, weights_a, weights_b, out, inner):
+    weights = weights_a, weights_b
+
     @pl.when(pl.program_id(0) == 0)
     def _():
-        inner[place[0]] = mine[...]
-        inner[1 - place[0]] = other[...]
+        inner[place[2]] = mine[...]
+        inner[1 - place[2]] = other[...]
 
     total = sum(
         lax.dot_general(
             inner[g, :, : 2 * HID],
-            weights[g, :, : 2 * HID],
+            weights[g][:, : 2 * HID],
             (((1,), (1,)), ((), ())),
             preferred_element_type=F32,
         )
@@ -239,13 +255,13 @@
         grid_spec=pltpu.PrefetchScalarGridSpec(
             num_scalar_prefetch=1,
             grid=(HALF // WIDE,),
-            in_specs=[whole(dims), whole(dims), weight_spec()],
+            in_specs=[whole(dims), whole(dims), *weight_specs()],
             out_specs=pl.BlockSpec((X, ROWS // 8, WIDE), lambda i, *_: (0, 0, i)),
             scratch_shapes=[pltpu.VMEM((2, *dims), BF16)],
         ),
         out_shape=shape((X, ROWS // 8, HALF), BF16),
         name="back",
-    )(place, mine, other, weights)
+    )(place, mine, other, *weights)
 
 
 def grads_kernel(kept, place, mine, other, own, left, right, far_a, far_b, *refs):
@@ -276,7 +292,9 @@
         part = total[k * CUT : (k + 1) * CUT]
         if kept:
             part = part + refs[0][k].astype(F32)
-        out[k] = part.astype(BF16)
+            out[place[3 + pl.program_id(0) * (WIDE // CUT) + k]] = part.astype(BF16)
+        else:
+            out[k] = part.astype(BF16)
 
 
 def grads(place, mine, other, blocks, received):
@@ -288,33 +306,54 @@
             num_scalar_prefetch=1,
             grid=(HALF // WIDE,),
             in_specs=[whole(dims), whole(dims), *row_specs(), *[part for _ in received]],
-            out_specs=part,
+            out_specs=whole((HALF // CUT, CUT, 3 * HID)) if received else part,
             scratch_shapes=[pltpu.VMEM((ROWS, 3 * HID), BF16)],
         ),
         out_shape=shape((HALF // CUT, CUT, 3 * HID), BF16),
     )(place, mine, other, *blocks, *received)
 
 
+def gathered(own, axis):
+    half = own.shape[0] // 2
+    left = lax.ppermute(own, axis, PLUS)
+    right = lax.ppermute(own, axis, MINUS)
+    far_a = lax.ppermute(left[:half], axis, PLUS)
+    far_b = lax.ppermute(right[half:], axis, MINUS)
+    return own, left, right, far_a, far_b
+
+
+def scattered(parts):
+    own, left, right, far = parts
+    half = own.shape[0] // 2
+    got_a = lax.ppermute(far[:half], "y", MINUS).astype(F32)
+    got_b = lax.ppermute(far[half:], "y", PLUS).astype(F32)
+    near_a = (left[:half].astype(F32) + got_a).astype(BF16)
+    near_b = (right[half:].astype(F32) + got_b).astype(BF16)
+    left = jnp.concatenate([near_a, left[half:]], axis=0)
+    right = jnp.concatenate([right[:half], near_b], axis=0)
+    left = lax.ppermute(left, "y", MINUS)
+    right = lax.ppermute(right, "y", PLUS)
+    return (own.astype(F32) + left.astype(F32) + right.astype(F32)).astype(BF16)
+
+
 def work(latent, dout, routes, gate_w, norm_gain, w_gate_up, w_down):
     zp = lax.axis_index("z") % 2
-    core = lax.axis_index("c")
-    place = jnp.stack([zp, lax.axis_index("x"), (zp + core) % 2]).astype(jnp.int32)
+    y = lax.axis_index("y")
+    away = (jnp.arange(Y, dtype=jnp.int32) - y) % Y
+    ring = jnp.where(away == 0, 0, jnp.where(away == 3, 1, away + 1))
+    first = [zp, lax.axis_index("x"), (zp + lax.axis_index("c")) % 2]
+    place = jnp.concatenate(
+        [jnp.stack(first), ring, jnp.stack([(y + off) % Y for off in ORDER])]
+    ).astype(jnp.int32)
     gain = norm_gain[None, :]
     routes = routes.T
 
     send, piece = send_rows(routes, gate_w.T, latent, dout, gain, w_gate_up, w_down)
     piece = lax.ppermute(piece, ("c", "z"), SWAP)
     got = lax.all_to_all(send, "z", 0, 0, tiled=True)
-    weights = lax.all_gather(hold(piece), ("c", "y"), axis=0, tiled=True)
-    weights = weights.reshape(2, HALF, 3 * HID)
-
-    own = got.reshape(ROWS // 4, HALF)
-    half = own.shape[0] // 2
-    left = lax.ppermute(own, "x", PLUS)
-    right = lax.ppermute(own, "x", MINUS)
-    far_a = lax.ppermute(left[:half], "x", PLUS)
-    far_b = lax.ppermute(right[half:], "x", MINUS)
-    blocks = own, left, right, far_a, far_b
+    joined = join(place, gathered(piece, "y"))
+    weights = joined, lax.ppermute(joined, "c", TURN)
+    blocks = gathered(got.reshape(ROWS // 4, HALF), "x")
 
     totals = []
     for some in (blocks[:3], blocks[3:]):
@@ -324,11 +363,10 @@
     inner = gates(jnp.concatenate(totals, axis=0))
     outer = lax.ppermute(inner, "z", FLIP)
 
-    received = lax.ppermute(grads(place, inner, outer, blocks, ()), "c", [(0, 1), (1, 0)])
     part = back(place, inner, outer, weights)
     part = lax.all_to_all(part, "x", 0, 0, tiled=True)
-    grad = grads(place, inner, outer, blocks, (received,)).reshape(HALF, 3 * HID)
-    grad = lax.psum_scatter(grad, "y", scatter_dimension=0, tiled=True)
+    received = lax.ppermute(grads(place, inner, outer, blocks, ()), "c", TURN)
+    grad = scattered(grads(place, inner, outer, blocks, (received,)))
     grad = lax.ppermute(grad, ("c", "z"), SWAP)
     grad_gu = grad[:, : 2 * HID][None]
     grad_d = grad[:, 2 * HID :].T[None]

time: 207 us -> 214 us (1.034)
  the two profiles are of different devices: /device:TPU:24 before, /device:TPU:32 now
where the time goes in v7:
time: 214 us; the launch traced here: 213 us
  starting transfers between devices  92.6 us (43%)
  waiting for transfers between devices  71.3 us (33%)
  Pallas kernels  33.5 us (16%)
  local copies, waits for them, and re-layouts  10.9 us (5%)
  other arithmetic  3.48 us (2%)
    ppermute x1, waiting for transfers between devices, work(): piece = lax.ppermute(piece, ('c', 'z'), SWAP)  25 us
    all_to_all x1, starting transfers between devices, work(): got = lax.all_to_all(send, 'z', 0, 0, tiled=True)  15.2 us
    all_to_all x1, waiting for transfers between devices, work(): home = lax.all_to_all(summed.reshape(Z, CAP, HALF), 'z', 0, 0, tiled=True)  14.7 us
    all_to_all x1, starting transfers between devices, work(): home = lax.all_to_all(summed.reshape(Z, CAP, HALF), 'z', 0, 0, tiled=True)  14.1 us
    ppermute x2, waiting for transfers between devices, gathered(): right = lax.ppermute(own, axis, MINUS)  13.2 us
    ppermute x2, starting transfers between devices, gathered(): far_b = lax.ppermute(right[half:], axis, MINUS)  11.2 us
    pallas_call x2, Pallas kernels, grads(): pl.pallas_call(functools.partial(grads_kernel, len(received)), grid_spec=...  9.86 us
    pallas_call x2, Pallas kernels, mix(): pl.pallas_call(functools.partial(mix_kernel, len(blocks)), grid_spec=pltp...  9.77 us
  transfers between devices with their start and end apart: 22, of which 11 were waited for; matrix products, arithmetic and copies ran while one was open for 3% of the time, Pallas kernels for 12%

profile of v7, /device:TPU:32, one launch (start us, length us, event | category | flops | bytes accessed | tf_op | source)
XLA Modules:
  0.0 212.9 jit_solution(14750114997012374706)
XLA Ops:
  0.6 3.2 %send_rows.1 = (bf16[16,8,2048]{2,1,0:T(8,128)(2,1)}, bf16[512,384]{1,0:T(8,128)(2,1)}) custom-call(s32[2,128]{1,0:T(2,128)} %bitcast.47, f32[2,128]{1,0:T(2,128)} %bitcast.49, bf16[128,4096]{1,0:T(8,128)(2,1)} %latent.3, bf16[128,4096]{1,0:T(8,128)(2,1)} %dout.1, f32[1,4096]{1,0:T(1,128)} %bitcast.45, bf16[1,512,256]{2,1,0:T(8,128)(2,1)} %gate_up.1, ...), custom_call_target="tpu_custom_call" | custom-call | tf_op jit(solution)/shard_map/send_rows/pallas_call | solution.py:85
  3.9 15.2 %all-to-all-start = ((bf16[16,8,2048]{2,1,0:T(8,128)(2,1)}), bf16[16,8,2048]{2,1,0:T(8,128)(2,1)S(1)}, u32[]{:S(2)}, u32[]{:S(2)}) async-start(bf16[16,8,2048]{2,1,0:T(8,128)(2,1)} %get-tuple-element.9), calls=%async_computation | async-start | bytes 1048576 | tf_op jit(solution)/shard_map/all_to_all | solution.py:353
  19.1 1.9 collective-permute-start.2
  21.0 25.0 %collective-permute-done.2.own = bf16[512,384]{1,0:T(8,128)(2,1)S(1)} collective-permute-done((bf16[512,384]{1,0:T(8,128)(2,1)}, bf16[512,384]{1,0:T(8,128)(2,1)S(1)}, u32[]{:S(2)}, u32[]{:S(2)}) %collective-permute-start.2) | collective-permute-done | bytes 393248 | tf_op jit(solution)/shard_map/ppermute | solution.py:352
  46.0 4.9 %collective-permute-start.4 = (bf16[512,384]{1,0:T(8,128)(2,1)S(1)}, bf16[512,384]{1,0:T(8,128)(2,1)S(1)}, u32[]{:S(2)}, u32[]{:S(2)}) collective-permute-start(bf16[512,384]{1,0:T(8,128)(2,1)S(1)} %collective-permute-done.2.own), channel_id=1, source_target_pairs={{0,384},{128,0},{256,128},{384,256},{1,385},{129,1},{257,129},{385... | collective-permute-start | bytes 1179656 | tf_op jit(solution)/shard_map/ppermute | solution.py:319
  50.9 1.9 collective-permute-start.3
  52.9 3.3 %collective-permute-done.4.right = bf16[512,384]{1,0:T(8,128)(2,1)S(1)} collective-permute-done((bf16[512,384]{1,0:T(8,128)(2,1)S(1)}, bf16[512,384]{1,0:T(8,128)(2,1)S(1)}, u32[]{:S(2)}, u32[]{:S(2)}) %collective-permute-start.4) | collective-permute-done | bytes 393248 | tf_op jit(solution)/shard_map/ppermute | solution.py:319
  56.2 5.6 %collective-permute-start.6 = (bf16[256,384]{1,0:T(8,128)(2,1)S(1)}, bf16[256,384]{1,0:T(8,128)(2,1)S(1)}, u32[]{:S(2)}, u32[]{:S(2)}) collective-permute-start(bf16[256,384]{1,0:T(8,128)(2,1)S(1)} %slice.85), channel_id=1, source_target_pairs={{0,384},{128,0},{256,128},{384,256},{1,385},{129,1},{257,129},{385... | collective-permute-start | bytes 589832 | tf_op jit(solution)/shard_map/ppermute | solution.py:321
  61.9 1.9 collective-permute-start.5
  65.0 5.7 %collective-permute-done.5.far_a = bf16[256,384]{1,0:T(8,128)(2,1)S(1)} collective-permute-done((bf16[256,384]{1,0:T(8,128)(2,1)S(1)}, bf16[256,384]{1,0:T(8,128)(2,1)S(1)}, u32[]{:S(2)}, u32[]{:S(2)}) %collective-permute-start.5) | collective-permute-done | bytes 196640 | tf_op jit(solution)/shard_map/ppermute | solution.py:320
  71.4 3.3 %join.1.refs_3_.refs_2_.weights_a = bf16[2048,384]{1,0:T(8,128)(2,1)} custom-call(s32[11]{0:T(128)} %concatenate.16.place, bf16[512,384]{1,0:T(8,128)(2,1)} %copy-done.12, bf16[512,384]{1,0:T(8,128)(2,1)} %copy-done.11, bf16[512,384]{1,0:T(8,128)(2,1)} %copy-done.10, bf16[256,384]{1,0:T(8,128)(2,1)} %copy-done.15, bf16[256,384]{1,0:T(8,128)(2,1)} %copy-done.14), custom_call_target="tpu_custom_call" | custom-call | tf_op jit(solution)/shard_map/join/pallas_call | solution.py:101
  74.7 1.9 collective-permute-start.7
  76.7 4.7 %collective-permute-start.1 = (bf16[128,2048]{1,0:T(8,128)(2,1)S(1)}, bf16[128,2048]{1,0:T(8,128)(2,1)S(1)}, u32[]{:S(2)}, u32[]{:S(2)}) collective-permute-start(bf16[128,2048]{1,0:T(8,128)(2,1)S(1)} %bitcast.40), channel_id=1, source_target_pairs={{0,3},{1,0},{2,1},{3,2},{4,7},{5,4},{6,5},{7,6},{8,11},{9,8},{10,9... | collective-permute-start | bytes 1572872 | tf_op jit(solution)/shard_map/ppermute | solution.py:319
  81.3 1.9 collective-permute-start
  83.3 9.9 %collective-permute-done.1.refs_2_.right = bf16[128,2048]{1,0:T(8,128)(2,1)S(1)} collective-permute-done((bf16[128,2048]{1,0:T(8,128)(2,1)S(1)}, bf16[128,2048]{1,0:T(8,128)(2,1)S(1)}, u32[]{:S(2)}, u32[]{:S(2)}) %collective-permute-start.1) | collective-permute-done | bytes 524320 | tf_op jit(solution)/shard_map/ppermute | solution.py:319
  93.2 0.8 slice.87
  93.9 5.6 %collective-permute-start.10 = (bf16[64,2048]{1,0:T(8,128)(2,1)}, bf16[64,2048]{1,0:T(8,128)(2,1)S(1)}, u32[]{:S(2)}, u32[]{:S(2)}) collective-permute-start(bf16[64,2048]{1,0:T(8,128)(2,1)} %slice.87), channel_id=1, source_target_pairs={{0,3},{1,0},{2,1},{3,2},{4,7},{5,4},{6,5},{7,6},{8,11},{9,8},{10,9... | collective-permute-start | bytes 786440 | tf_op jit(solution)/shard_map/ppermute | solution.py:321
  100.3 1.9 collective-permute-start.9
  102.3 1.2 copy-done
  103.4 5.6 %shard_map.94 = (f32[192,384]{1,0:T(8,128)}, bf16[192,384]{1,0:T(8,128)(2,1)}) custom-call(s32[11]{0:T(128)} %concatenate.16.place, bf16[128,2048]{1,0:T(8,128)(2,1)} %bitcast.42, bf16[128,2048]{1,0:T(8,128)(2,1)} %copy-done.3, bf16[128,2048]{1,0:T(8,128)(2,1)} %copy-done.2, bf16[2048,384]{1,0:T(8,128)(2,1)} %join.1.refs_3_.refs_2_.weights_a, ...), custom_call_target="tpu_custom_call" | custom-call | tf_op jit(solution)/shard_map/pallas_call | solution.py:203
  109.1 2.0 collective-permute-start.8
  111.8 4.2 %shard_map.95 = (f32[64,384]{1,0:T(8,128)}, bf16[64,384]{1,0:T(8,128)(2,1)}) custom-call(s32[11]{0:T(128)} %concatenate.16.place, bf16[64,2048]{1,0:T(8,128)(2,1)} %collective-permute-done.9.refs_0_.far_a, bf16[64,2048]{1,0:T(8,128)(2,1)} %copy-done.6, bf16[2048,384]{1,0:T(8,128)(2,1)} %join.1.refs_3_.refs_2_.weights_a, bf16[2048,384]{1,0:T(8,128)(2,1)} %copy-done), custom_call_target="tpu_custom_call" | custom-call | tf_op jit(solution)/shard_map/pallas_call | solution.py:203
  116.0 3.9 %collective-permute-start.11 = (bf16[64,384]{1,0:T(8,128)(2,1)}, bf16[64,384]{1,0:T(8,128)(2,1)S(1)}, u32[]{:S(2)}, u32[]{:S(2)}) collective-permute-start(bf16[64,384]{1,0:T(8,128)(2,1)} %get-tuple-element.14), channel_id=1, source_target_pairs={{0,4},{4,0},{8,12},{12,8},{16,20},{20,16},{24,28},{28,24},{32,36},... | collective-permute-start | bytes 147464 | tf_op jit(solution)/shard_map/ppermute | solution.py:361
  120.0 2.2 %collective-permute-done.11 = bf16[64,384]{1,0:T(8,128)(2,1)S(1)} collective-permute-done((bf16[64,384]{1,0:T(8,128)(2,1)}, bf16[64,384]{1,0:T(8,128)(2,1)S(1)}, u32[]{:S(2)}, u32[]{:S(2)}) %collective-permute-start.11) | collective-permute-done | bytes 49184 | tf_op jit(solution)/shard_map/ppermute | solution.py:361
  122.2 0.9 convert_add_fusion.4
  123.3 3.9 %collective-permute-start.12 = (bf16[256,384]{1,0:T(8,128)(2,1)S(1)}, bf16[256,384]{1,0:T(8,128)(2,1)S(1)}, u32[]{:S(2)}, u32[]{:S(2)}) collective-permute-start(bf16[256,384]{1,0:T(8,128)(2,1)S(1)} %pad_maximum_fusion.2.mine), channel_id=1, source_target_pairs={{0,4},{4,0},{8,12},{12,8},{16,20},{20,16},{24,28},{28,24},{32,36},... | collective-permute-start | bytes 589832 | tf_op jit(solution)/shard_map/ppermute | solution.py:364
  127.2 3.6 %collective-permute-done.12.other = bf16[256,384]{1,0:T(8,128)(2,1)S(1)} collective-permute-done((bf16[256,384]{1,0:T(8,128)(2,1)S(1)}, bf16[256,384]{1,0:T(8,128)(2,1)S(1)}, u32[]{:S(2)}, u32[]{:S(2)}) %collective-permute-start.12) | collective-permute-done | bytes 196640 | tf_op jit(solution)/shard_map/ppermute | solution.py:364
  131.5 4.7 %shard_map.96 = bf16[4,512,384]{2,1,0:T(8,128)(2,1)} custom-call(s32[11]{0:T(128)} %concatenate.16.place, bf16[256,384]{1,0:T(8,128)(2,1)} %copy-done.5, bf16[256,384]{1,0:T(8,128)(2,1)} %copy-done.7, bf16[128,2048]{1,0:T(8,128)(2,1)} %bitcast.43, bf16[128,2048]{1,0:T(8,128)(2,1)} %copy-done.3, bf16[128,2048]{1,0:T(8,128)(2,1)} %copy-done.2, ...), custom_call_target="tpu_custom_call" | custom-call | tf_op jit(solution)/shard_map/pallas_call | solution.py:303
  136.2 1.9 collective-permute-start.13
  138.1 3.9 %back.1 = bf16[4,64,2048]{2,1,0:T(8,128)(2,1)} custom-call(s32[11]{0:T(128)} %concatenate.16.place, bf16[256,384]{1,0:T(8,128)(2,1)} %copy-done.5, bf16[256,384]{1,0:T(8,128)(2,1)} %copy-done.7, bf16[2048,384]{1,0:T(8,128)(2,1)} %join.1.refs_3_.refs_2_.weights_a, bf16[2048,384]{1,0:T(8,128)(2,1)} %copy-done), custom_call_target="tpu_custom_call" | custom-call | tf_op jit(solution)/shard_map/back/pallas_call | solution.py:253
  142.0 4.5 %all-to-all-start.1 = ((bf16[4,64,2048]{2,1,0:T(8,128)(2,1)}), bf16[4,64,2048]{2,1,0:T(8,128)(2,1)S(1)}, u32[]{:S(2)}, u32[]{:S(2)}) async-start(bf16[4,64,2048]{2,1,0:T(8,128)(2,1)} %back.1), calls=%async_computation.1 | async-start | bytes 2097152 | tf_op jit(solution)/shard_map/all_to_all | solution.py:367
  146.5 1.2 copy-done.8
  147.7 5.2 %shard_map.97 = bf16[4,512,384]{2,1,0:T(8,128)(2,1)} custom-call(s32[11]{0:T(128)} %concatenate.16.place, bf16[256,384]{1,0:T(8,128)(2,1)} %copy-done.5, bf16[256,384]{1,0:T(8,128)(2,1)} %copy-done.7, bf16[128,2048]{1,0:T(8,128)(2,1)} %bitcast.44, bf16[128,2048]{1,0:T(8,128)(2,1)} %copy-done.3, bf16[128,2048]{1,0:T(8,128)(2,1)} %copy-done.2, ...), custom_call_target="tpu_custom_call" | custom-call | tf_op jit(solution)/shard_map/pallas_call | solution.py:303
  152.9 1.4 slice_bitcast_fusion.6
  154.3 1.9 collective-permute-start.14
  156.2 3.9 %collective-permute-start.16 = (bf16[256,384]{1,0:T(8,128)(2,1)S(1)}, bf16[256,384]{1,0:T(8,128)(2,1)S(1)}, u32[]{:S(2)}, u32[]{:S(2)}) collective-permute-start(bf16[256,384]{1,0:T(8,128)(2,1)S(1)} %get-tuple-element.23), channel_id=1, source_target_pairs={{0,128},{128,256},{256,384},{384,0},{1,129},{129,257},{257,385},{3... | collective-permute-start | bytes 589832 | tf_op jit(solution)/shard_map/ppermute | solution.py:329
  160.2 3.1 %collective-permute-done.14 = bf16[256,384]{1,0:T(8,128)(2,1)S(1)} collective-permute-done((bf16[256,384]{1,0:T(8,128)(2,1)S(1)}, bf16[256,384]{1,0:T(8,128)(2,1)S(1)}, u32[]{:S(2)}, u32[]{:S(2)}) %collective-permute-start.14) | collective-permute-done | bytes 196640 | tf_op jit(solution)/shard_map/ppermute | solution.py:328
  163.2 3.1 %collective-permute-done.16 = bf16[256,384]{1,0:T(8,128)(2,1)S(1)} collective-permute-done((bf16[256,384]{1,0:T(8,128)(2,1)S(1)}, bf16[256,384]{1,0:T(8,128)(2,1)S(1)}, u32[]{:S(2)}, u32[]{:S(2)}) %collective-permute-start.16) | collective-permute-done | bytes 196640 | tf_op jit(solution)/shard_map/ppermute | solution.py:329
  166.5 2.4 %collective-permute-start.17 = (bf16[512,384]{1,0:T(8,128)(2,1)S(1)}, bf16[512,384]{1,0:T(8,128)(2,1)}, u32[]{:S(2)}, u32[]{:S(2)}) collective-permute-start(bf16[512,384]{1,0:T(8,128)(2,1)S(1)} %pad_maximum_fusion.1), channel_id=1, source_target_pairs={{0,128},{128,256},{256,384},{384,0},{1,129},{129,257},{257,385},{3... | collective-permute-start | bytes 1179656 | tf_op jit(solution)/shard_map/ppermute | solution.py:335
  169.0 0.8 pad_maximum_fusion
  169.7 4.6 %collective-permute-start.15 = (bf16[512,384]{1,0:T(8,128)(2,1)}, bf16[512,384]{1,0:T(8,128)(2,1)}, u32[]{:S(2)}, u32[]{:S(2)}) collective-permute-start(bf16[512,384]{1,0:T(8,128)(2,1)} %pad_maximum_fusion), channel_id=1, source_target_pairs={{0,384},{128,0},{256,128},{384,256},{1,385},{129,1},{257,129},{385... | collective-permute-start | bytes 1179656 | tf_op jit(solution)/shard_map/ppermute | solution.py:334
  174.6 0.8 reshape.25
  175.4 14.1 %all-to-all-start.2 = ((bf16[16,4,2048]{2,1,0:T(4,128)(2,1)}), bf16[16,4,2048]{2,1,0:T(4,128)(2,1)S(1)}, u32[]{:S(2)}, u32[]{:S(2)}) async-start(bf16[16,4,2048]{2,1,0:T(4,128)(2,1)} %reshape.25), calls=%async_computation.2 | async-start | bytes 524288 | tf_op jit(solution)/shard_map/all_to_all | solution.py:375
  189.5 1.3 fusion.1
  190.8 1.9 collective-permute-start.18
  192.7 14.7 %all-to-all-done.2.home = bf16[16,4,2048]{2,1,0:T(4,128)(2,1)S(1)} async-done(((bf16[16,4,2048]{2,1,0:T(4,128)(2,1)}), bf16[16,4,2048]{2,1,0:T(4,128)(2,1)S(1)}, u32[]{:S(2)}, u32[]{:S(2)}) %all-to-all-start.2) | async-done | bytes 262176 | tf_op jit(solution)/shard_map/all_to_all | solution.py:375
  208.1 3.3 %home_rows.1 = bf16[128,4096]{1,0:T(8,128)(2,1)} custom-call(s32[2,128]{1,0:T(2,128)} %bitcast.48, bf16[128,4096]{1,0:T(8,128)(2,1)} %latent.3, f32[1,4096]{1,0:T(1,128)} %bitcast.46, bf16[16,4,2048]{2,1,0:T(4,128)(2,1)} %copy-done.9), custom_call_target="tpu_custom_call" | custom-call | tf_op jit(solution)/shard_map/home_rows/pallas_call | solution.py:134
  211.4 0.8 copy.10
  (57 shorter events, 6.0 us)
Async XLA Ops:
  3.9 72.8 %all-to-all-start = ((bf16[16,8,2048]{2,1,0:T(8,128)(2,1)}), bf16[16,8,2048]{2,1,0:T(8,128)(2,1)S(1)}, u32[]{:S(2)}, u32[]{:S(2)}) async-start(bf16[16,8,2048]{2,1,0:T(8,128)(2,1)} %get-tuple-element.9), calls=%async_computation | async-start | bytes 1048576 | tf_op jit(solution)/shard_map/all_to_all | solution.py:353
  19.1 26.9 %collective-permute-start.2 = (bf16[512,384]{1,0:T(8,128)(2,1)}, bf16[512,384]{1,0:T(8,128)(2,1)S(1)}, u32[]{:S(2)}, u32[]{:S(2)}) collective-permute-start(bf16[512,384]{1,0:T(8,128)(2,1)} %get-tuple-element.10), channel_id=1, source_target_pairs={{0,0},{4,64},{8,8},{12,72},{16,16},{20,80},{24,24},{28,88},{32,32}... | collective-permute-start | bytes 1179656 | tf_op jit(solution)/shard_map/ppermute | solution.py:352
  46.0 24.7 %copy-start.12 = (bf16[512,384]{1,0:T(8,128)(2,1)}, bf16[512,384]{1,0:T(8,128)(2,1)S(1)}, u32[]{:S(2)}) copy-start(bf16[512,384]{1,0:T(8,128)(2,1)S(1)} %collective-permute-done.2.own) | copy-start | bytes 1179652
  46.0 10.2 %collective-permute-start.4 = (bf16[512,384]{1,0:T(8,128)(2,1)S(1)}, bf16[512,384]{1,0:T(8,128)(2,1)S(1)}, u32[]{:S(2)}, u32[]{:S(2)}) collective-permute-start(bf16[512,384]{1,0:T(8,128)(2,1)S(1)} %collective-permute-done.2.own), channel_id=1, source_target_pairs={{0,384},{128,0},{256,128},{384,256},{1,385},{129,1},{257,129},{385... | collective-permute-start | bytes 1179656 | tf_op jit(solution)/shard_map/ppermute | solution.py:319
  50.9 10.9 %collective-permute-start.3 = (bf16[512,384]{1,0:T(8,128)(2,1)S(1)}, bf16[512,384]{1,0:T(8,128)(2,1)S(1)}, u32[]{:S(2)}, u32[]{:S(2)}) collective-permute-start(bf16[512,384]{1,0:T(8,128)(2,1)S(1)} %collective-permute-done.2.own), channel_id=1, source_target_pairs={{0,128},{128,256},{256,384},{384,0},{1,129},{129,257},{257,385},{3... | collective-permute-start | bytes 1179656 | tf_op jit(solution)/shard_map/ppermute | solution.py:318
  56.2 14.5 %copy-start.10 = (bf16[512,384]{1,0:T(8,128)(2,1)}, bf16[512,384]{1,0:T(8,128)(2,1)S(1)}, u32[]{:S(2)}) copy-start(bf16[512,384]{1,0:T(8,128)(2,1)S(1)} %collective-permute-done.4.right) | copy-start | bytes 1179652
  56.2 8.8 %collective-permute-start.6 = (bf16[256,384]{1,0:T(8,128)(2,1)S(1)}, bf16[256,384]{1,0:T(8,128)(2,1)S(1)}, u32[]{:S(2)}, u32[]{:S(2)}) collective-permute-start(bf16[256,384]{1,0:T(8,128)(2,1)S(1)} %slice.85), channel_id=1, source_target_pairs={{0,384},{128,0},{256,128},{384,256},{1,385},{129,1},{257,129},{385... | collective-permute-start | bytes 589832 | tf_op jit(solution)/shard_map/ppermute | solution.py:321
  61.9 8.8 %copy-start.11 = (bf16[512,384]{1,0:T(8,128)(2,1)}, bf16[512,384]{1,0:T(8,128)(2,1)S(1)}, u32[]{:S(2)}) copy-start(bf16[512,384]{1,0:T(8,128)(2,1)S(1)} %collective-permute-done.3.left) | copy-start | bytes 1179652
  61.9 8.8 %collective-permute-start.5 = (bf16[256,384]{1,0:T(8,128)(2,1)S(1)}, bf16[256,384]{1,0:T(8,128)(2,1)S(1)}, u32[]{:S(2)}, u32[]{:S(2)}) collective-permute-start(bf16[256,384]{1,0:T(8,128)(2,1)S(1)} %slice.84), channel_id=1, source_target_pairs={{0,128},{128,256},{256,384},{384,0},{1,129},{129,257},{257,385},{3... | collective-permute-start | bytes 589832 | tf_op jit(solution)/shard_map/ppermute | solution.py:320
  65.0 5.7 %copy-start.14 = (bf16[256,384]{1,0:T(8,128)(2,1)}, bf16[256,384]{1,0:T(8,128)(2,1)S(1)}, u32[]{:S(2)}) copy-start(bf16[256,384]{1,0:T(8,128)(2,1)S(1)} %collective-permute-done.6.far_b) | copy-start | bytes 589828
  70.7 0.7 copy-start.15
  74.7 27.5 %collective-permute-start.7 = (bf16[2048,384]{1,0:T(8,128)(2,1)}, bf16[2048,384]{1,0:T(8,128)(2,1)S(1)}, u32[]{:S(2)}, u32[]{:S(2)}) collective-permute-start(bf16[2048,384]{1,0:T(8,128)(2,1)} %join.1.refs_3_.refs_2_.weights_a), channel_id=1, source_target_pairs={{0,64},{64,0},{1,65},{65,1},{2,66},{66,2},{3,67},{67,3},{4,68},{68... | collective-permute-start | bytes 4718600 | tf_op jit(solution)/shard_map/ppermute | solution.py:355
  76.6 25.6 %copy-start.1 = (bf16[16,8,2048]{2,1,0:T(8,128)(2,1)}, bf16[16,8,2048]{2,1,0:T(8,128)(2,1)S(1)}, u32[]{:S(2)}) copy-start(bf16[16,8,2048]{2,1,0:T(8,128)(2,1)S(1)} %all-to-all-done) | copy-start | bytes 1572868
  76.7 16.5 %collective-permute-start.1 = (bf16[128,2048]{1,0:T(8,128)(2,1)S(1)}, bf16[128,2048]{1,0:T(8,128)(2,1)S(1)}, u32[]{:S(2)}, u32[]{:S(2)}) collective-permute-start(bf16[128,2048]{1,0:T(8,128)(2,1)S(1)} %bitcast.40), channel_id=1, source_target_pairs={{0,3},{1,0},{2,1},{3,2},{4,7},{5,4},{6,5},{7,6},{8,11},{9,8},{10,9... | collective-permute-start | bytes 1572872 | tf_op jit(solution)/shard_map/ppermute | solution.py:319
  81.3 18.2 %collective-permute-start = (bf16[128,2048]{1,0:T(8,128)(2,1)S(1)}, bf16[128,2048]{1,0:T(8,128)(2,1)S(1)}, u32[]{:S(2)}, u32[]{:S(2)}) collective-permute-start(bf16[128,2048]{1,0:T(8,128)(2,1)S(1)} %bitcast.41), channel_id=1, source_target_pairs={{0,1},{1,2},{2,3},{3,0},{4,5},{5,6},{6,7},{7,4},{8,9},{9,10},{10,1... | collective-permute-start | bytes 1572872 | tf_op jit(solution)/shard_map/ppermute | solution.py:318
  93.2 9.1 %copy-start.2 = (bf16[128,2048]{1,0:T(8,128)(2,1)}, bf16[128,2048]{1,0:T(8,128)(2,1)S(1)}, u32[]{:S(2)}) copy-start(bf16[128,2048]{1,0:T(8,128)(2,1)S(1)} %collective-permute-done.1.refs_2_.right) | copy-start | bytes 1572868
  93.9 17.2 %collective-permute-start.10 = (bf16[64,2048]{1,0:T(8,128)(2,1)}, bf16[64,2048]{1,0:T(8,128)(2,1)S(1)}, u32[]{:S(2)}, u32[]{:S(2)}) collective-permute-start(bf16[64,2048]{1,0:T(8,128)(2,1)} %slice.87), channel_id=1, source_target_pairs={{0,3},{1,0},{2,1},{3,2},{4,7},{5,4},{6,5},{7,6},{8,11},{9,8},{10,9... | collective-permute-start | bytes 786440 | tf_op jit(solution)/shard_map/ppermute | solution.py:321
  99.5 2.7 %copy-start.3 = (bf16[128,2048]{1,0:T(8,128)(2,1)}, bf16[128,2048]{1,0:T(8,128)(2,1)S(1)}, u32[]{:S(2)}) copy-start(bf16[128,2048]{1,0:T(8,128)(2,1)S(1)} %collective-permute-done.refs_1_.left) | copy-start | bytes 1572868
  100.3 11.0 %collective-permute-start.9 = (bf16[64,2048]{1,0:T(8,128)(2,1)}, bf16[64,2048]{1,0:T(8,128)(2,1)}, u32[]{:S(2)}, u32[]{:S(2)}) collective-permute-start(bf16[64,2048]{1,0:T(8,128)(2,1)} %slice.86), channel_id=1, source_target_pairs={{0,1},{1,2},{2,3},{3,0},{4,5},{5,6},{6,7},{7,4},{8,9},{9,10},{10,1... | collective-permute-start | bytes 786440 | tf_op jit(solution)/shard_map/ppermute | solution.py:320
  102.3 1.2 copy-start
  109.1 10.9 %copy-start.13 = (f32[192,384]{1,0:T(8,128)S(1)}, f32[192,384]{1,0:T(8,128)}, u32[]{:S(2)}) copy-start(f32[192,384]{1,0:T(8,128)} %get-tuple-element.11) | copy-start | bytes 884740
  109.1 10.8 %collective-permute-start.8 = (bf16[192,384]{1,0:T(8,128)(2,1)}, bf16[192,384]{1,0:T(8,128)(2,1)S(1)}, u32[]{:S(2)}, u32[]{:S(2)}) collective-permute-start(bf16[192,384]{1,0:T(8,128)(2,1)} %get-tuple-element.12), channel_id=1, source_target_pairs={{0,4},{4,0},{8,12},{12,8},{16,20},{20,16},{24,28},{28,24},{32,36},... | collective-permute-start | bytes 442376 | tf_op jit(solution)/shard_map/ppermute | solution.py:361
  111.1 0.7 copy-start.6
  116.0 6.2 %collective-permute-start.11 = (bf16[64,384]{1,0:T(8,128)(2,1)}, bf16[64,384]{1,0:T(8,128)(2,1)S(1)}, u32[]{:S(2)}, u32[]{:S(2)}) collective-permute-start(bf16[64,384]{1,0:T(8,128)(2,1)} %get-tuple-element.14), channel_id=1, source_target_pairs={{0,4},{4,0},{8,12},{12,8},{16,20},{20,16},{24,28},{28,24},{32,36},... | collective-permute-start | bytes 147464 | tf_op jit(solution)/shard_map/ppermute | solution.py:361
  123.2 7.6 %copy-start.5 = (bf16[256,384]{1,0:T(8,128)(2,1)}, bf16[256,384]{1,0:T(8,128)(2,1)S(1)}, u32[]{:S(2)}) copy-start(bf16[256,384]{1,0:T(8,128)(2,1)S(1)} %pad_maximum_fusion.2.mine) | copy-start | bytes 589828
  123.3 7.6 %collective-permute-start.12 = (bf16[256,384]{1,0:T(8,128)(2,1)S(1)}, bf16[256,384]{1,0:T(8,128)(2,1)S(1)}, u32[]{:S(2)}, u32[]{:S(2)}) collective-permute-start(bf16[256,384]{1,0:T(8,128)(2,1)S(1)} %pad_maximum_fusion.2.mine), channel_id=1, source_target_pairs={{0,4},{4,0},{8,12},{12,8},{16,20},{20,16},{24,28},{28,24},{32,36},... | collective-permute-start | bytes 589832 | tf_op jit(solution)/shard_map/ppermute | solution.py:364
  130.8 0.7 copy-start.7
  136.2 10.4 %collective-permute-start.13 = (bf16[4,512,384]{2,1,0:T(8,128)(2,1)}, bf16[4,512,384]{2,1,0:T(8,128)(2,1)S(1)}, u32[]{:S(2)}, u32[]{:S(2)}) collective-permute-start(bf16[4,512,384]{2,1,0:T(8,128)(2,1)} %shard_map.96), channel_id=1, source_target_pairs={{0,64},{64,0},{1,65},{65,1},{2,66},{66,2},{3,67},{67,3},{4,68},{68... | collective-permute-start | bytes 4718600 | tf_op jit(solution)/shard_map/ppermute | solution.py:368
  142.0 32.3 %all-to-all-start.1 = ((bf16[4,64,2048]{2,1,0:T(8,128)(2,1)}), bf16[4,64,2048]{2,1,0:T(8,128)(2,1)S(1)}, u32[]{:S(2)}, u32[]{:S(2)}) async-start(bf16[4,64,2048]{2,1,0:T(8,128)(2,1)} %back.1), calls=%async_computation.1 | async-start | bytes 2097152 | tf_op jit(solution)/shard_map/all_to_all | solution.py:367
  146.5 1.2 copy-start.8
  152.9 13.5 %copy-start.4 = (bf16[4,512,384]{2,1,0:T(8,128)(2,1)S(1)}, bf16[4,512,384]{2,1,0:T(8,128)(2,1)}, u32[]{:S(2)}) copy-start(bf16[4,512,384]{2,1,0:T(8,128)(2,1)} %shard_map.97) | copy-start | bytes 4718596
  154.3 8.9 %collective-permute-start.14 = (bf16[256,384]{1,0:T(8,128)(2,1)S(1)}, bf16[256,384]{1,0:T(8,128)(2,1)S(1)}, u32[]{:S(2)}, u32[]{:S(2)}) collective-permute-start(bf16[256,384]{1,0:T(8,128)(2,1)S(1)} %get-tuple-element.22), channel_id=1, source_target_pairs={{0,384},{128,0},{256,128},{384,256},{1,385},{129,1},{257,129},{385... | collective-permute-start | bytes 589832 | tf_op jit(solution)/shard_map/ppermute | solution.py:328
  156.2 10.1 %collective-permute-start.16 = (bf16[256,384]{1,0:T(8,128)(2,1)S(1)}, bf16[256,384]{1,0:T(8,128)(2,1)S(1)}, u32[]{:S(2)}, u32[]{:S(2)}) collective-permute-start(bf16[256,384]{1,0:T(8,128)(2,1)S(1)} %get-tuple-element.23), channel_id=1, source_target_pairs={{0,128},{128,256},{256,384},{384,0},{1,129},{129,257},{257,385},{3... | collective-permute-start | bytes 589832 | tf_op jit(solution)/shard_map/ppermute | solution.py:329
  166.5 23.0 %collective-permute-start.17 = (bf16[512,384]{1,0:T(8,128)(2,1)S(1)}, bf16[512,384]{1,0:T(8,128)(2,1)}, u32[]{:S(2)}, u32[]{:S(2)}) collective-permute-start(bf16[512,384]{1,0:T(8,128)(2,1)S(1)} %pad_maximum_fusion.1), channel_id=1, source_target_pairs={{0,128},{128,256},{256,384},{384,0},{1,129},{129,257},{257,385},{3... | collective-permute-start | bytes 1179656 | tf_op jit(solution)/shard_map/ppermute | solution.py:335
  169.7 19.8 %collective-permute-start.15 = (bf16[512,384]{1,0:T(8,128)(2,1)}, bf16[512,384]{1,0:T(8,128)(2,1)}, u32[]{:S(2)}, u32[]{:S(2)}) collective-permute-start(bf16[512,384]{1,0:T(8,128)(2,1)} %pad_maximum_fusion), channel_id=1, source_target_pairs={{0,384},{128,0},{256,128},{384,256},{1,385},{129,1},{257,129},{385... | collective-permute-start | bytes 1179656 | tf_op jit(solution)/shard_map/ppermute | solution.py:334
  175.4 32.0 %all-to-all-start.2 = ((bf16[16,4,2048]{2,1,0:T(4,128)(2,1)}), bf16[16,4,2048]{2,1,0:T(4,128)(2,1)S(1)}, u32[]{:S(2)}, u32[]{:S(2)}) async-start(bf16[16,4,2048]{2,1,0:T(4,128)(2,1)} %reshape.25), calls=%async_computation.2 | async-start | bytes 524288 | tf_op jit(solution)/shard_map/all_to_all | solution.py:375
  190.8 20.6 %collective-permute-start.18 = (bf16[512,384]{1,0:T(8,128)(2,1)S(1)}, bf16[512,384]{1,0:T(8,128)(2,1)S(1)}, u32[]{:S(2)}, u32[]{:S(2)}) collective-permute-start(bf16[512,384]{1,0:T(8,128)(2,1)S(1)} %fusion.1), channel_id=1, source_target_pairs={{0,0},{4,64},{8,8},{12,72},{16,16},{20,80},{24,24},{28,88},{32,32}... | collective-permute-start | bytes 1179656 | tf_op jit(solution)/shard_map/ppermute | solution.py:370
  207.4 0.7 copy-start.9

commit v8 on v7

--- a/solution.py
+++ b/solution.py
@@ -265,7 +265,7 @@
 
 
 def grads_kernel(kept, place, mine, other, own, left, right, far_a, far_b, *refs):
-    out, inner = refs[-2:]
+    out, inner = refs[kept], refs[-1]
 
     @pl.when(pl.program_id(0) == 0)
     def _():
@@ -288,11 +288,24 @@
     total = lax.dot_general(
         rows, inner[...], (((0,), (0,)), ((), ())), preferred_element_type=F32
     )
+
+    def store(at, value):
+        for i, near in enumerate(refs[1:4]):
+
+            @pl.when(at == i)
+            def _():
+                near[...] = value.astype(BF16)
+
+        for i, far in enumerate(refs[4:6]):
+
+            @pl.when(at == 3)
+            def _():
+                far[...] = value[i * CUT // 2 : (i + 1) * CUT // 2].astype(BF16)
+
     for k in range(WIDE // CUT):
         part = total[k * CUT : (k + 1) * CUT]
         if kept:
-            part = part + refs[0][k].astype(F32)
-            out[place[3 + pl.program_id(0) * (WIDE // CUT) + k]] = part.astype(BF16)
+            store(place[3 + pl.program_id(0) * (WIDE // CUT) + k], part + refs[0][k].astype(F32))
         else:
             out[k] = part.astype(BF16)
 
@@ -300,16 +313,21 @@
 def grads(place, mine, other, blocks, received):
     dims = (ROWS // 2, 3 * HID)
     part = pl.BlockSpec((WIDE // CUT, CUT, 3 * HID), lambda i, *_: (i, 0, 0))
+    cuts = [(n, 3 * HID) for n in (CUT, CUT, CUT, CUT // 2, CUT // 2)]
     return pl.pallas_call(
         functools.partial(grads_kernel, len(received)),
         grid_spec=pltpu.PrefetchScalarGridSpec(
             num_scalar_prefetch=1,
             grid=(HALF // WIDE,),
             in_specs=[whole(dims), whole(dims), *row_specs(), *[part for _ in received]],
-            out_specs=whole((HALF // CUT, CUT, 3 * HID)) if received else part,
+            out_specs=[whole(dims) for dims in cuts] if received else part,
             scratch_shapes=[pltpu.VMEM((ROWS, 3 * HID), BF16)],
         ),
-        out_shape=shape((HALF // CUT, CUT, 3 * HID), BF16),
+        out_shape=(
+            [shape(dims, BF16) for dims in cuts]
+            if received
+            else shape((HALF // CUT, CUT, 3 * HID), BF16)
+        ),
     )(place, mine, other, *blocks, *received)
 
 
@@ -323,10 +341,10 @@
 
 
 def scattered(parts):
-    own, left, right, far = parts
+    own, left, right, far_a, far_b = parts
     half = own.shape[0] // 2
-    got_a = lax.ppermute(far[:half], "y", MINUS).astype(F32)
-    got_b = lax.ppermute(far[half:], "y", PLUS).astype(F32)
+    got_a = lax.ppermute(far_a, "y", MINUS).astype(F32)
+    got_b = lax.ppermute(far_b, "y", PLUS).astype(F32)
     near_a = (left[:half].astype(F32) + got_a).astype(BF16)
     near_b = (right[half:].astype(F32) + got_b).astype(BF16)
     left = jnp.concatenate([near_a, left[half:]], axis=0)
@@ -363,9 +381,10 @@
     inner = gates(jnp.concatenate(totals, axis=0))
     outer = lax.ppermute(inner, "z", FLIP)
 
+    sent = grads(place, inner, outer, blocks, ())
+    received = lax.ppermute(sent, "c", TURN)
     part = back(place, inner, outer, weights)
     part = lax.all_to_all(part, "x", 0, 0, tiled=True)
-    received = lax.ppermute(grads(place, inner, outer, blocks, ()), "c", TURN)
     grad = scattered(grads(place, inner, outer, blocks, (received,)))
     grad = lax.ppermute(grad, ("c", "z"), SWAP)
     grad_gu = grad[:, : 2 * HID][None]

time: 214 us -> 215 us (level)
  the two profiles are of different devices: /device:TPU:32 before, /device:TPU:24 now
where the time goes in v8:
time: 215 us; the launch traced here: 212 us
  starting transfers between devices  115 us (53%)
  waiting for transfers between devices  51.3 us (24%)
  Pallas kernels  33.9 us (16%)
  local copies, waits for them, and re-layouts  9.76 us (5%)
    ppermute x1, starting transfers between devices, work(): weights = (joined, lax.ppermute(joined, 'c', TURN))  27.1 us
    all_to_all x1, waiting for transfers between devices, work(): home = lax.all_to_all(summed.reshape(Z, CAP, HALF), 'z', 0, 0, tiled=True)  16.5 us
    all_to_all x1, starting transfers between devices, work(): got = lax.all_to_all(send, 'z', 0, 0, tiled=True)  15.2 us
    ppermute x2, waiting for transfers between devices, gathered(): right = lax.ppermute(own, axis, MINUS)  13.2 us
    all_to_all x1, starting transfers between devices, work(): home = lax.all_to_all(summed.reshape(Z, CAP, HALF), 'z', 0, 0, tiled=True)  12.2 us
    pallas_call x2, Pallas kernels, grads(): pl.pallas_call(functools.partial(grads_kernel, len(received)), grid_spec=...  10.3 us
    pallas_call x2, Pallas kernels, mix(): pl.pallas_call(functools.partial(mix_kernel, len(blocks)), grid_spec=pltp...  9.79 us
    ppermute x2, starting transfers between devices, gathered(): far_b = lax.ppermute(right[half:], axis, MINUS)  7.51 us
  transfers between devices with their start and end apart: 22, of which 10 were waited for; matrix products, arithmetic and copies ran while one was open for 2% of the time, Pallas kernels for 10%

profile of v8, /device:TPU:24, one launch (start us, length us, event | category | flops | bytes accessed | tf_op | source)
XLA Modules:
  0.0 212.4 jit_solution(14228519497408958262)
XLA Ops:
  0.6 3.2 %send_rows.1 = (bf16[16,8,2048]{2,1,0:T(8,128)(2,1)}, bf16[512,384]{1,0:T(8,128)(2,1)}) custom-call(s32[2,128]{1,0:T(2,128)} %bitcast.24, f32[2,128]{1,0:T(2,128)} %bitcast.26, bf16[128,4096]{1,0:T(8,128)(2,1)} %latent.3, bf16[128,4096]{1,0:T(8,128)(2,1)} %dout.1, f32[1,4096]{1,0:T(1,128)} %bitcast.22, bf16[1,512,256]{2,1,0:T(8,128)(2,1)} %gate_up.1, ...), custom_call_target="tpu_custom_call" | custom-call | tf_op jit(solution)/shard_map/send_rows/pallas_call | solution.py:85
  3.9 15.2 %all-to-all-start = ((bf16[16,8,2048]{2,1,0:T(8,128)(2,1)}), bf16[16,8,2048]{2,1,0:T(8,128)(2,1)S(1)}, u32[]{:S(2)}, u32[]{:S(2)}) async-start(bf16[16,8,2048]{2,1,0:T(8,128)(2,1)} %get-tuple-element.14), calls=%async_computation | async-start | bytes 1048576 | tf_op jit(solution)/shard_map/all_to_all | solution.py:371
  19.1 1.7 collective-permute-start.2
  20.7 2.6 %collective-permute-start.4 = (bf16[512,384]{1,0:T(8,128)(2,1)S(1)}, bf16[512,384]{1,0:T(8,128)(2,1)S(1)}, u32[]{:S(2)}, u32[]{:S(2)}) collective-permute-start(bf16[512,384]{1,0:T(8,128)(2,1)S(1)} %collective-permute-done.2.own), channel_id=1, source_target_pairs={{0,384},{128,0},{256,128},{384,256},{1,385},{129,1},{257,129},{385... | collective-permute-start | bytes 1179656 | tf_op jit(solution)/shard_map/ppermute | solution.py:337
  23.4 4.4 %collective-permute-start.3 = (bf16[512,384]{1,0:T(8,128)(2,1)S(1)}, bf16[512,384]{1,0:T(8,128)(2,1)S(1)}, u32[]{:S(2)}, u32[]{:S(2)}) collective-permute-start(bf16[512,384]{1,0:T(8,128)(2,1)S(1)} %collective-permute-done.2.own), channel_id=1, source_target_pairs={{0,128},{128,256},{256,384},{384,0},{1,129},{129,257},{257,385},{3... | collective-permute-start | bytes 1179656 | tf_op jit(solution)/shard_map/ppermute | solution.py:336
  27.8 3.8 %collective-permute-done.4.right = bf16[512,384]{1,0:T(8,128)(2,1)S(1)} collective-permute-done((bf16[512,384]{1,0:T(8,128)(2,1)S(1)}, bf16[512,384]{1,0:T(8,128)(2,1)S(1)}, u32[]{:S(2)}, u32[]{:S(2)}) %collective-permute-start.4) | collective-permute-done | bytes 393248 | tf_op jit(solution)/shard_map/ppermute | solution.py:337
  31.6 1.9 collective-permute-start.6
  33.6 5.1 %collective-permute-start.5 = (bf16[256,384]{1,0:T(8,128)(2,1)S(1)}, bf16[256,384]{1,0:T(8,128)(2,1)S(1)}, u32[]{:S(2)}, u32[]{:S(2)}) collective-permute-start(bf16[256,384]{1,0:T(8,128)(2,1)S(1)} %slice.52), channel_id=1, source_target_pairs={{0,128},{128,256},{256,384},{384,0},{1,129},{129,257},{257,385},{3... | collective-permute-start | bytes 589832 | tf_op jit(solution)/shard_map/ppermute | solution.py:338
  39.5 0.9 collective-permute-done.6.far_b
  40.4 1.5 collective-permute-done.5.far_a
  42.6 3.4 %join.1.refs_3_.refs_2_.weights_a = bf16[2048,384]{1,0:T(8,128)(2,1)} custom-call(s32[11]{0:T(128)} %concatenate.16.place, bf16[512,384]{1,0:T(8,128)(2,1)} %copy-done.14, bf16[512,384]{1,0:T(8,128)(2,1)} %copy-done.10, bf16[512,384]{1,0:T(8,128)(2,1)} %copy-done.9, bf16[256,384]{1,0:T(8,128)(2,1)} %copy-done.17, bf16[256,384]{1,0:T(8,128)(2,1)} %copy-done.16), custom_call_target="tpu_custom_call" | custom-call | tf_op jit(solution)/shard_map/join/pallas_call | solution.py:101
  46.0 27.1 %collective-permute-start.7 = (bf16[2048,384]{1,0:T(8,128)(2,1)}, bf16[2048,384]{1,0:T(8,128)(2,1)S(1)}, u32[]{:S(2)}, u32[]{:S(2)}) collective-permute-start(bf16[2048,384]{1,0:T(8,128)(2,1)} %join.1.refs_3_.refs_2_.weights_a), channel_id=1, source_target_pairs={{0,64},{64,0},{1,65},{65,1},{2,66},{66,2},{3,67},{67,3},{4,68},{68... | collective-permute-start | bytes 4718600 | tf_op jit(solution)/shard_map/ppermute | solution.py:373
  73.0 4.7 %collective-permute-start.1 = (bf16[128,2048]{1,0:T(8,128)(2,1)S(1)}, bf16[128,2048]{1,0:T(8,128)(2,1)S(1)}, u32[]{:S(2)}, u32[]{:S(2)}) collective-permute-start(bf16[128,2048]{1,0:T(8,128)(2,1)S(1)} %bitcast.17), channel_id=1, source_target_pairs={{0,3},{1,0},{2,1},{3,2},{4,7},{5,4},{6,5},{7,6},{8,11},{9,8},{10,9... | collective-permute-start | bytes 1572872 | tf_op jit(solution)/shard_map/ppermute | solution.py:337
  77.7 1.9 collective-permute-start
  79.6 9.4 %collective-permute-done.1.refs_2_.right = bf16[128,2048]{1,0:T(8,128)(2,1)S(1)} collective-permute-done((bf16[128,2048]{1,0:T(8,128)(2,1)S(1)}, bf16[128,2048]{1,0:T(8,128)(2,1)S(1)}, u32[]{:S(2)}, u32[]{:S(2)}) %collective-permute-start.1) | collective-permute-done | bytes 524320 | tf_op jit(solution)/shard_map/ppermute | solution.py:337
  89.1 0.8 slice.55
  89.8 5.6 %collective-permute-start.10 = (bf16[64,2048]{1,0:T(8,128)(2,1)}, bf16[64,2048]{1,0:T(8,128)(2,1)S(1)}, u32[]{:S(2)}, u32[]{:S(2)}) collective-permute-start(bf16[64,2048]{1,0:T(8,128)(2,1)} %slice.55), channel_id=1, source_target_pairs={{0,3},{1,0},{2,1},{3,2},{4,7},{5,4},{6,5},{7,6},{8,11},{9,8},{10,9... | collective-permute-start | bytes 786440 | tf_op jit(solution)/shard_map/ppermute | solution.py:339
  95.4 0.8 slice.54
  96.2 1.9 collective-permute-start.9
  98.2 1.2 copy-done
  99.3 5.6 %shard_map.94 = (f32[192,384]{1,0:T(8,128)}, bf16[192,384]{1,0:T(8,128)(2,1)}) custom-call(s32[11]{0:T(128)} %concatenate.16.place, bf16[128,2048]{1,0:T(8,128)(2,1)} %bitcast.19, bf16[128,2048]{1,0:T(8,128)(2,1)} %copy-done.3, bf16[128,2048]{1,0:T(8,128)(2,1)} %copy-done.2, bf16[2048,384]{1,0:T(8,128)(2,1)} %join.1.refs_3_.refs_2_.weights_a, ...), custom_call_target="tpu_custom_call" | custom-call | tf_op jit(solution)/shard_map/pallas_call | solution.py:203
  105.0 4.6 %collective-permute-start.8 = (bf16[192,384]{1,0:T(8,128)(2,1)}, bf16[192,384]{1,0:T(8,128)(2,1)S(1)}, u32[]{:S(2)}, u32[]{:S(2)}) collective-permute-start(bf16[192,384]{1,0:T(8,128)(2,1)} %get-tuple-element.17), channel_id=1, source_target_pairs={{0,4},{4,0},{8,12},{12,8},{16,20},{20,16},{24,28},{28,24},{32,36},... | collective-permute-start | bytes 442376 | tf_op jit(solution)/shard_map/ppermute | solution.py:379
  110.3 4.2 %shard_map.95 = (f32[64,384]{1,0:T(8,128)}, bf16[64,384]{1,0:T(8,128)(2,1)}) custom-call(s32[11]{0:T(128)} %concatenate.16.place, bf16[64,2048]{1,0:T(8,128)(2,1)} %collective-permute-done.9.refs_0_.far_a, bf16[64,2048]{1,0:T(8,128)(2,1)} %copy-done.5, bf16[2048,384]{1,0:T(8,128)(2,1)} %join.1.refs_3_.refs_2_.weights_a, bf16[2048,384]{1,0:T(8,128)(2,1)} %copy-done), custom_call_target="tpu_custom_call" | custom-call | tf_op jit(solution)/shard_map/pallas_call | solution.py:203
  114.4 1.9 collective-permute-start.11
  116.4 4.2 %collective-permute-done.11 = bf16[64,384]{1,0:T(8,128)(2,1)S(1)} collective-permute-done((bf16[64,384]{1,0:T(8,128)(2,1)}, bf16[64,384]{1,0:T(8,128)(2,1)S(1)}, u32[]{:S(2)}, u32[]{:S(2)}) %collective-permute-start.11) | collective-permute-done | bytes 49184 | tf_op jit(solution)/shard_map/ppermute | solution.py:379
  120.6 0.9 convert_add_fusion.1
  121.7 1.9 collective-permute-start.12
  123.6 5.6 %collective-permute-done.12.other = bf16[256,384]{1,0:T(8,128)(2,1)S(1)} collective-permute-done((bf16[256,384]{1,0:T(8,128)(2,1)S(1)}, bf16[256,384]{1,0:T(8,128)(2,1)S(1)}, u32[]{:S(2)}, u32[]{:S(2)}) %collective-permute-start.12) | collective-permute-done | bytes 196640 | tf_op jit(solution)/shard_map/ppermute | solution.py:382
  129.3 0.7 copy-done.6
  130.0 4.7 %shard_map.96 = bf16[4,512,384]{2,1,0:T(8,128)(2,1)} custom-call(s32[11]{0:T(128)} %concatenate.16.place, bf16[256,384]{1,0:T(8,128)(2,1)} %copy-done.4, bf16[256,384]{1,0:T(8,128)(2,1)} %copy-done.6, bf16[128,2048]{1,0:T(8,128)(2,1)} %bitcast.20, bf16[128,2048]{1,0:T(8,128)(2,1)} %copy-done.3, bf16[128,2048]{1,0:T(8,128)(2,1)} %copy-done.2, ...), custom_call_target="tpu_custom_call" | custom-call | tf_op jit(solution)/shard_map/pallas_call | solution.py:317
  134.7 1.9 collective-permute-start.13
  136.6 3.6 %collective-permute-done.13.refs_0_ = bf16[4,512,384]{2,1,0:T(8,128)(2,1)S(1)} collective-permute-done((bf16[4,512,384]{2,1,0:T(8,128)(2,1)}, bf16[4,512,384]{2,1,0:T(8,128)(2,1)S(1)}, u32[]{:S(2)}, u32[]{:S(2)}) %collective-permute-start.13) | collective-permute-done | bytes 1572896 | tf_op jit(solution)/shard_map/ppermute | solution.py:385
  140.2 1.2 copy-done.7
  141.4 5.6 %shard_map.97 = (bf16[512,384]{1,0:T(8,128)(2,1)}, bf16[512,384]{1,0:T(8,128)(2,1)}, bf16[512,384]{1,0:T(8,128)(2,1)}, bf16[256,384]{1,0:T(8,128)(2,1)}, bf16[256,384]{1,0:T(8,128)(2,1)}) custom-call(s32[11]{0:T(128)} %concatenate.16.place, bf16[256,384]{1,0:T(8,128)(2,1)} %copy-done.4, bf16[256,384]{1,0:T(8,128)(2,1)} %copy-done.6, ...), custom_call_target="tpu_custom_call" | custom-call | tf_op jit(solution)/shard_map/pallas_call | solution.py:317
  146.9 5.6 %collective-permute-start.16 = (bf16[256,384]{1,0:T(8,128)(2,1)}, bf16[256,384]{1,0:T(8,128)(2,1)S(1)}, u32[]{:S(2)}, u32[]{:S(2)}) collective-permute-start(bf16[256,384]{1,0:T(8,128)(2,1)} %get-tuple-element.24), channel_id=1, source_target_pairs={{0,128},{128,256},{256,384},{384,0},{1,129},{129,257},{257,385},{3... | collective-permute-start | bytes 589832 | tf_op jit(solution)/shard_map/ppermute | solution.py:347
  152.5 3.9 %back.1 = bf16[4,64,2048]{2,1,0:T(8,128)(2,1)} custom-call(s32[11]{0:T(128)} %concatenate.16.place, bf16[256,384]{1,0:T(8,128)(2,1)} %copy-done.4, bf16[256,384]{1,0:T(8,128)(2,1)} %copy-done.6, bf16[2048,384]{1,0:T(8,128)(2,1)} %join.1.refs_3_.refs_2_.weights_a, bf16[2048,384]{1,0:T(8,128)(2,1)} %copy-done), custom_call_target="tpu_custom_call" | custom-call | tf_op jit(solution)/shard_map/back/pallas_call | solution.py:253
  156.5 4.6 %all-to-all-start.1 = ((bf16[4,64,2048]{2,1,0:T(8,128)(2,1)}), bf16[4,64,2048]{2,1,0:T(8,128)(2,1)S(1)}, u32[]{:S(2)}, u32[]{:S(2)}) async-start(bf16[4,64,2048]{2,1,0:T(8,128)(2,1)} %back.1), calls=%async_computation.1 | async-start | bytes 2097152 | tf_op jit(solution)/shard_map/all_to_all | solution.py:387
  161.2 1.9 collective-permute-start.14
  163.2 5.1 %collective-permute-start.17 = (bf16[512,384]{1,0:T(8,128)(2,1)S(1)}, bf16[512,384]{1,0:T(8,128)(2,1)S(1)}, u32[]{:S(2)}, u32[]{:S(2)}) collective-permute-start(bf16[512,384]{1,0:T(8,128)(2,1)S(1)} %pad_maximum_fusion.1), channel_id=1, source_target_pairs={{0,128},{128,256},{256,384},{384,0},{1,129},{129,257},{257,385},{3... | collective-permute-start | bytes 1179656 | tf_op jit(solution)/shard_map/ppermute | solution.py:353
  168.4 2.3 %collective-permute-done.14 = bf16[256,384]{1,0:T(8,128)(2,1)S(1)} collective-permute-done((bf16[256,384]{1,0:T(8,128)(2,1)S(1)}, bf16[256,384]{1,0:T(8,128)(2,1)S(1)}, u32[]{:S(2)}, u32[]{:S(2)}) %collective-permute-start.14) | collective-permute-done | bytes 196640 | tf_op jit(solution)/shard_map/ppermute | solution.py:346
  170.8 2.1 collective-permute-start.15
  172.9 3.4 %all-to-all-done.1 = bf16[4,64,2048]{2,1,0:T(8,128)(2,1)S(1)} async-done(((bf16[4,64,2048]{2,1,0:T(8,128)(2,1)}), bf16[4,64,2048]{2,1,0:T(8,128)(2,1)S(1)}, u32[]{:S(2)}, u32[]{:S(2)}) %all-to-all-start.1) | async-done | bytes 1048608 | tf_op jit(solution)/shard_map/all_to_all | solution.py:387
  176.4 0.8 reshape.13
  177.2 12.2 %all-to-all-start.2 = ((bf16[16,4,2048]{2,1,0:T(4,128)(2,1)}), bf16[16,4,2048]{2,1,0:T(4,128)(2,1)S(1)}, u32[]{:S(2)}, u32[]{:S(2)}) async-start(bf16[16,4,2048]{2,1,0:T(4,128)(2,1)} %reshape.13), calls=%async_computation.2 | async-start | bytes 524288 | tf_op jit(solution)/shard_map/all_to_all | solution.py:394
  190.3 16.5 %all-to-all-done.2.home = bf16[16,4,2048]{2,1,0:T(4,128)(2,1)S(1)} async-done(((bf16[16,4,2048]{2,1,0:T(4,128)(2,1)}), bf16[16,4,2048]{2,1,0:T(4,128)(2,1)S(1)}, u32[]{:S(2)}, u32[]{:S(2)}) %all-to-all-start.2) | async-done | bytes 262176 | tf_op jit(solution)/shard_map/all_to_all | solution.py:394
  207.5 3.3 %home_rows.1 = bf16[128,4096]{1,0:T(8,128)(2,1)} custom-call(s32[2,128]{1,0:T(2,128)} %bitcast.25, bf16[128,4096]{1,0:T(8,128)(2,1)} %latent.3, f32[1,4096]{1,0:T(1,128)} %bitcast.23, bf16[16,4,2048]{2,1,0:T(4,128)(2,1)} %copy-done.8), custom_call_target="tpu_custom_call" | custom-call | tf_op jit(solution)/shard_map/home_rows/pallas_call | solution.py:134
  210.9 0.8 copy.10
  211.7 0.7 slice_bitcast_fusion
  (65 shorter events, 4.3 us)
Async XLA Ops:
  3.9 69.2 %all-to-all-start = ((bf16[16,8,2048]{2,1,0:T(8,128)(2,1)}), bf16[16,8,2048]{2,1,0:T(8,128)(2,1)S(1)}, u32[]{:S(2)}, u32[]{:S(2)}) async-start(bf16[16,8,2048]{2,1,0:T(8,128)(2,1)} %get-tuple-element.14), calls=%async_computation | async-start | bytes 1048576 | tf_op jit(solution)/shard_map/all_to_all | solution.py:371
  19.1 1.7 collective-permute-start.2
  20.7 21.2 %copy-start.14 = (bf16[512,384]{1,0:T(8,128)(2,1)}, bf16[512,384]{1,0:T(8,128)(2,1)S(1)}, u32[]{:S(2)}) copy-start(bf16[512,384]{1,0:T(8,128)(2,1)S(1)} %collective-permute-done.2.own) | copy-start | bytes 1179652
  20.7 10.9 %collective-permute-start.4 = (bf16[512,384]{1,0:T(8,128)(2,1)S(1)}, bf16[512,384]{1,0:T(8,128)(2,1)S(1)}, u32[]{:S(2)}, u32[]{:S(2)}) collective-permute-start(bf16[512,384]{1,0:T(8,128)(2,1)S(1)} %collective-permute-done.2.own), channel_id=1, source_target_pairs={{0,384},{128,0},{256,128},{384,256},{1,385},{129,1},{257,129},{385... | collective-permute-start | bytes 1179656 | tf_op jit(solution)/shard_map/ppermute | solution.py:337
  23.4 10.2 %collective-permute-start.3 = (bf16[512,384]{1,0:T(8,128)(2,1)S(1)}, bf16[512,384]{1,0:T(8,128)(2,1)S(1)}, u32[]{:S(2)}, u32[]{:S(2)}) collective-permute-start(bf16[512,384]{1,0:T(8,128)(2,1)S(1)} %collective-permute-done.2.own), channel_id=1, source_target_pairs={{0,128},{128,256},{256,384},{384,0},{1,129},{129,257},{257,385},{3... | collective-permute-start | bytes 1179656 | tf_op jit(solution)/shard_map/ppermute | solution.py:336
  31.6 10.3 %copy-start.9 = (bf16[512,384]{1,0:T(8,128)(2,1)}, bf16[512,384]{1,0:T(8,128)(2,1)S(1)}, u32[]{:S(2)}) copy-start(bf16[512,384]{1,0:T(8,128)(2,1)S(1)} %collective-permute-done.4.right) | copy-start | bytes 1179652
  31.6 8.8 %collective-permute-start.6 = (bf16[256,384]{1,0:T(8,128)(2,1)S(1)}, bf16[256,384]{1,0:T(8,128)(2,1)S(1)}, u32[]{:S(2)}, u32[]{:S(2)}) collective-permute-start(bf16[256,384]{1,0:T(8,128)(2,1)S(1)} %slice.53), channel_id=1, source_target_pairs={{0,384},{128,0},{256,128},{384,256},{1,385},{129,1},{257,129},{385... | collective-permute-start | bytes 589832 | tf_op jit(solution)/shard_map/ppermute | solution.py:339
  33.6 8.4 %copy-start.10 = (bf16[512,384]{1,0:T(8,128)(2,1)}, bf16[512,384]{1,0:T(8,128)(2,1)S(1)}, u32[]{:S(2)}) copy-start(bf16[512,384]{1,0:T(8,128)(2,1)S(1)} %collective-permute-done.3.left) | copy-start | bytes 1179652
  33.6 8.3 %collective-permute-start.5 = (bf16[256,384]{1,0:T(8,128)(2,1)S(1)}, bf16[256,384]{1,0:T(8,128)(2,1)S(1)}, u32[]{:S(2)}, u32[]{:S(2)}) collective-permute-start(bf16[256,384]{1,0:T(8,128)(2,1)S(1)} %slice.52), channel_id=1, source_target_pairs={{0,128},{128,256},{256,384},{384,0},{1,129},{129,257},{257,385},{3... | collective-permute-start | bytes 589832 | tf_op jit(solution)/shard_map/ppermute | solution.py:338
  40.4 1.5 copy-start.16
  41.9 0.7 copy-start.17
  46.0 52.2 %collective-permute-start.7 = (bf16[2048,384]{1,0:T(8,128)(2,1)}, bf16[2048,384]{1,0:T(8,128)(2,1)S(1)}, u32[]{:S(2)}, u32[]{:S(2)}) collective-permute-start(bf16[2048,384]{1,0:T(8,128)(2,1)} %join.1.refs_3_.refs_2_.weights_a), channel_id=1, source_target_pairs={{0,64},{64,0},{1,65},{65,1},{2,66},{66,2},{3,67},{67,3},{4,68},{68... | collective-permute-start | bytes 4718600 | tf_op jit(solution)/shard_map/ppermute | solution.py:373
  73.0 25.1 %copy-start.1 = (bf16[16,8,2048]{2,1,0:T(8,128)(2,1)}, bf16[16,8,2048]{2,1,0:T(8,128)(2,1)S(1)}, u32[]{:S(2)}) copy-start(bf16[16,8,2048]{2,1,0:T(8,128)(2,1)S(1)} %all-to-all-done) | copy-start | bytes 1572868
  73.0 16.0 %collective-permute-start.1 = (bf16[128,2048]{1,0:T(8,128)(2,1)S(1)}, bf16[128,2048]{1,0:T(8,128)(2,1)S(1)}, u32[]{:S(2)}, u32[]{:S(2)}) collective-permute-start(bf16[128,2048]{1,0:T(8,128)(2,1)S(1)} %bitcast.17), channel_id=1, source_target_pairs={{0,3},{1,0},{2,1},{3,2},{4,7},{5,4},{6,5},{7,6},{8,11},{9,8},{10,9... | collective-permute-start | bytes 1572872 | tf_op jit(solution)/shard_map/ppermute | solution.py:337
  77.7 17.7 %collective-permute-start = (bf16[128,2048]{1,0:T(8,128)(2,1)S(1)}, bf16[128,2048]{1,0:T(8,128)(2,1)S(1)}, u32[]{:S(2)}, u32[]{:S(2)}) collective-permute-start(bf16[128,2048]{1,0:T(8,128)(2,1)S(1)} %bitcast.18), channel_id=1, source_target_pairs={{0,1},{1,2},{2,3},{3,0},{4,5},{5,6},{6,7},{7,4},{8,9},{9,10},{10,1... | collective-permute-start | bytes 1572872 | tf_op jit(solution)/shard_map/ppermute | solution.py:336
  89.1 9.1 %copy-start.2 = (bf16[128,2048]{1,0:T(8,128)(2,1)}, bf16[128,2048]{1,0:T(8,128)(2,1)S(1)}, u32[]{:S(2)}) copy-start(bf16[128,2048]{1,0:T(8,128)(2,1)S(1)} %collective-permute-done.1.refs_2_.right) | copy-start | bytes 1572868
  89.8 19.8 %collective-permute-start.10 = (bf16[64,2048]{1,0:T(8,128)(2,1)}, bf16[64,2048]{1,0:T(8,128)(2,1)S(1)}, u32[]{:S(2)}, u32[]{:S(2)}) collective-permute-start(bf16[64,2048]{1,0:T(8,128)(2,1)} %slice.55), channel_id=1, source_target_pairs={{0,3},{1,0},{2,1},{3,2},{4,7},{5,4},{6,5},{7,6},{8,11},{9,8},{10,9... | collective-permute-start | bytes 786440 | tf_op jit(solution)/shard_map/ppermute | solution.py:339
  95.4 2.7 %copy-start.3 = (bf16[128,2048]{1,0:T(8,128)(2,1)}, bf16[128,2048]{1,0:T(8,128)(2,1)S(1)}, u32[]{:S(2)}) copy-start(bf16[128,2048]{1,0:T(8,128)(2,1)S(1)} %collective-permute-done.refs_1_.left) | copy-start | bytes 1572868
  96.2 13.4 %collective-permute-start.9 = (bf16[64,2048]{1,0:T(8,128)(2,1)}, bf16[64,2048]{1,0:T(8,128)(2,1)}, u32[]{:S(2)}, u32[]{:S(2)}) collective-permute-start(bf16[64,2048]{1,0:T(8,128)(2,1)} %slice.54), channel_id=1, source_target_pairs={{0,1},{1,2},{2,3},{3,0},{4,5},{5,6},{6,7},{7,4},{8,9},{9,10},{10,1... | collective-permute-start | bytes 786440 | tf_op jit(solution)/shard_map/ppermute | solution.py:338
  98.2 1.2 copy-start
  105.0 11.4 %copy-start.15 = (f32[192,384]{1,0:T(8,128)S(1)}, f32[192,384]{1,0:T(8,128)}, u32[]{:S(2)}) copy-start(f32[192,384]{1,0:T(8,128)} %get-tuple-element.16) | copy-start | bytes 884740
  105.0 11.4 %collective-permute-start.8 = (bf16[192,384]{1,0:T(8,128)(2,1)}, bf16[192,384]{1,0:T(8,128)(2,1)S(1)}, u32[]{:S(2)}, u32[]{:S(2)}) collective-permute-start(bf16[192,384]{1,0:T(8,128)(2,1)} %get-tuple-element.17), channel_id=1, source_target_pairs={{0,4},{4,0},{8,12},{12,8},{16,20},{20,16},{24,28},{28,24},{32,36},... | collective-permute-start | bytes 442376 | tf_op jit(solution)/shard_map/ppermute | solution.py:379
  109.6 0.7 copy-start.5
  114.4 6.2 %collective-permute-start.11 = (bf16[64,384]{1,0:T(8,128)(2,1)}, bf16[64,384]{1,0:T(8,128)(2,1)S(1)}, u32[]{:S(2)}, u32[]{:S(2)}) collective-permute-start(bf16[64,384]{1,0:T(8,128)(2,1)} %get-tuple-element.19), channel_id=1, source_target_pairs={{0,4},{4,0},{8,12},{12,8},{16,20},{20,16},{24,28},{28,24},{32,36},... | collective-permute-start | bytes 147464 | tf_op jit(solution)/shard_map/ppermute | solution.py:379
  121.7 7.6 %copy-start.4 = (bf16[256,384]{1,0:T(8,128)(2,1)}, bf16[256,384]{1,0:T(8,128)(2,1)S(1)}, u32[]{:S(2)}) copy-start(bf16[256,384]{1,0:T(8,128)(2,1)S(1)} %pad_maximum_fusion.2.mine) | copy-start | bytes 589828
  121.7 7.6 %collective-permute-start.12 = (bf16[256,384]{1,0:T(8,128)(2,1)S(1)}, bf16[256,384]{1,0:T(8,128)(2,1)S(1)}, u32[]{:S(2)}, u32[]{:S(2)}) collective-permute-start(bf16[256,384]{1,0:T(8,128)(2,1)S(1)} %pad_maximum_fusion.2.mine), channel_id=1, source_target_pairs={{0,4},{4,0},{8,12},{12,8},{16,20},{20,16},{24,28},{28,24},{32,36},... | collective-permute-start | bytes 589832 | tf_op jit(solution)/shard_map/ppermute | solution.py:382
  129.3 0.7 copy-start.6
  134.7 5.5 %collective-permute-start.13 = (bf16[4,512,384]{2,1,0:T(8,128)(2,1)}, bf16[4,512,384]{2,1,0:T(8,128)(2,1)S(1)}, u32[]{:S(2)}, u32[]{:S(2)}) collective-permute-start(bf16[4,512,384]{2,1,0:T(8,128)(2,1)} %shard_map.96), channel_id=1, source_target_pairs={{0,64},{64,0},{1,65},{65,1},{2,66},{66,2},{3,67},{67,3},{4,68},{68... | collective-permute-start | bytes 4718600 | tf_op jit(solution)/shard_map/ppermute | solution.py:385
  140.2 1.2 copy-start.7
  146.9 16.2 %collective-permute-start.16 = (bf16[256,384]{1,0:T(8,128)(2,1)}, bf16[256,384]{1,0:T(8,128)(2,1)S(1)}, u32[]{:S(2)}, u32[]{:S(2)}) collective-permute-start(bf16[256,384]{1,0:T(8,128)(2,1)} %get-tuple-element.24), channel_id=1, source_target_pairs={{0,128},{128,256},{256,384},{384,0},{1,129},{129,257},{257,385},{3... | collective-permute-start | bytes 589832 | tf_op jit(solution)/shard_map/ppermute | solution.py:347
  156.5 4.6 %copy-start.11 = (bf16[512,384]{1,0:T(8,128)(2,1)S(1)}, bf16[512,384]{1,0:T(8,128)(2,1)}, u32[]{:S(2)}) copy-start(bf16[512,384]{1,0:T(8,128)(2,1)} %get-tuple-element.21) | copy-start | bytes 1179652
  156.5 4.7 %copy-start.12 = (bf16[512,384]{1,0:T(8,128)(2,1)S(1)}, bf16[512,384]{1,0:T(8,128)(2,1)}, u32[]{:S(2)}) copy-start(bf16[512,384]{1,0:T(8,128)(2,1)} %get-tuple-element.23) | copy-start | bytes 1179652
  156.5 4.7 %copy-start.18 = (bf16[256,384]{1,0:T(8,128)(2,1)S(1)}, bf16[256,384]{1,0:T(8,128)(2,1)}, u32[]{:S(2)}) copy-start(bf16[256,384]{1,0:T(8,128)(2,1)} %get-tuple-element.22) | copy-start | bytes 589828
  156.5 19.7 %all-to-all-start.1 = ((bf16[4,64,2048]{2,1,0:T(8,128)(2,1)}), bf16[4,64,2048]{2,1,0:T(8,128)(2,1)S(1)}, u32[]{:S(2)}, u32[]{:S(2)}) async-start(bf16[4,64,2048]{2,1,0:T(8,128)(2,1)} %back.1), calls=%async_computation.1 | async-start | bytes 2097152 | tf_op jit(solution)/shard_map/all_to_all | solution.py:387
  161.2 9.5 %collective-permute-start.14 = (bf16[256,384]{1,0:T(8,128)(2,1)S(1)}, bf16[256,384]{1,0:T(8,128)(2,1)S(1)}, u32[]{:S(2)}, u32[]{:S(2)}) collective-permute-start(bf16[256,384]{1,0:T(8,128)(2,1)S(1)} %copy-done.18), channel_id=1, source_target_pairs={{0,384},{128,0},{256,128},{384,256},{1,385},{129,1},{257,129},{385... | collective-permute-start | bytes 589832 | tf_op jit(solution)/shard_map/ppermute | solution.py:346
  163.2 26.2 %collective-permute-start.17 = (bf16[512,384]{1,0:T(8,128)(2,1)S(1)}, bf16[512,384]{1,0:T(8,128)(2,1)S(1)}, u32[]{:S(2)}, u32[]{:S(2)}) collective-permute-start(bf16[512,384]{1,0:T(8,128)(2,1)S(1)} %pad_maximum_fusion.1), channel_id=1, source_target_pairs={{0,128},{128,256},{256,384},{384,0},{1,129},{129,257},{257,385},{3... | collective-permute-start | bytes 1179656 | tf_op jit(solution)/shard_map/ppermute | solution.py:353
  170.7 18.7 %copy-start.13 = (bf16[512,384]{1,0:T(8,128)(2,1)S(1)}, bf16[512,384]{1,0:T(8,128)(2,1)}, u32[]{:S(2)}) copy-start(bf16[512,384]{1,0:T(8,128)(2,1)} %get-tuple-element.20) | copy-start | bytes 1179652
  170.8 18.7 %collective-permute-start.15 = (bf16[512,384]{1,0:T(8,128)(2,1)S(1)}, bf16[512,384]{1,0:T(8,128)(2,1)S(1)}, u32[]{:S(2)}, u32[]{:S(2)}) collective-permute-start(bf16[512,384]{1,0:T(8,128)(2,1)S(1)} %pad_maximum_fusion), channel_id=1, source_target_pairs={{0,384},{128,0},{256,128},{384,256},{1,385},{129,1},{257,129},{385... | collective-permute-start | bytes 1179656 | tf_op jit(solution)/shard_map/ppermute | solution.py:352
  177.2 29.6 %all-to-all-start.2 = ((bf16[16,4,2048]{2,1,0:T(4,128)(2,1)}), bf16[16,4,2048]{2,1,0:T(4,128)(2,1)S(1)}, u32[]{:S(2)}, u32[]{:S(2)}) async-start(bf16[16,4,2048]{2,1,0:T(4,128)(2,1)} %reshape.13), calls=%async_computation.2 | async-start | bytes 524288 | tf_op jit(solution)/shard_map/all_to_all | solution.py:394
  189.6 21.2 %collective-permute-start.18 = (bf16[512,384]{1,0:T(8,128)(2,1)S(1)}, bf16[512,384]{1,0:T(8,128)(2,1)S(1)}, u32[]{:S(2)}, u32[]{:S(2)}) collective-permute-start(bf16[512,384]{1,0:T(8,128)(2,1)S(1)} %add_convert_fusion), channel_id=1, source_target_pairs={{0,0},{4,64},{8,8},{12,72},{16,16},{20,80},{24,24},{28,88},{32,32}... | collective-permute-start | bytes 1179656 | tf_op jit(solution)/shard_map/ppermute | solution.py:389
  206.8 0.7 copy-start.8

commit v9 on v8

--- a/solution.py
+++ b/solution.py
@@ -345,10 +345,8 @@
     half = own.shape[0] // 2
     got_a = lax.ppermute(far_a, "y", MINUS).astype(F32)
     got_b = lax.ppermute(far_b, "y", PLUS).astype(F32)
-    near_a = (left[:half].astype(F32) + got_a).astype(BF16)
-    near_b = (right[half:].astype(F32) + got_b).astype(BF16)
-    left = jnp.concatenate([near_a, left[half:]], axis=0)
-    right = jnp.concatenate([right[:half], near_b], axis=0)
+    left = (left.astype(F32) + jnp.pad(got_a, ((0, half), (0, 0)))).astype(BF16)
+    right = (right.astype(F32) + jnp.pad(got_b, ((half, 0), (0, 0)))).astype(BF16)
     left = lax.ppermute(left, "y", MINUS)
     right = lax.ppermute(right, "y", PLUS)
     return (own.astype(F32) + left.astype(F32) + right.astype(F32)).astype(BF16)

time: 215 us -> 213 us (level)
  the two profiles are of different devices: /device:TPU:24 before, /device:TPU:34 now
where the time goes in v9:
time: 213 us; the launch traced here: 212 us
  starting transfers between devices  93.9 us (44%)
  waiting for transfers between devices  69.6 us (33%)
  Pallas kernels  33.9 us (16%)
  local copies, waits for them, and re-layouts  9.63 us (5%)
  other arithmetic  3.61 us (2%)
    ppermute x1, waiting for transfers between devices, work(): piece = lax.ppermute(piece, ('c', 'z'), SWAP)  25 us
    all_to_all x1, waiting for transfers between devices, work(): home = lax.all_to_all(summed.reshape(Z, CAP, HALF), 'z', 0, 0, tiled=True)  15.9 us
    all_to_all x1, starting transfers between devices, work(): got = lax.all_to_all(send, 'z', 0, 0, tiled=True)  15.2 us
    all_to_all x1, starting transfers between devices, work(): home = lax.all_to_all(summed.reshape(Z, CAP, HALF), 'z', 0, 0, tiled=True)  14.1 us
    ppermute x2, waiting for transfers between devices, gathered(): right = lax.ppermute(own, axis, MINUS)  13.7 us
    pallas_call x2, Pallas kernels, grads(): pl.pallas_call(functools.partial(grads_kernel, len(received)), grid_spec=...  10.3 us
    pallas_call x2, Pallas kernels, mix(): pl.pallas_call(functools.partial(mix_kernel, len(blocks)), grid_spec=pltp...  9.78 us
    ppermute x2, starting transfers between devices, gathered(): far_b = lax.ppermute(right[half:], axis, MINUS)  8.3 us
  transfers between devices with their start and end apart: 22, of which 9 were waited for; matrix products, arithmetic and copies ran while one was open for 3% of the time, Pallas kernels for 12%

profile of v9, /device:TPU:34, one launch (start us, length us, event | category | flops | bytes accessed | tf_op | source)
XLA Modules:
  0.0 211.8 jit_solution(5619654375758843211)
XLA Ops:
  0.6 3.2 %send_rows.1 = (bf16[16,8,2048]{2,1,0:T(8,128)(2,1)}, bf16[512,384]{1,0:T(8,128)(2,1)}) custom-call(s32[2,128]{1,0:T(2,128)} %bitcast.24, f32[2,128]{1,0:T(2,128)} %bitcast.26, bf16[128,4096]{1,0:T(8,128)(2,1)} %latent.3, bf16[128,4096]{1,0:T(8,128)(2,1)} %dout.1, f32[1,4096]{1,0:T(1,128)} %bitcast.22, bf16[1,512,256]{2,1,0:T(8,128)(2,1)} %gate_up.1, ...), custom_call_target="tpu_custom_call" | custom-call | tf_op jit(solution)/shard_map/send_rows/pallas_call | solution.py:85
  3.9 15.2 %all-to-all-start = ((bf16[16,8,2048]{2,1,0:T(8,128)(2,1)}), bf16[16,8,2048]{2,1,0:T(8,128)(2,1)S(1)}, u32[]{:S(2)}, u32[]{:S(2)}) async-start(bf16[16,8,2048]{2,1,0:T(8,128)(2,1)} %get-tuple-element.14), calls=%async_computation | async-start | bytes 1048576 | tf_op jit(solution)/shard_map/all_to_all | solution.py:369
  19.1 1.9 collective-permute-start.2
  21.0 25.0 %collective-permute-done.2.own = bf16[512,384]{1,0:T(8,128)(2,1)S(1)} collective-permute-done((bf16[512,384]{1,0:T(8,128)(2,1)}, bf16[512,384]{1,0:T(8,128)(2,1)S(1)}, u32[]{:S(2)}, u32[]{:S(2)}) %collective-permute-start.2) | collective-permute-done | bytes 393248 | tf_op jit(solution)/shard_map/ppermute | solution.py:368
  46.0 4.9 %collective-permute-start.4 = (bf16[512,384]{1,0:T(8,128)(2,1)S(1)}, bf16[512,384]{1,0:T(8,128)(2,1)S(1)}, u32[]{:S(2)}, u32[]{:S(2)}) collective-permute-start(bf16[512,384]{1,0:T(8,128)(2,1)S(1)} %collective-permute-done.2.own), channel_id=1, source_target_pairs={{0,384},{128,0},{256,128},{384,256},{1,385},{129,1},{257,129},{385... | collective-permute-start | bytes 1179656 | tf_op jit(solution)/shard_map/ppermute | solution.py:337
  50.9 1.9 collective-permute-start.3
  52.9 3.3 %collective-permute-done.4.right = bf16[512,384]{1,0:T(8,128)(2,1)S(1)} collective-permute-done((bf16[512,384]{1,0:T(8,128)(2,1)S(1)}, bf16[512,384]{1,0:T(8,128)(2,1)S(1)}, u32[]{:S(2)}, u32[]{:S(2)}) %collective-permute-start.4) | collective-permute-done | bytes 393248 | tf_op jit(solution)/shard_map/ppermute | solution.py:337
  56.2 5.6 %collective-permute-start.6 = (bf16[256,384]{1,0:T(8,128)(2,1)S(1)}, bf16[256,384]{1,0:T(8,128)(2,1)S(1)}, u32[]{:S(2)}, u32[]{:S(2)}) collective-permute-start(bf16[256,384]{1,0:T(8,128)(2,1)S(1)} %slice.37), channel_id=1, source_target_pairs={{0,384},{128,0},{256,128},{384,256},{1,385},{129,1},{257,129},{385... | collective-permute-start | bytes 589832 | tf_op jit(solution)/shard_map/ppermute | solution.py:339
  61.9 1.9 collective-permute-start.5
  65.0 5.7 %collective-permute-done.5.far_a = bf16[256,384]{1,0:T(8,128)(2,1)S(1)} collective-permute-done((bf16[256,384]{1,0:T(8,128)(2,1)S(1)}, bf16[256,384]{1,0:T(8,128)(2,1)S(1)}, u32[]{:S(2)}, u32[]{:S(2)}) %collective-permute-start.5) | collective-permute-done | bytes 196640 | tf_op jit(solution)/shard_map/ppermute | solution.py:338
  71.4 3.4 %join.1.refs_3_.refs_2_.weights_a = bf16[2048,384]{1,0:T(8,128)(2,1)} custom-call(s32[11]{0:T(128)} %concatenate.10.place, bf16[512,384]{1,0:T(8,128)(2,1)} %copy-done.12, bf16[512,384]{1,0:T(8,128)(2,1)} %copy-done.10, bf16[512,384]{1,0:T(8,128)(2,1)} %copy-done.9, bf16[256,384]{1,0:T(8,128)(2,1)} %copy-done.15, bf16[256,384]{1,0:T(8,128)(2,1)} %copy-done.14), custom_call_target="tpu_custom_call" | custom-call | tf_op jit(solution)/shard_map/join/pallas_call | solution.py:101
  74.7 1.9 collective-permute-start.7
  76.7 2.4 %collective-permute-start.1 = (bf16[128,2048]{1,0:T(8,128)(2,1)S(1)}, bf16[128,2048]{1,0:T(8,128)(2,1)S(1)}, u32[]{:S(2)}, u32[]{:S(2)}) collective-permute-start(bf16[128,2048]{1,0:T(8,128)(2,1)S(1)} %bitcast.17), channel_id=1, source_target_pairs={{0,3},{1,0},{2,1},{3,2},{4,7},{5,4},{6,5},{7,6},{8,11},{9,8},{10,9... | collective-permute-start | bytes 1572872 | tf_op jit(solution)/shard_map/ppermute | solution.py:337
  79.1 3.4 %collective-permute-start = (bf16[128,2048]{1,0:T(8,128)(2,1)S(1)}, bf16[128,2048]{1,0:T(8,128)(2,1)S(1)}, u32[]{:S(2)}, u32[]{:S(2)}) collective-permute-start(bf16[128,2048]{1,0:T(8,128)(2,1)S(1)} %bitcast.18), channel_id=1, source_target_pairs={{0,1},{1,2},{2,3},{3,0},{4,5},{5,6},{6,7},{7,4},{8,9},{9,10},{10,1... | collective-permute-start | bytes 1572872 | tf_op jit(solution)/shard_map/ppermute | solution.py:336
  82.5 10.4 %collective-permute-done.1.refs_2_.right = bf16[128,2048]{1,0:T(8,128)(2,1)S(1)} collective-permute-done((bf16[128,2048]{1,0:T(8,128)(2,1)S(1)}, bf16[128,2048]{1,0:T(8,128)(2,1)S(1)}, u32[]{:S(2)}, u32[]{:S(2)}) %collective-permute-start.1) | collective-permute-done | bytes 524320 | tf_op jit(solution)/shard_map/ppermute | solution.py:337
  92.9 0.8 slice.39
  93.7 2.7 %collective-permute-start.10 = (bf16[64,2048]{1,0:T(8,128)(2,1)}, bf16[64,2048]{1,0:T(8,128)(2,1)S(1)}, u32[]{:S(2)}, u32[]{:S(2)}) collective-permute-start(bf16[64,2048]{1,0:T(8,128)(2,1)} %slice.39), channel_id=1, source_target_pairs={{0,3},{1,0},{2,1},{3,2},{4,7},{5,4},{6,5},{7,6},{8,11},{9,8},{10,9... | collective-permute-start | bytes 786440 | tf_op jit(solution)/shard_map/ppermute | solution.py:339
  96.4 0.8 slice.38
  97.2 3.1 %collective-permute-start.9 = (bf16[64,2048]{1,0:T(8,128)(2,1)}, bf16[64,2048]{1,0:T(8,128)(2,1)}, u32[]{:S(2)}, u32[]{:S(2)}) collective-permute-start(bf16[64,2048]{1,0:T(8,128)(2,1)} %slice.38), channel_id=1, source_target_pairs={{0,1},{1,2},{2,3},{3,0},{4,5},{5,6},{6,7},{7,4},{8,9},{9,10},{10,1... | collective-permute-start | bytes 786440 | tf_op jit(solution)/shard_map/ppermute | solution.py:338
  100.3 1.1 copy-done
  101.5 5.6 %shard_map.94 = (f32[192,384]{1,0:T(8,128)}, bf16[192,384]{1,0:T(8,128)(2,1)}) custom-call(s32[11]{0:T(128)} %concatenate.10.place, bf16[128,2048]{1,0:T(8,128)(2,1)} %bitcast.19, bf16[128,2048]{1,0:T(8,128)(2,1)} %copy-done.3, bf16[128,2048]{1,0:T(8,128)(2,1)} %copy-done.2, bf16[2048,384]{1,0:T(8,128)(2,1)} %join.1.refs_3_.refs_2_.weights_a, ...), custom_call_target="tpu_custom_call" | custom-call | tf_op jit(solution)/shard_map/pallas_call | solution.py:203
  107.1 2.0 collective-permute-start.8
  109.9 4.2 %shard_map.95 = (f32[64,384]{1,0:T(8,128)}, bf16[64,384]{1,0:T(8,128)(2,1)}) custom-call(s32[11]{0:T(128)} %concatenate.10.place, bf16[64,2048]{1,0:T(8,128)(2,1)} %collective-permute-done.9.refs_0_.far_a, bf16[64,2048]{1,0:T(8,128)(2,1)} %copy-done.5, bf16[2048,384]{1,0:T(8,128)(2,1)} %join.1.refs_3_.refs_2_.weights_a, bf16[2048,384]{1,0:T(8,128)(2,1)} %copy-done), custom_call_target="tpu_custom_call" | custom-call | tf_op jit(solution)/shard_map/pallas_call | solution.py:203
  114.0 3.9 %collective-permute-start.11 = (bf16[64,384]{1,0:T(8,128)(2,1)}, bf16[64,384]{1,0:T(8,128)(2,1)S(1)}, u32[]{:S(2)}, u32[]{:S(2)}) collective-permute-start(bf16[64,384]{1,0:T(8,128)(2,1)} %get-tuple-element.19), channel_id=1, source_target_pairs={{0,4},{4,0},{8,12},{12,8},{16,20},{20,16},{24,28},{28,24},{32,36},... | collective-permute-start | bytes 147464 | tf_op jit(solution)/shard_map/ppermute | solution.py:377
  118.0 2.2 %collective-permute-done.11 = bf16[64,384]{1,0:T(8,128)(2,1)S(1)} collective-permute-done((bf16[64,384]{1,0:T(8,128)(2,1)}, bf16[64,384]{1,0:T(8,128)(2,1)S(1)}, u32[]{:S(2)}, u32[]{:S(2)}) %collective-permute-start.11) | collective-permute-done | bytes 49184 | tf_op jit(solution)/shard_map/ppermute | solution.py:377
  120.2 0.9 convert_add_fusion.1
  121.3 3.9 %collective-permute-start.12 = (bf16[256,384]{1,0:T(8,128)(2,1)S(1)}, bf16[256,384]{1,0:T(8,128)(2,1)S(1)}, u32[]{:S(2)}, u32[]{:S(2)}) collective-permute-start(bf16[256,384]{1,0:T(8,128)(2,1)S(1)} %pad_maximum_fusion.mine), channel_id=1, source_target_pairs={{0,4},{4,0},{8,12},{12,8},{16,20},{20,16},{24,28},{28,24},{32,36},... | collective-permute-start | bytes 589832 | tf_op jit(solution)/shard_map/ppermute | solution.py:380
  125.2 3.6 %collective-permute-done.12.other = bf16[256,384]{1,0:T(8,128)(2,1)S(1)} collective-permute-done((bf16[256,384]{1,0:T(8,128)(2,1)S(1)}, bf16[256,384]{1,0:T(8,128)(2,1)S(1)}, u32[]{:S(2)}, u32[]{:S(2)}) %collective-permute-start.12) | collective-permute-done | bytes 196640 | tf_op jit(solution)/shard_map/ppermute | solution.py:380
  129.6 4.7 %shard_map.96 = bf16[4,512,384]{2,1,0:T(8,128)(2,1)} custom-call(s32[11]{0:T(128)} %concatenate.10.place, bf16[256,384]{1,0:T(8,128)(2,1)} %copy-done.4, bf16[256,384]{1,0:T(8,128)(2,1)} %copy-done.6, bf16[128,2048]{1,0:T(8,128)(2,1)} %bitcast.20, bf16[128,2048]{1,0:T(8,128)(2,1)} %copy-done.3, bf16[128,2048]{1,0:T(8,128)(2,1)} %copy-done.2, ...), custom_call_target="tpu_custom_call" | custom-call | tf_op jit(solution)/shard_map/pallas_call | solution.py:317
  134.2 1.9 collective-permute-start.13
  136.1 3.9 %back.1 = bf16[4,64,2048]{2,1,0:T(8,128)(2,1)} custom-call(s32[11]{0:T(128)} %concatenate.10.place, bf16[256,384]{1,0:T(8,128)(2,1)} %copy-done.4, bf16[256,384]{1,0:T(8,128)(2,1)} %copy-done.6, bf16[2048,384]{1,0:T(8,128)(2,1)} %join.1.refs_3_.refs_2_.weights_a, bf16[2048,384]{1,0:T(8,128)(2,1)} %copy-done), custom_call_target="tpu_custom_call" | custom-call | tf_op jit(solution)/shard_map/back/pallas_call | solution.py:253
  140.1 7.0 %all-to-all-start.1 = ((bf16[4,64,2048]{2,1,0:T(8,128)(2,1)}), bf16[4,64,2048]{2,1,0:T(8,128)(2,1)S(1)}, u32[]{:S(2)}, u32[]{:S(2)}) async-start(bf16[4,64,2048]{2,1,0:T(8,128)(2,1)} %back.1), calls=%async_computation.1 | async-start | bytes 2097152 | tf_op jit(solution)/shard_map/all_to_all | solution.py:385
  147.1 1.2 copy-done.7
  148.2 5.6 %shard_map.97 = (bf16[512,384]{1,0:T(8,128)(2,1)}, bf16[512,384]{1,0:T(8,128)(2,1)}, bf16[512,384]{1,0:T(8,128)(2,1)}, bf16[256,384]{1,0:T(8,128)(2,1)}, bf16[256,384]{1,0:T(8,128)(2,1)}) custom-call(s32[11]{0:T(128)} %concatenate.10.place, bf16[256,384]{1,0:T(8,128)(2,1)} %copy-done.4, bf16[256,384]{1,0:T(8,128)(2,1)} %copy-done.6, ...), custom_call_target="tpu_custom_call" | custom-call | tf_op jit(solution)/shard_map/pallas_call | solution.py:317
  153.8 1.9 collective-permute-start.16
  155.8 5.1 %collective-permute-start.14 = (bf16[256,384]{1,0:T(8,128)(2,1)}, bf16[256,384]{1,0:T(8,128)(2,1)S(1)}, u32[]{:S(2)}, u32[]{:S(2)}) collective-permute-start(bf16[256,384]{1,0:T(8,128)(2,1)} %get-tuple-element.22), channel_id=1, source_target_pairs={{0,384},{128,0},{256,128},{384,256},{1,385},{129,1},{257,129},{385... | collective-permute-start | bytes 589832 | tf_op jit(solution)/shard_map/ppermute | solution.py:346
  160.9 3.0 %collective-permute-done.16 = bf16[256,384]{1,0:T(8,128)(2,1)S(1)} collective-permute-done((bf16[256,384]{1,0:T(8,128)(2,1)}, bf16[256,384]{1,0:T(8,128)(2,1)S(1)}, u32[]{:S(2)}, u32[]{:S(2)}) %collective-permute-start.16) | collective-permute-done | bytes 196640 | tf_op jit(solution)/shard_map/ppermute | solution.py:347
  163.9 1.1 add_convert_fusion.1
  164.9 1.9 collective-permute-start.17
  166.9 1.1 add_convert_fusion.2
  168.0 5.1 %collective-permute-start.15 = (bf16[512,384]{1,0:T(8,128)(2,1)S(1)}, bf16[512,384]{1,0:T(8,128)(2,1)S(1)}, u32[]{:S(2)}, u32[]{:S(2)}) collective-permute-start(bf16[512,384]{1,0:T(8,128)(2,1)S(1)} %add_convert_fusion.2), channel_id=1, source_target_pairs={{0,384},{128,0},{256,128},{384,256},{1,385},{129,1},{257,129},{385... | collective-permute-start | bytes 1179656 | tf_op jit(solution)/shard_map/ppermute | solution.py:350
  173.4 0.8 reshape.13
  174.2 14.1 %all-to-all-start.2 = ((bf16[16,4,2048]{2,1,0:T(4,128)(2,1)}), bf16[16,4,2048]{2,1,0:T(4,128)(2,1)S(1)}, u32[]{:S(2)}, u32[]{:S(2)}) async-start(bf16[16,4,2048]{2,1,0:T(4,128)(2,1)} %reshape.13), calls=%async_computation.2 | async-start | bytes 524288 | tf_op jit(solution)/shard_map/all_to_all | solution.py:392
  188.5 1.9 collective-permute-start.18
  190.4 15.9 %all-to-all-done.2.home = bf16[16,4,2048]{2,1,0:T(4,128)(2,1)S(1)} async-done(((bf16[16,4,2048]{2,1,0:T(4,128)(2,1)}), bf16[16,4,2048]{2,1,0:T(4,128)(2,1)S(1)}, u32[]{:S(2)}, u32[]{:S(2)}) %all-to-all-start.2) | async-done | bytes 262176 | tf_op jit(solution)/shard_map/all_to_all | solution.py:392
  207.0 3.3 %home_rows.1 = bf16[128,4096]{1,0:T(8,128)(2,1)} custom-call(s32[2,128]{1,0:T(2,128)} %bitcast.25, bf16[128,4096]{1,0:T(8,128)(2,1)} %latent.3, f32[1,4096]{1,0:T(1,128)} %bitcast.23, bf16[16,4,2048]{2,1,0:T(4,128)(2,1)} %copy-done.8), custom_call_target="tpu_custom_call" | custom-call | tf_op jit(solution)/shard_map/home_rows/pallas_call | solution.py:134
  210.3 0.8 copy.10
  211.1 0.7 slice_bitcast_fusion
  (55 shorter events, 4.5 us)
Async XLA Ops:
  3.9 72.8 %all-to-all-start = ((bf16[16,8,2048]{2,1,0:T(8,128)(2,1)}), bf16[16,8,2048]{2,1,0:T(8,128)(2,1)S(1)}, u32[]{:S(2)}, u32[]{:S(2)}) async-start(bf16[16,8,2048]{2,1,0:T(8,128)(2,1)} %get-tuple-element.14), calls=%async_computation | async-start | bytes 1048576 | tf_op jit(solution)/shard_map/all_to_all | solution.py:369
  19.1 26.9 %collective-permute-start.2 = (bf16[512,384]{1,0:T(8,128)(2,1)}, bf16[512,384]{1,0:T(8,128)(2,1)S(1)}, u32[]{:S(2)}, u32[]{:S(2)}) collective-permute-start(bf16[512,384]{1,0:T(8,128)(2,1)} %get-tuple-element.15), channel_id=1, source_target_pairs={{0,0},{4,64},{8,8},{12,72},{16,16},{20,80},{24,24},{28,88},{32,32}... | collective-permute-start | bytes 1179656 | tf_op jit(solution)/shard_map/ppermute | solution.py:368
  46.0 24.7 %copy-start.12 = (bf16[512,384]{1,0:T(8,128)(2,1)}, bf16[512,384]{1,0:T(8,128)(2,1)S(1)}, u32[]{:S(2)}) copy-start(bf16[512,384]{1,0:T(8,128)(2,1)S(1)} %collective-permute-done.2.own) | copy-start | bytes 1179652
  46.0 10.2 %collective-permute-start.4 = (bf16[512,384]{1,0:T(8,128)(2,1)S(1)}, bf16[512,384]{1,0:T(8,128)(2,1)S(1)}, u32[]{:S(2)}, u32[]{:S(2)}) collective-permute-start(bf16[512,384]{1,0:T(8,128)(2,1)S(1)} %collective-permute-done.2.own), channel_id=1, source_target_pairs={{0,384},{128,0},{256,128},{384,256},{1,385},{129,1},{257,129},{385... | collective-permute-start | bytes 1179656 | tf_op jit(solution)/shard_map/ppermute | solution.py:337
  50.9 10.9 %collective-permute-start.3 = (bf16[512,384]{1,0:T(8,128)(2,1)S(1)}, bf16[512,384]{1,0:T(8,128)(2,1)S(1)}, u32[]{:S(2)}, u32[]{:S(2)}) collective-permute-start(bf16[512,384]{1,0:T(8,128)(2,1)S(1)} %collective-permute-done.2.own), channel_id=1, source_target_pairs={{0,128},{128,256},{256,384},{384,0},{1,129},{129,257},{257,385},{3... | collective-permute-start | bytes 1179656 | tf_op jit(solution)/shard_map/ppermute | solution.py:336
  56.2 14.5 %copy-start.9 = (bf16[512,384]{1,0:T(8,128)(2,1)}, bf16[512,384]{1,0:T(8,128)(2,1)S(1)}, u32[]{:S(2)}) copy-start(bf16[512,384]{1,0:T(8,128)(2,1)S(1)} %collective-permute-done.4.right) | copy-start | bytes 1179652
  56.2 8.8 %collective-permute-start.6 = (bf16[256,384]{1,0:T(8,128)(2,1)S(1)}, bf16[256,384]{1,0:T(8,128)(2,1)S(1)}, u32[]{:S(2)}, u32[]{:S(2)}) collective-permute-start(bf16[256,384]{1,0:T(8,128)(2,1)S(1)} %slice.37), channel_id=1, source_target_pairs={{0,384},{128,0},{256,128},{384,256},{1,385},{129,1},{257,129},{385... | collective-permute-start | bytes 589832 | tf_op jit(solution)/shard_map/ppermute | solution.py:339
  61.9 8.8 %copy-start.10 = (bf16[512,384]{1,0:T(8,128)(2,1)}, bf16[512,384]{1,0:T(8,128)(2,1)S(1)}, u32[]{:S(2)}) copy-start(bf16[512,384]{1,0:T(8,128)(2,1)S(1)} %collective-permute-done.3.left) | copy-start | bytes 1179652
  61.9 8.8 %collective-permute-start.5 = (bf16[256,384]{1,0:T(8,128)(2,1)S(1)}, bf16[256,384]{1,0:T(8,128)(2,1)S(1)}, u32[]{:S(2)}, u32[]{:S(2)}) collective-permute-start(bf16[256,384]{1,0:T(8,128)(2,1)S(1)} %slice.36), channel_id=1, source_target_pairs={{0,128},{128,256},{256,384},{384,0},{1,129},{129,257},{257,385},{3... | collective-permute-start | bytes 589832 | tf_op jit(solution)/shard_map/ppermute | solution.py:338
  65.0 5.7 %copy-start.14 = (bf16[256,384]{1,0:T(8,128)(2,1)}, bf16[256,384]{1,0:T(8,128)(2,1)S(1)}, u32[]{:S(2)}) copy-start(bf16[256,384]{1,0:T(8,128)(2,1)S(1)} %collective-permute-done.6.far_b) | copy-start | bytes 589828
  70.7 0.7 copy-start.15
  74.7 25.6 %collective-permute-start.7 = (bf16[2048,384]{1,0:T(8,128)(2,1)}, bf16[2048,384]{1,0:T(8,128)(2,1)S(1)}, u32[]{:S(2)}, u32[]{:S(2)}) collective-permute-start(bf16[2048,384]{1,0:T(8,128)(2,1)} %join.1.refs_3_.refs_2_.weights_a), channel_id=1, source_target_pairs={{0,64},{64,0},{1,65},{65,1},{2,66},{66,2},{3,67},{67,3},{4,68},{68... | collective-permute-start | bytes 4718600 | tf_op jit(solution)/shard_map/ppermute | solution.py:371
  76.7 23.6 %copy-start.1 = (bf16[16,8,2048]{2,1,0:T(8,128)(2,1)}, bf16[16,8,2048]{2,1,0:T(8,128)(2,1)S(1)}, u32[]{:S(2)}) copy-start(bf16[16,8,2048]{2,1,0:T(8,128)(2,1)S(1)} %all-to-all-done) | copy-start | bytes 1572868
  76.7 16.2 %collective-permute-start.1 = (bf16[128,2048]{1,0:T(8,128)(2,1)S(1)}, bf16[128,2048]{1,0:T(8,128)(2,1)S(1)}, u32[]{:S(2)}, u32[]{:S(2)}) collective-permute-start(bf16[128,2048]{1,0:T(8,128)(2,1)S(1)} %bitcast.17), channel_id=1, source_target_pairs={{0,3},{1,0},{2,1},{3,2},{4,7},{5,4},{6,5},{7,6},{8,11},{9,8},{10,9... | collective-permute-start | bytes 1572872 | tf_op jit(solution)/shard_map/ppermute | solution.py:337
  79.1 17.3 %collective-permute-start = (bf16[128,2048]{1,0:T(8,128)(2,1)S(1)}, bf16[128,2048]{1,0:T(8,128)(2,1)S(1)}, u32[]{:S(2)}, u32[]{:S(2)}) collective-permute-start(bf16[128,2048]{1,0:T(8,128)(2,1)S(1)} %bitcast.18), channel_id=1, source_target_pairs={{0,1},{1,2},{2,3},{3,0},{4,5},{5,6},{6,7},{7,4},{8,9},{9,10},{10,1... | collective-permute-start | bytes 1572872 | tf_op jit(solution)/shard_map/ppermute | solution.py:336
  92.9 7.4 %copy-start.2 = (bf16[128,2048]{1,0:T(8,128)(2,1)}, bf16[128,2048]{1,0:T(8,128)(2,1)S(1)}, u32[]{:S(2)}) copy-start(bf16[128,2048]{1,0:T(8,128)(2,1)S(1)} %collective-permute-done.1.refs_2_.right) | copy-start | bytes 1572868
  93.7 15.5 %collective-permute-start.10 = (bf16[64,2048]{1,0:T(8,128)(2,1)}, bf16[64,2048]{1,0:T(8,128)(2,1)S(1)}, u32[]{:S(2)}, u32[]{:S(2)}) collective-permute-start(bf16[64,2048]{1,0:T(8,128)(2,1)} %slice.39), channel_id=1, source_target_pairs={{0,3},{1,0},{2,1},{3,2},{4,7},{5,4},{6,5},{7,6},{8,11},{9,8},{10,9... | collective-permute-start | bytes 786440 | tf_op jit(solution)/shard_map/ppermute | solution.py:339
  96.4 3.9 %copy-start.3 = (bf16[128,2048]{1,0:T(8,128)(2,1)}, bf16[128,2048]{1,0:T(8,128)(2,1)S(1)}, u32[]{:S(2)}) copy-start(bf16[128,2048]{1,0:T(8,128)(2,1)S(1)} %collective-permute-done.refs_1_.left) | copy-start | bytes 1572868
  97.2 12.0 %collective-permute-start.9 = (bf16[64,2048]{1,0:T(8,128)(2,1)}, bf16[64,2048]{1,0:T(8,128)(2,1)}, u32[]{:S(2)}, u32[]{:S(2)}) collective-permute-start(bf16[64,2048]{1,0:T(8,128)(2,1)} %slice.38), channel_id=1, source_target_pairs={{0,1},{1,2},{2,3},{3,0},{4,5},{5,6},{6,7},{7,4},{8,9},{9,10},{10,1... | collective-permute-start | bytes 786440 | tf_op jit(solution)/shard_map/ppermute | solution.py:338
  100.3 1.2 copy-start
  107.1 10.9 %copy-start.13 = (f32[192,384]{1,0:T(8,128)S(1)}, f32[192,384]{1,0:T(8,128)}, u32[]{:S(2)}) copy-start(f32[192,384]{1,0:T(8,128)} %get-tuple-element.16) | copy-start | bytes 884740
  107.1 10.8 %collective-permute-start.8 = (bf16[192,384]{1,0:T(8,128)(2,1)}, bf16[192,384]{1,0:T(8,128)(2,1)S(1)}, u32[]{:S(2)}, u32[]{:S(2)}) collective-permute-start(bf16[192,384]{1,0:T(8,128)(2,1)} %get-tuple-element.17), channel_id=1, source_target_pairs={{0,4},{4,0},{8,12},{12,8},{16,20},{20,16},{24,28},{28,24},{32,36},... | collective-permute-start | bytes 442376 | tf_op jit(solution)/shard_map/ppermute | solution.py:377
  109.2 0.7 copy-start.5
  114.0 6.2 %collective-permute-start.11 = (bf16[64,384]{1,0:T(8,128)(2,1)}, bf16[64,384]{1,0:T(8,128)(2,1)S(1)}, u32[]{:S(2)}, u32[]{:S(2)}) collective-permute-start(bf16[64,384]{1,0:T(8,128)(2,1)} %get-tuple-element.19), channel_id=1, source_target_pairs={{0,4},{4,0},{8,12},{12,8},{16,20},{20,16},{24,28},{28,24},{32,36},... | collective-permute-start | bytes 147464 | tf_op jit(solution)/shard_map/ppermute | solution.py:377
  121.3 7.6 %copy-start.4 = (bf16[256,384]{1,0:T(8,128)(2,1)}, bf16[256,384]{1,0:T(8,128)(2,1)S(1)}, u32[]{:S(2)}) copy-start(bf16[256,384]{1,0:T(8,128)(2,1)S(1)} %pad_maximum_fusion.mine) | copy-start | bytes 589828
  121.3 7.6 %collective-permute-start.12 = (bf16[256,384]{1,0:T(8,128)(2,1)S(1)}, bf16[256,384]{1,0:T(8,128)(2,1)S(1)}, u32[]{:S(2)}, u32[]{:S(2)}) collective-permute-start(bf16[256,384]{1,0:T(8,128)(2,1)S(1)} %pad_maximum_fusion.mine), channel_id=1, source_target_pairs={{0,4},{4,0},{8,12},{12,8},{16,20},{20,16},{24,28},{28,24},{32,36},... | collective-permute-start | bytes 589832 | tf_op jit(solution)/shard_map/ppermute | solution.py:380
  128.9 0.7 copy-start.6
  134.2 12.8 %collective-permute-start.13 = (bf16[4,512,384]{2,1,0:T(8,128)(2,1)}, bf16[4,512,384]{2,1,0:T(8,128)(2,1)S(1)}, u32[]{:S(2)}, u32[]{:S(2)}) collective-permute-start(bf16[4,512,384]{2,1,0:T(8,128)(2,1)} %shard_map.96), channel_id=1, source_target_pairs={{0,64},{64,0},{1,65},{65,1},{2,66},{66,2},{3,67},{67,3},{4,68},{68... | collective-permute-start | bytes 4718600 | tf_op jit(solution)/shard_map/ppermute | solution.py:383
  140.1 33.1 %all-to-all-start.1 = ((bf16[4,64,2048]{2,1,0:T(8,128)(2,1)}), bf16[4,64,2048]{2,1,0:T(8,128)(2,1)S(1)}, u32[]{:S(2)}, u32[]{:S(2)}) async-start(bf16[4,64,2048]{2,1,0:T(8,128)(2,1)} %back.1), calls=%async_computation.1 | async-start | bytes 2097152 | tf_op jit(solution)/shard_map/all_to_all | solution.py:385
  147.1 1.2 copy-start.7
  153.8 10.0 %collective-permute-start.16 = (bf16[256,384]{1,0:T(8,128)(2,1)}, bf16[256,384]{1,0:T(8,128)(2,1)S(1)}, u32[]{:S(2)}, u32[]{:S(2)}) collective-permute-start(bf16[256,384]{1,0:T(8,128)(2,1)} %get-tuple-element.24), channel_id=1, source_target_pairs={{0,128},{128,256},{256,384},{384,0},{1,129},{129,257},{257,385},{3... | collective-permute-start | bytes 589832 | tf_op jit(solution)/shard_map/ppermute | solution.py:347
  155.8 11.1 %collective-permute-start.14 = (bf16[256,384]{1,0:T(8,128)(2,1)}, bf16[256,384]{1,0:T(8,128)(2,1)S(1)}, u32[]{:S(2)}, u32[]{:S(2)}) collective-permute-start(bf16[256,384]{1,0:T(8,128)(2,1)} %get-tuple-element.22), channel_id=1, source_target_pairs={{0,384},{128,0},{256,128},{384,256},{1,385},{129,1},{257,129},{385... | collective-permute-start | bytes 589832 | tf_op jit(solution)/shard_map/ppermute | solution.py:346
  164.9 23.3 %collective-permute-start.17 = (bf16[512,384]{1,0:T(8,128)(2,1)S(1)}, bf16[512,384]{1,0:T(8,128)(2,1)S(1)}, u32[]{:S(2)}, u32[]{:S(2)}) collective-permute-start(bf16[512,384]{1,0:T(8,128)(2,1)S(1)} %add_convert_fusion.1), channel_id=1, source_target_pairs={{0,128},{128,256},{256,384},{384,0},{1,129},{129,257},{257,385},{3... | collective-permute-start | bytes 1179656 | tf_op jit(solution)/shard_map/ppermute | solution.py:351
  166.9 21.4 %copy-start.11 = (bf16[512,384]{1,0:T(8,128)(2,1)S(1)}, bf16[512,384]{1,0:T(8,128)(2,1)}, u32[]{:S(2)}) copy-start(bf16[512,384]{1,0:T(8,128)(2,1)} %get-tuple-element.20) | copy-start | bytes 1179652
  168.0 20.3 %collective-permute-start.15 = (bf16[512,384]{1,0:T(8,128)(2,1)S(1)}, bf16[512,384]{1,0:T(8,128)(2,1)S(1)}, u32[]{:S(2)}, u32[]{:S(2)}) collective-permute-start(bf16[512,384]{1,0:T(8,128)(2,1)S(1)} %add_convert_fusion.2), channel_id=1, source_target_pairs={{0,384},{128,0},{256,128},{384,256},{1,385},{129,1},{257,129},{385... | collective-permute-start | bytes 1179656 | tf_op jit(solution)/shard_map/ppermute | solution.py:350
  174.2 32.1 %all-to-all-start.2 = ((bf16[16,4,2048]{2,1,0:T(4,128)(2,1)}), bf16[16,4,2048]{2,1,0:T(4,128)(2,1)S(1)}, u32[]{:S(2)}, u32[]{:S(2)}) async-start(bf16[16,4,2048]{2,1,0:T(4,128)(2,1)} %reshape.13), calls=%async_computation.2 | async-start | bytes 524288 | tf_op jit(solution)/shard_map/all_to_all | solution.py:392
  188.5 21.9 %collective-permute-start.18 = (bf16[512,384]{1,0:T(8,128)(2,1)S(1)}, bf16[512,384]{1,0:T(8,128)(2,1)S(1)}, u32[]{:S(2)}, u32[]{:S(2)}) collective-permute-start(bf16[512,384]{1,0:T(8,128)(2,1)S(1)} %add_convert_fusion), channel_id=1, source_target_pairs={{0,0},{4,64},{8,8},{12,72},{16,16},{20,80},{24,24},{28,88},{32,32}... | collective-permute-start | bytes 1179656 | tf_op jit(solution)/shard_map/ppermute | solution.py:387
  206.3 0.7 copy-start.8

commit v10 on v9

--- a/solution.py
+++ b/solution.py
@@ -18,6 +18,7 @@
 CUT = 512
 WIDE = 2 * CUT
 ROWS = 2 * Z * X * CAP
+ROOM = pltpu.CompilerParams(vmem_limit_bytes=24 << 20)
 F32 = jnp.float32
 BF16 = jnp.bfloat16
 
@@ -86,6 +87,7 @@
         send_kernel,
         out_shape=[shape((Z, 8, HALF), BF16), shape((CUT, 3 * HID), BF16)],
         scratch_shapes=[pltpu.VMEM((2 * GROUPS * CAP, D), F32)],
+        compiler_params=ROOM,
         name="send_rows",
     )(*args)
 
@@ -107,6 +109,7 @@
             out_specs=whole((HALF, 3 * HID)),
         ),
         out_shape=shape((HALF, 3 * HID), BF16),
+        compiler_params=ROOM,
         name="join",
     )(place, *blocks)
 
@@ -135,6 +138,7 @@
         home_kernel,
         out_shape=shape(latent.shape, BF16),
         scratch_shapes=[pltpu.VMEM((GROUPS * CAP, D), F32)],
+        compiler_params=ROOM,
         name="home_rows",
     )(routes, latent, gain, home)
 
@@ -213,6 +217,7 @@
             scratch_shapes=[pltpu.VMEM((2, rows, 3 * HID), F32)],
         ),
         out_shape=[shape(dims, F32), shape(dims, BF16)],
+        compiler_params=ROOM,
     )(place, *blocks, *weights)
 
 
@@ -260,6 +265,7 @@
             scratch_shapes=[pltpu.VMEM((2, *dims), BF16)],
         ),
         out_shape=shape((X, ROWS // 8, HALF), BF16),
+        compiler_params=ROOM,
         name="back",
     )(place, mine, other, *weights)
 
@@ -328,6 +334,7 @@
             if received
             else shape((HALF // CUT, CUT, 3 * HID), BF16)
         ),
+        compiler_params=ROOM,
     )(place, mine, other, *blocks, *received)
 
 

time: 213 us -> 200 us (0.939)
  the two profiles are of different devices: /device:TPU:34 before, /device:TPU:32 now
where the time goes in v10:
time: 200 us; the launch traced here: 199 us
  starting transfers between devices  88.1 us (44%)
  waiting for transfers between devices  77.4 us (39%)
  Pallas kernels  19.7 us (10%)
  local copies, waits for them, and re-layouts  9.85 us (5%)
  other arithmetic  2.63 us (1%)
    ppermute x1, waiting for transfers between devices, work(): piece = lax.ppermute(piece, ('c', 'z'), SWAP)  25 us
    all_to_all x1, waiting for transfers between devices, work(): home = lax.all_to_all(summed.reshape(Z, CAP, HALF), 'z', 0, 0, tiled=True)  16.4 us
    all_to_all x1, starting transfers between devices, work(): got = lax.all_to_all(send, 'z', 0, 0, tiled=True)  15.2 us
    ppermute x2, waiting for transfers between devices, gathered(): right = lax.ppermute(own, axis, MINUS)  13.6 us
    all_to_all x1, starting transfers between devices, work(): home = lax.all_to_all(summed.reshape(Z, CAP, HALF), 'z', 0, 0, tiled=True)  12.6 us
    ppermute x2, starting transfers between devices, gathered(): far_b = lax.ppermute(right[half:], axis, MINUS)  11.1 us
    ppermute x2, starting transfers between devices, gathered(): right = lax.ppermute(own, axis, MINUS)  9.58 us
    ppermute x2, waiting for transfers between devices, gathered(): far_a = lax.ppermute(left[:half], axis, PLUS)  8.36 us
  transfers between devices with their start and end apart: 22, of which 10 were waited for; matrix products, arithmetic and copies ran while one was open for 2% of the time, Pallas kernels for 7%

profile of v10, /device:TPU:32, one launch (start us, length us, event | category | flops | bytes accessed | tf_op | source)
XLA Modules:
  0.0 198.9 jit_solution(18041472714594118833)
XLA Ops:
  0.6 1.2 copy-done.5
  1.9 1.2 copy-done.11
  3.1 0.9 copy-done.12
  4.0 0.9 copy-done.13
  7.0 1.5 send_rows.1
  8.5 15.2 %all-to-all-start = ((bf16[16,8,2048]{2,1,0:T(8,128)(2,1)}), bf16[16,8,2048]{2,1,0:T(8,128)(2,1)}, u32[]{:S(2)}, u32[]{:S(2)}) async-start(bf16[16,8,2048]{2,1,0:T(8,128)(2,1)} %get-tuple-element.14), calls=%async_computation | async-start | bytes 1048576 | tf_op jit(solution)/shard_map/all_to_all | solution.py:376
  23.7 1.9 collective-permute-start.2
  25.6 25.0 %collective-permute-done.2.own = bf16[512,384]{1,0:T(8,128)(2,1)S(1)} collective-permute-done((bf16[512,384]{1,0:T(8,128)(2,1)S(1)}, bf16[512,384]{1,0:T(8,128)(2,1)S(1)}, u32[]{:S(2)}, u32[]{:S(2)}) %collective-permute-start.2) | collective-permute-done | bytes 393248 | tf_op jit(solution)/shard_map/ppermute | solution.py:375
  50.7 4.9 %collective-permute-start.4 = (bf16[512,384]{1,0:T(8,128)(2,1)S(1)}, bf16[512,384]{1,0:T(8,128)(2,1)S(1)}, u32[]{:S(2)}, u32[]{:S(2)}) collective-permute-start(bf16[512,384]{1,0:T(8,128)(2,1)S(1)} %collective-permute-done.2.own), channel_id=1, source_target_pairs={{0,384},{128,0},{256,128},{384,256},{1,385},{129,1},{257,129},{385... | collective-permute-start | bytes 1179656 | tf_op jit(solution)/shard_map/ppermute | solution.py:344
  55.6 1.9 collective-permute-start.3
  57.5 3.3 %collective-permute-done.4.right = bf16[512,384]{1,0:T(8,128)(2,1)S(1)} collective-permute-done((bf16[512,384]{1,0:T(8,128)(2,1)S(1)}, bf16[512,384]{1,0:T(8,128)(2,1)S(1)}, u32[]{:S(2)}, u32[]{:S(2)}) %collective-permute-start.4) | collective-permute-done | bytes 393248 | tf_op jit(solution)/shard_map/ppermute | solution.py:344
  60.9 5.6 %collective-permute-start.6 = (bf16[256,384]{1,0:T(8,128)(2,1)S(1)}, bf16[256,384]{1,0:T(8,128)(2,1)S(1)}, u32[]{:S(2)}, u32[]{:S(2)}) collective-permute-start(bf16[256,384]{1,0:T(8,128)(2,1)S(1)} %slice.37), channel_id=1, source_target_pairs={{0,384},{128,0},{256,128},{384,256},{1,385},{129,1},{257,129},{385... | collective-permute-start | bytes 589832 | tf_op jit(solution)/shard_map/ppermute | solution.py:346
  66.5 1.9 collective-permute-start.5
  68.6 1.0 collective-permute-done.6.far_b
  69.7 5.6 %collective-permute-done.5.far_a = bf16[256,384]{1,0:T(8,128)(2,1)S(1)} collective-permute-done((bf16[256,384]{1,0:T(8,128)(2,1)S(1)}, bf16[256,384]{1,0:T(8,128)(2,1)S(1)}, u32[]{:S(2)}, u32[]{:S(2)}) %collective-permute-start.5) | collective-permute-done | bytes 196640 | tf_op jit(solution)/shard_map/ppermute | solution.py:345
  76.0 1.9 collective-permute-start.7
  77.9 4.7 %collective-permute-start.1 = (bf16[128,2048]{1,0:T(8,128)(2,1)}, bf16[128,2048]{1,0:T(8,128)(2,1)S(1)}, u32[]{:S(2)}, u32[]{:S(2)}) collective-permute-start(bf16[128,2048]{1,0:T(8,128)(2,1)} %bitcast.10.refs_0_.own), channel_id=1, source_target_pairs={{0,3},{1,0},{2,1},{3,2},{4,7},{5,4},{6,5},{7,6},{8,11},{9,8},{10,9... | collective-permute-start | bytes 1572872 | tf_op jit(solution)/shard_map/ppermute | solution.py:344
  82.6 1.9 collective-permute-start
  84.5 10.2 %collective-permute-done.1.refs_2_.right = bf16[128,2048]{1,0:T(8,128)(2,1)S(1)} collective-permute-done((bf16[128,2048]{1,0:T(8,128)(2,1)}, bf16[128,2048]{1,0:T(8,128)(2,1)S(1)}, u32[]{:S(2)}, u32[]{:S(2)}) %collective-permute-start.1) | collective-permute-done | bytes 524320 | tf_op jit(solution)/shard_map/ppermute | solution.py:344
  94.8 5.5 %collective-permute-start.10 = (bf16[64,2048]{1,0:T(8,128)(2,1)S(1)}, bf16[64,2048]{1,0:T(8,128)(2,1)S(1)}, u32[]{:S(2)}, u32[]{:S(2)}) collective-permute-start(bf16[64,2048]{1,0:T(8,128)(2,1)S(1)} %slice.39), channel_id=1, source_target_pairs={{0,3},{1,0},{2,1},{3,2},{4,7},{5,4},{6,5},{7,6},{8,11},{9,8},{10,9... | collective-permute-start | bytes 786440 | tf_op jit(solution)/shard_map/ppermute | solution.py:346
  100.3 1.9 collective-permute-start.9
  102.3 4.1 %shard_map.94 = (f32[192,384]{1,0:T(8,128)S(1)}, bf16[192,384]{1,0:T(8,128)(2,1)S(1)}) custom-call(s32[11]{0:T(128)S(1)} %concatenate.10.place, bf16[128,2048]{1,0:T(8,128)(2,1)} %bitcast.10.refs_0_.own, bf16[128,2048]{1,0:T(8,128)(2,1)S(1)} %collective-permute-done.refs_1_.left, bf16[128,2048]{1,0:T(8,128)(2,1)S(1)} %collective-permute-done.1.refs_2_.right, ...), custom_call_target="tpu_custom_call" | custom-call | tf_op jit(solution)/shard_map/pallas_call | solution.py:207
  106.3 1.9 collective-permute-start.8
  108.3 2.7 %collective-permute-done.9.refs_0_.far_a = bf16[64,2048]{1,0:T(8,128)(2,1)S(1)} collective-permute-done((bf16[64,2048]{1,0:T(8,128)(2,1)S(1)}, bf16[64,2048]{1,0:T(8,128)(2,1)S(1)}, u32[]{:S(2)}, u32[]{:S(2)}) %collective-permute-start.9) | collective-permute-done | bytes 262176 | tf_op jit(solution)/shard_map/ppermute | solution.py:345
  111.0 1.9 shard_map.95
  112.9 1.9 collective-permute-start.11
  114.9 4.0 %collective-permute-done.11 = bf16[64,384]{1,0:T(8,128)(2,1)S(1)} collective-permute-done((bf16[64,384]{1,0:T(8,128)(2,1)S(1)}, bf16[64,384]{1,0:T(8,128)(2,1)S(1)}, u32[]{:S(2)}, u32[]{:S(2)}) %collective-permute-start.11) | collective-permute-done | bytes 49184 | tf_op jit(solution)/shard_map/ppermute | solution.py:384
  119.1 1.9 collective-permute-start.12
  121.0 5.6 %collective-permute-done.12.other = bf16[256,384]{1,0:T(8,128)(2,1)S(1)} collective-permute-done((bf16[256,384]{1,0:T(8,128)(2,1)S(1)}, bf16[256,384]{1,0:T(8,128)(2,1)S(1)}, u32[]{:S(2)}, u32[]{:S(2)}) %collective-permute-start.12) | collective-permute-done | bytes 196640 | tf_op jit(solution)/shard_map/ppermute | solution.py:387
  126.7 4.0 %shard_map.96 = bf16[4,512,384]{2,1,0:T(8,128)(2,1)} custom-call(s32[11]{0:T(128)S(1)} %concatenate.10.place, bf16[256,384]{1,0:T(8,128)(2,1)S(1)} %pad_maximum_fusion.mine, bf16[256,384]{1,0:T(8,128)(2,1)S(1)} %collective-permute-done.12.other, bf16[128,2048]{1,0:T(8,128)(2,1)} %bitcast.10.refs_0_.own, ...), custom_call_target="tpu_custom_call" | custom-call | tf_op jit(solution)/shard_map/pallas_call | solution.py:323
  130.7 1.9 collective-permute-start.13
  132.6 1.6 back.1
  134.3 1.0 copy-done.4
  135.3 4.4 %all-to-all-start.1 = ((bf16[4,64,2048]{2,1,0:T(8,128)(2,1)}), bf16[4,64,2048]{2,1,0:T(8,128)(2,1)}, u32[]{:S(2)}, u32[]{:S(2)}) async-start(bf16[4,64,2048]{2,1,0:T(8,128)(2,1)} %copy-done.4), calls=%async_computation.1 | async-start | bytes 2097152 | tf_op jit(solution)/shard_map/all_to_all | solution.py:392
  139.7 3.8 %shard_map.97 = (bf16[512,384]{1,0:T(8,128)(2,1)S(1)}, bf16[512,384]{1,0:T(8,128)(2,1)S(1)}, bf16[512,384]{1,0:T(8,128)(2,1)S(1)}, bf16[256,384]{1,0:T(8,128)(2,1)S(1)}, bf16[256,384]{1,0:T(8,128)(2,1)S(1)}) custom-call(s32[11]{0:T(128)S(1)} %concatenate.10.place, bf16[256,384]{1,0:T(8,128)(2,1)S(1)} %pad_maximum_fusion.mine, ...), custom_call_target="tpu_custom_call" | custom-call | tf_op jit(solution)/shard_map/pallas_call | solution.py:323
  143.6 1.9 collective-permute-start.16
  145.5 5.1 %collective-permute-start.14 = (bf16[256,384]{1,0:T(8,128)(2,1)S(1)}, bf16[256,384]{1,0:T(8,128)(2,1)S(1)}, u32[]{:S(2)}, u32[]{:S(2)}) collective-permute-start(bf16[256,384]{1,0:T(8,128)(2,1)S(1)} %get-tuple-element.22), channel_id=1, source_target_pairs={{0,384},{128,0},{256,128},{384,256},{1,385},{129,1},{257,129},{385... | collective-permute-start | bytes 589832 | tf_op jit(solution)/shard_map/ppermute | solution.py:353
  150.6 3.3 %collective-permute-done.16 = bf16[256,384]{1,0:T(8,128)(2,1)S(1)} collective-permute-done((bf16[256,384]{1,0:T(8,128)(2,1)S(1)}, bf16[256,384]{1,0:T(8,128)(2,1)S(1)}, u32[]{:S(2)}, u32[]{:S(2)}) %collective-permute-start.16) | collective-permute-done | bytes 196640 | tf_op jit(solution)/shard_map/ppermute | solution.py:354
  154.0 1.9 collective-permute-start.17
  156.0 0.8 add_convert_fusion.2
  156.8 5.1 %collective-permute-start.15 = (bf16[512,384]{1,0:T(8,128)(2,1)}, bf16[512,384]{1,0:T(8,128)(2,1)S(1)}, u32[]{:S(2)}, u32[]{:S(2)}) collective-permute-start(bf16[512,384]{1,0:T(8,128)(2,1)} %add_convert_fusion.2), channel_id=1, source_target_pairs={{0,384},{128,0},{256,128},{384,256},{1,385},{129,1},{257,129},{385... | collective-permute-start | bytes 1179656 | tf_op jit(solution)/shard_map/ppermute | solution.py:357
  161.9 1.4 reduce_sum.12
  163.4 0.8 reshape.13
  164.2 12.6 %all-to-all-start.2 = ((bf16[16,4,2048]{2,1,0:T(4,128)(2,1)}), bf16[16,4,2048]{2,1,0:T(4,128)(2,1)S(1)}, u32[]{:S(2)}, u32[]{:S(2)}) async-start(bf16[16,4,2048]{2,1,0:T(4,128)(2,1)} %reshape.13), calls=%async_computation.2 | async-start | bytes 524288 | tf_op jit(solution)/shard_map/all_to_all | solution.py:399
  177.0 1.9 collective-permute-start.18
  178.9 16.4 %all-to-all-done.2.home = bf16[16,4,2048]{2,1,0:T(4,128)(2,1)S(1)} async-done(((bf16[16,4,2048]{2,1,0:T(4,128)(2,1)}), bf16[16,4,2048]{2,1,0:T(4,128)(2,1)S(1)}, u32[]{:S(2)}, u32[]{:S(2)}) %all-to-all-start.2) | async-done | bytes 262176 | tf_op jit(solution)/shard_map/all_to_all | solution.py:399
  195.3 2.0 %home_rows.1 = bf16[128,4096]{1,0:T(8,128)(2,1)} custom-call(s32[2,128]{1,0:T(2,128)S(1)} %bitcast.20, bf16[128,4096]{1,0:T(8,128)(2,1)S(1)} %copy-done.6, f32[1,4096]{1,0:T(1,128)S(1)} %bitcast.18, bf16[16,4,2048]{2,1,0:T(4,128)(2,1)S(1)} %all-to-all-done.2.home), custom_call_target="tpu_custom_call" | custom-call | tf_op jit(solution)/shard_map/home_rows/pallas_call | solution.py:137
  197.4 0.8 copy.10
  (61 shorter events, 4.1 us)
Async XLA Ops:
  0.6 1.2 copy-start.5
  1.9 1.2 copy-start.11
  3.1 0.9 copy-start.12
  4.0 0.9 copy-start.13
  4.9 0.7 copy-start.14
  5.7 0.7 copy-start.16
  6.3 0.7 copy-start.18
  8.5 69.4 %all-to-all-start = ((bf16[16,8,2048]{2,1,0:T(8,128)(2,1)}), bf16[16,8,2048]{2,1,0:T(8,128)(2,1)}, u32[]{:S(2)}, u32[]{:S(2)}) async-start(bf16[16,8,2048]{2,1,0:T(8,128)(2,1)} %get-tuple-element.14), calls=%async_computation | async-start | bytes 1048576 | tf_op jit(solution)/shard_map/all_to_all | solution.py:376
  23.7 26.9 %collective-permute-start.2 = (bf16[512,384]{1,0:T(8,128)(2,1)S(1)}, bf16[512,384]{1,0:T(8,128)(2,1)S(1)}, u32[]{:S(2)}, u32[]{:S(2)}) collective-permute-start(bf16[512,384]{1,0:T(8,128)(2,1)S(1)} %get-tuple-element.15), channel_id=1, source_target_pairs={{0,0},{4,64},{8,8},{12,72},{16,16},{20,80},{24,24},{28,88},{32,32}... | collective-permute-start | bytes 1179656 | tf_op jit(solution)/shard_map/ppermute | solution.py:375
  50.7 10.2 %collective-permute-start.4 = (bf16[512,384]{1,0:T(8,128)(2,1)S(1)}, bf16[512,384]{1,0:T(8,128)(2,1)S(1)}, u32[]{:S(2)}, u32[]{:S(2)}) collective-permute-start(bf16[512,384]{1,0:T(8,128)(2,1)S(1)} %collective-permute-done.2.own), channel_id=1, source_target_pairs={{0,384},{128,0},{256,128},{384,256},{1,385},{129,1},{257,129},{385... | collective-permute-start | bytes 1179656 | tf_op jit(solution)/shard_map/ppermute | solution.py:344
  55.6 10.9 %collective-permute-start.3 = (bf16[512,384]{1,0:T(8,128)(2,1)S(1)}, bf16[512,384]{1,0:T(8,128)(2,1)S(1)}, u32[]{:S(2)}, u32[]{:S(2)}) collective-permute-start(bf16[512,384]{1,0:T(8,128)(2,1)S(1)} %collective-permute-done.2.own), channel_id=1, source_target_pairs={{0,128},{128,256},{256,384},{384,0},{1,129},{129,257},{257,385},{3... | collective-permute-start | bytes 1179656 | tf_op jit(solution)/shard_map/ppermute | solution.py:343
  60.9 8.8 %collective-permute-start.6 = (bf16[256,384]{1,0:T(8,128)(2,1)S(1)}, bf16[256,384]{1,0:T(8,128)(2,1)S(1)}, u32[]{:S(2)}, u32[]{:S(2)}) collective-permute-start(bf16[256,384]{1,0:T(8,128)(2,1)S(1)} %slice.37), channel_id=1, source_target_pairs={{0,384},{128,0},{256,128},{384,256},{1,385},{129,1},{257,129},{385... | collective-permute-start | bytes 589832 | tf_op jit(solution)/shard_map/ppermute | solution.py:346
  66.5 8.8 %collective-permute-start.5 = (bf16[256,384]{1,0:T(8,128)(2,1)S(1)}, bf16[256,384]{1,0:T(8,128)(2,1)S(1)}, u32[]{:S(2)}, u32[]{:S(2)}) collective-permute-start(bf16[256,384]{1,0:T(8,128)(2,1)S(1)} %slice.36), channel_id=1, source_target_pairs={{0,128},{128,256},{256,384},{384,0},{1,129},{129,257},{257,385},{3... | collective-permute-start | bytes 589832 | tf_op jit(solution)/shard_map/ppermute | solution.py:345
  76.0 26.3 %collective-permute-start.7 = (bf16[2048,384]{1,0:T(8,128)(2,1)S(1)}, bf16[2048,384]{1,0:T(8,128)(2,1)S(1)}, u32[]{:S(2)}, u32[]{:S(2)}) collective-permute-start(bf16[2048,384]{1,0:T(8,128)(2,1)S(1)} %join.1.refs_3_.refs_2_.weights_a), channel_id=1, source_target_pairs={{0,64},{64,0},{1,65},{65,1},{2,66},{66,2},{3,67},{67,3},{4,68},{68... | collective-permute-start | bytes 4718600 | tf_op jit(solution)/shard_map/ppermute | solution.py:378
  77.9 16.8 %collective-permute-start.1 = (bf16[128,2048]{1,0:T(8,128)(2,1)}, bf16[128,2048]{1,0:T(8,128)(2,1)S(1)}, u32[]{:S(2)}, u32[]{:S(2)}) collective-permute-start(bf16[128,2048]{1,0:T(8,128)(2,1)} %bitcast.10.refs_0_.own), channel_id=1, source_target_pairs={{0,3},{1,0},{2,1},{3,2},{4,7},{5,4},{6,5},{7,6},{8,11},{9,8},{10,9... | collective-permute-start | bytes 1572872 | tf_op jit(solution)/shard_map/ppermute | solution.py:344
  82.6 17.7 %collective-permute-start = (bf16[128,2048]{1,0:T(8,128)(2,1)}, bf16[128,2048]{1,0:T(8,128)(2,1)S(1)}, u32[]{:S(2)}, u32[]{:S(2)}) collective-permute-start(bf16[128,2048]{1,0:T(8,128)(2,1)} %bitcast.10.refs_0_.own), channel_id=1, source_target_pairs={{0,1},{1,2},{2,3},{3,0},{4,5},{5,6},{6,7},{7,4},{8,9},{9,10},{10,1... | collective-permute-start | bytes 1572872 | tf_op jit(solution)/shard_map/ppermute | solution.py:343
  94.8 31.9 %copy-start = (bf16[128,2048]{1,0:T(8,128)(2,1)}, bf16[128,2048]{1,0:T(8,128)(2,1)S(1)}, u32[]{:S(2)}) copy-start(bf16[128,2048]{1,0:T(8,128)(2,1)S(1)} %collective-permute-done.1.refs_2_.right) | copy-start | bytes 1572868
  94.8 13.5 %collective-permute-start.10 = (bf16[64,2048]{1,0:T(8,128)(2,1)S(1)}, bf16[64,2048]{1,0:T(8,128)(2,1)S(1)}, u32[]{:S(2)}, u32[]{:S(2)}) collective-permute-start(bf16[64,2048]{1,0:T(8,128)(2,1)S(1)} %slice.39), channel_id=1, source_target_pairs={{0,3},{1,0},{2,1},{3,2},{4,7},{5,4},{6,5},{7,6},{8,11},{9,8},{10,9... | collective-permute-start | bytes 786440 | tf_op jit(solution)/shard_map/ppermute | solution.py:346
  100.3 26.4 %copy-start.2 = (bf16[128,2048]{1,0:T(8,128)(2,1)}, bf16[128,2048]{1,0:T(8,128)(2,1)S(1)}, u32[]{:S(2)}) copy-start(bf16[128,2048]{1,0:T(8,128)(2,1)S(1)} %collective-permute-done.refs_1_.left) | copy-start | bytes 1572868
  100.3 10.7 %collective-permute-start.9 = (bf16[64,2048]{1,0:T(8,128)(2,1)S(1)}, bf16[64,2048]{1,0:T(8,128)(2,1)S(1)}, u32[]{:S(2)}, u32[]{:S(2)}) collective-permute-start(bf16[64,2048]{1,0:T(8,128)(2,1)S(1)} %slice.38), channel_id=1, source_target_pairs={{0,1},{1,2},{2,3},{3,0},{4,5},{5,6},{6,7},{7,4},{8,9},{9,10},{10,1... | collective-permute-start | bytes 786440 | tf_op jit(solution)/shard_map/ppermute | solution.py:345
  106.3 8.5 %collective-permute-start.8 = (bf16[192,384]{1,0:T(8,128)(2,1)S(1)}, bf16[192,384]{1,0:T(8,128)(2,1)S(1)}, u32[]{:S(2)}, u32[]{:S(2)}) collective-permute-start(bf16[192,384]{1,0:T(8,128)(2,1)S(1)} %get-tuple-element.17), channel_id=1, source_target_pairs={{0,4},{4,0},{8,12},{12,8},{16,20},{20,16},{24,28},{28,24},{32,36},... | collective-permute-start | bytes 442376 | tf_op jit(solution)/shard_map/ppermute | solution.py:384
  108.3 18.4 %copy-start.7 = (bf16[64,2048]{1,0:T(8,128)(2,1)}, bf16[64,2048]{1,0:T(8,128)(2,1)S(1)}, u32[]{:S(2)}) copy-start(bf16[64,2048]{1,0:T(8,128)(2,1)S(1)} %collective-permute-done.10.refs_1_.far_b) | copy-start | bytes 786436
  111.0 15.7 %copy-start.9 = (bf16[64,2048]{1,0:T(8,128)(2,1)}, bf16[64,2048]{1,0:T(8,128)(2,1)S(1)}, u32[]{:S(2)}) copy-start(bf16[64,2048]{1,0:T(8,128)(2,1)S(1)} %collective-permute-done.9.refs_0_.far_a) | copy-start | bytes 786436
  112.9 6.0 %collective-permute-start.11 = (bf16[64,384]{1,0:T(8,128)(2,1)S(1)}, bf16[64,384]{1,0:T(8,128)(2,1)S(1)}, u32[]{:S(2)}, u32[]{:S(2)}) collective-permute-start(bf16[64,384]{1,0:T(8,128)(2,1)S(1)} %get-tuple-element.19), channel_id=1, source_target_pairs={{0,4},{4,0},{8,12},{12,8},{16,20},{20,16},{24,28},{28,24},{32,36},... | collective-permute-start | bytes 147464 | tf_op jit(solution)/shard_map/ppermute | solution.py:384
  119.1 7.6 %collective-permute-start.12 = (bf16[256,384]{1,0:T(8,128)(2,1)S(1)}, bf16[256,384]{1,0:T(8,128)(2,1)S(1)}, u32[]{:S(2)}, u32[]{:S(2)}) collective-permute-start(bf16[256,384]{1,0:T(8,128)(2,1)S(1)} %pad_maximum_fusion.mine), channel_id=1, source_target_pairs={{0,4},{4,0},{8,12},{12,8},{16,20},{20,16},{24,28},{28,24},{32,36},... | collective-permute-start | bytes 589832 | tf_op jit(solution)/shard_map/ppermute | solution.py:387
  130.7 9.0 %collective-permute-start.13 = (bf16[4,512,384]{2,1,0:T(8,128)(2,1)}, bf16[4,512,384]{2,1,0:T(8,128)(2,1)}, u32[]{:S(2)}, u32[]{:S(2)}) collective-permute-start(bf16[4,512,384]{2,1,0:T(8,128)(2,1)} %shard_map.96), channel_id=1, source_target_pairs={{0,64},{64,0},{1,65},{65,1},{2,66},{66,2},{3,67},{67,3},{4,68},{68... | collective-permute-start | bytes 4718600 | tf_op jit(solution)/shard_map/ppermute | solution.py:390
  134.3 1.0 copy-start.4
  135.3 4.4 %copy-start.1 = (bf16[128,2048]{1,0:T(8,128)(2,1)S(1)}, bf16[128,2048]{1,0:T(8,128)(2,1)}, u32[]{:S(2)}) copy-start(bf16[128,2048]{1,0:T(8,128)(2,1)} %copy-done) | copy-start | bytes 1572868
  135.3 4.4 %copy-start.3 = (bf16[128,2048]{1,0:T(8,128)(2,1)S(1)}, bf16[128,2048]{1,0:T(8,128)(2,1)}, u32[]{:S(2)}) copy-start(bf16[128,2048]{1,0:T(8,128)(2,1)} %copy-done.2) | copy-start | bytes 1572868
  135.3 4.4 %copy-start.8 = (bf16[64,2048]{1,0:T(8,128)(2,1)S(1)}, bf16[64,2048]{1,0:T(8,128)(2,1)}, u32[]{:S(2)}) copy-start(bf16[64,2048]{1,0:T(8,128)(2,1)} %copy-done.7) | copy-start | bytes 786436
  135.3 4.5 %copy-start.10 = (bf16[64,2048]{1,0:T(8,128)(2,1)S(1)}, bf16[64,2048]{1,0:T(8,128)(2,1)}, u32[]{:S(2)}) copy-start(bf16[64,2048]{1,0:T(8,128)(2,1)} %copy-done.9) | copy-start | bytes 786436
  135.3 26.6 %all-to-all-start.1 = ((bf16[4,64,2048]{2,1,0:T(8,128)(2,1)}), bf16[4,64,2048]{2,1,0:T(8,128)(2,1)}, u32[]{:S(2)}, u32[]{:S(2)}) async-start(bf16[4,64,2048]{2,1,0:T(8,128)(2,1)} %copy-done.4), calls=%async_computation.1 | async-start | bytes 2097152 | tf_op jit(solution)/shard_map/all_to_all | solution.py:392
  143.6 10.4 %collective-permute-start.16 = (bf16[256,384]{1,0:T(8,128)(2,1)S(1)}, bf16[256,384]{1,0:T(8,128)(2,1)S(1)}, u32[]{:S(2)}, u32[]{:S(2)}) collective-permute-start(bf16[256,384]{1,0:T(8,128)(2,1)S(1)} %get-tuple-element.24), channel_id=1, source_target_pairs={{0,128},{128,256},{256,384},{384,0},{1,129},{129,257},{257,385},{3... | collective-permute-start | bytes 589832 | tf_op jit(solution)/shard_map/ppermute | solution.py:354
  145.5 10.5 %collective-permute-start.14 = (bf16[256,384]{1,0:T(8,128)(2,1)S(1)}, bf16[256,384]{1,0:T(8,128)(2,1)S(1)}, u32[]{:S(2)}, u32[]{:S(2)}) collective-permute-start(bf16[256,384]{1,0:T(8,128)(2,1)S(1)} %get-tuple-element.22), channel_id=1, source_target_pairs={{0,384},{128,0},{256,128},{384,256},{1,385},{129,1},{257,129},{385... | collective-permute-start | bytes 589832 | tf_op jit(solution)/shard_map/ppermute | solution.py:353
  154.0 22.8 %collective-permute-start.17 = (bf16[512,384]{1,0:T(8,128)(2,1)S(1)}, bf16[512,384]{1,0:T(8,128)(2,1)S(1)}, u32[]{:S(2)}, u32[]{:S(2)}) collective-permute-start(bf16[512,384]{1,0:T(8,128)(2,1)S(1)} %add_convert_fusion.1), channel_id=1, source_target_pairs={{0,128},{128,256},{256,384},{384,0},{1,129},{129,257},{257,385},{3... | collective-permute-start | bytes 1179656 | tf_op jit(solution)/shard_map/ppermute | solution.py:358
  156.8 20.0 %collective-permute-start.15 = (bf16[512,384]{1,0:T(8,128)(2,1)}, bf16[512,384]{1,0:T(8,128)(2,1)S(1)}, u32[]{:S(2)}, u32[]{:S(2)}) collective-permute-start(bf16[512,384]{1,0:T(8,128)(2,1)} %add_convert_fusion.2), channel_id=1, source_target_pairs={{0,384},{128,0},{256,128},{384,256},{1,385},{129,1},{257,129},{385... | collective-permute-start | bytes 1179656 | tf_op jit(solution)/shard_map/ppermute | solution.py:357
  163.3 32.0 %copy-start.6 = (bf16[128,4096]{1,0:T(8,128)(2,1)S(1)}, bf16[128,4096]{1,0:T(8,128)(2,1)}, u32[]{:S(2)}) copy-start(bf16[128,4096]{1,0:T(8,128)(2,1)} %latent.3) | copy-start | bytes 3145732
  163.3 32.0 %copy-start.15 = (f32[4096]{0:T(1024)S(1)}, f32[4096]{0:T(1024)}, u32[]{:S(2)}) copy-start(f32[4096]{0:T(1024)} %param.11) | copy-start | bytes 49156
  163.4 32.0 %copy-start.17 = (s32[128,2]{0,1:T(2,128)S(1)}, s32[128,2]{0,1:T(2,128)}, u32[]{:S(2)}) copy-start(s32[128,2]{0,1:T(2,128)} %param.9) | copy-start | bytes 3076
  164.2 31.1 %all-to-all-start.2 = ((bf16[16,4,2048]{2,1,0:T(4,128)(2,1)}), bf16[16,4,2048]{2,1,0:T(4,128)(2,1)S(1)}, u32[]{:S(2)}, u32[]{:S(2)}) async-start(bf16[16,4,2048]{2,1,0:T(4,128)(2,1)} %reshape.13), calls=%async_computation.2 | async-start | bytes 524288 | tf_op jit(solution)/shard_map/all_to_all | solution.py:399
  177.0 20.4 %collective-permute-start.18 = (bf16[512,384]{1,0:T(8,128)(2,1)S(1)}, bf16[512,384]{1,0:T(8,128)(2,1)S(1)}, u32[]{:S(2)}, u32[]{:S(2)}) collective-permute-start(bf16[512,384]{1,0:T(8,128)(2,1)S(1)} %add_convert_fusion), channel_id=1, source_target_pairs={{0,0},{4,64},{8,8},{12,72},{16,16},{20,80},{24,24},{28,88},{32,32}... | collective-permute-start | bytes 1179656 | tf_op jit(solution)/shard_map/ppermute | solution.py:394
